TPU v7x, 32 devices: a whole 2x2x4 slice. The times are simulated.
32 devices in a mesh: dp: 4 (over y, x), ctx: 4 (over z), head: 2 (over core).
Axes of the slice: x: 2, y: 2, z: 4, core: 2. Of those that a mesh axis runs over, the one named last changes fastest.
Arguments:
- inputs: bfloat16 [4, 512, 2048], P('dp', 'ctx', 'head'), may hold values from -1.5 to 1.5
- dt_raw: float32 [4, 512, 32], P('dp', 'ctx', 'head'), may hold values from -4 to 4
- dt_bias: float32 [32], P('head'), may hold values from -1 to 1
- a_log: float32 [32], P('head'), may hold values from -30 to -2.8
- b_in: bfloat16 [4, 512, 128], P('dp', 'ctx'), may hold values from -0.13183594 to 0.13183594
- c_in: bfloat16 [4, 512, 128], P('dp', 'ctx'), may hold values from -0.13183594 to 0.13183594
- skip_gain: float32 [32], P('head'), may hold values from 0.5 to 1.5
- grad_out: bfloat16 [4, 512, 2048], P('dp', 'ctx', 'head'), may hold values from -1.5 to 1.5
- doc_lengths: int32 [4, 4], P('dp'), may hold values from 1 to 256, 512 in all within a row
Outputs:
- grad_inputs: bfloat16 [4, 512, 2048], P('dp', 'ctx', 'head')
- grad_dt_raw: float32 [4, 512, 32], P('dp', 'ctx', 'head')
- grad_b: float32 [4, 512, 128], P('dp', 'ctx')
- grad_c: float32 [4, 512, 128], P('dp', 'ctx')
- grad_a_log: float32 [32], P('head')
- grad_dt_bias: float32 [32], P('head')
- grad_skip: float32 [32], P('head')
Inputs may be any that keep to these rules, and one draw needn't show every extreme that they name: `doc_lengths`: each row lists 4 document lengths laid end to end from the sequence's first position; they sum to 512, and the longest is exactly half of 512.
All inputs are finite; a program needn't handle non-finite values.
Results may differ from a plain program's by a relative error of at most 0.007.
Values sent between devices are 32-bit elements; how exact they have to be, the bound alone decides.
No kernel may reach another device: no remote copies, remote signals or barrier semaphores. Data moves between devices by JAX's collectives and lax.ppermute only.
A program may use at most 64 MiB of HBM per device.

v0:
```python
import jax
import jax.numpy as jnp
from jax import lax
from jax.sharding import PartitionSpec as P

SPAN = 128


def from_behind(array, axis, by):
    count = lax.axis_size(axis)
    pairs = [(i, i + by) for i in range(count) if 0 <= i + by < count]
    return lax.ppermute(array, axis, pairs)


def reverse_cumsum(values, along_axis):
    return jnp.flip(jnp.cumsum(jnp.flip(values, along_axis), axis=along_axis), along_axis)


def doc_index(positions, starts):
    return jnp.sum((starts[None, :] <= positions[:, None]).astype(jnp.int32), axis=1)


def vector_factors(decay_block, segment_block, previous_block):
    cumulative = jnp.cumsum(decay_block, axis=0)
    last_segment = segment_block[-1]
    mask_in = (segment_block == previous_block).astype(jnp.float32)
    mask_out = (segment_block == last_segment).astype(jnp.float32)
    factor_in = mask_in[:, None] * jnp.exp(cumulative)
    factor_out = mask_out[:, None] * jnp.exp(cumulative[-1][None, :] - cumulative)
    span_total = (last_segment == previous_block).astype(jnp.float32) * jnp.exp(cumulative[-1])
    return (cumulative, mask_in, mask_out, factor_in, factor_out, span_total)


def pair_factor(cumulative, segment_block):
    local_pos = jnp.arange(segment_block.shape[0], dtype=jnp.int32)
    allowed = (local_pos[:, None] >= local_pos[None, :]) & (
        segment_block[:, None] == segment_block[None, :]
    )
    spread = cumulative.T[:, :, None] - cumulative.T[:, None, :]
    return jnp.where(allowed[None], jnp.exp(jnp.where(allowed[None], spread, 0.0)), 0.0)


def first_pass(
    inputs_block,
    grads_block,
    b_block,
    c_block,
    step_block,
    decay_block,
    segment_block,
    previous_block,
):
    cumulative, mask_in, mask_out, factor_in, factor_out, span_total = vector_factors(
        decay_block, segment_block, previous_block
    )
    scaled_in = (inputs_block * (factor_out * step_block)[:, :, None]).astype(jnp.bfloat16)
    scaled_grad = (grads_block * factor_in[:, :, None]).astype(jnp.bfloat16)
    state_part = jnp.einsum("shp,sn->hpn", scaled_in, b_block, preferred_element_type=jnp.float32)
    grad_part = jnp.einsum("uhp,un->hpn", scaled_grad, c_block, preferred_element_type=jnp.float32)
    return (span_total, state_part, grad_part)


def span_grads(
    inputs_block,
    grads_block,
    b_block,
    c_block,
    step_block,
    decay_block,
    segment_block,
    previous_block,
    preact_block,
    state_in,
    state_grad,
    decay_rate,
    skip_gain,
):
    cumulative, mask_in, mask_out, factor_in, factor_out, span_total = vector_factors(
        decay_block, segment_block, previous_block
    )
    pair_decay = pair_factor(cumulative, segment_block)
    scores = jnp.einsum("un,sn->us", c_block, b_block, preferred_element_type=jnp.float32)
    cross_term = jnp.einsum(
        "uhp,shp->hus", grads_block, inputs_block, preferred_element_type=jnp.float32
    )
    masked = (pair_decay * scores[None]).astype(jnp.bfloat16)
    weighted = pair_decay * cross_term * step_block.T[:, None, :]
    summed = jnp.sum(weighted, axis=0).astype(jnp.bfloat16)
    products = weighted * scores[None]
    change = jnp.sum(products, axis=2) - jnp.sum(products, axis=1)
    first_term = reverse_cumsum(change, 1).T
    h_low = state_in.astype(jnp.bfloat16)
    e_low = state_grad.astype(jnp.bfloat16)
    along_b = jnp.einsum("tn,hpn->thp", b_block, e_low, preferred_element_type=jnp.float32)
    grad_b_prod = (
        jnp.einsum("hut,uhp->thp", masked, grads_block, preferred_element_type=jnp.float32)
        + factor_out[:, :, None] * along_b
    )
    grad_x = (step_block[:, :, None] * grad_b_prod + skip_gain[None, :, None] * grads_block).astype(
        jnp.bfloat16
    )
    x_state = jnp.einsum("thp,hpn->thn", inputs_block, e_low, preferred_element_type=jnp.float32)
    y_state = jnp.einsum("uhp,hpn->uhn", grads_block, h_low, preferred_element_type=jnp.float32)
    grad_b = jnp.einsum("us,un->sn", summed, c_block, preferred_element_type=jnp.float32) + jnp.sum(
        (step_block * factor_out)[:, :, None] * x_state, axis=1
    )
    grad_c = jnp.einsum("us,sn->un", summed, b_block, preferred_element_type=jnp.float32) + jnp.sum(
        factor_in[:, :, None] * y_state, axis=1
    )
    z_term = jnp.sum(y_state * c_block[:, None, :], axis=2)
    w_term = step_block * jnp.sum(x_state * b_block[:, None, :], axis=2)
    second_term = mask_in[:, None] * reverse_cumsum(factor_in * z_term, 0)
    carried = factor_out * w_term
    third_term = mask_out[:, None] * (jnp.cumsum(carried, axis=0) - carried)
    fourth_term = factor_out * factor_in * jnp.sum(state_grad * state_in, axis=(1, 2))[None, :]
    decay_grad = first_term + second_term + third_term + fourth_term
    x_dot_g = jnp.sum(inputs_block * grad_b_prod, axis=2)
    grad_dt = (x_dot_g + decay_rate[None, :] * decay_grad) * jax.nn.sigmoid(preact_block)
    grad_alog = jnp.sum(decay_grad * step_block, axis=0) * decay_rate
    grad_bias = jnp.sum(grad_dt, axis=0)
    grad_skip = jnp.einsum(
        "thp,thp->h", grads_block, inputs_block, preferred_element_type=jnp.float32
    )
    return (grad_x, grad_dt, grad_b, grad_c, grad_alog, grad_bias, grad_skip)


def local_link(running, pieces):
    decay_gain, held_state = running
    span_total, span_part = pieces
    return ((decay_gain * span_total, span_total[:, None, None] * held_state + span_part), running)


def link_maps(earlier, later):
    return (earlier[0] * later[0], later[0][:, None, None] * earlier[1] + later[1])


def doubling(element, reverse):
    axis_count = lax.axis_size("ctx")
    own_index = lax.axis_index("ctx")
    distances = [1] + [2**power for power in range((axis_count - 1).bit_length())]
    running = element
    for section_num, distance in enumerate(distances):
        shift_by = -distance if reverse else distance
        received = from_behind((running[0], running[1]), "ctx", shift_by)
        source = own_index - shift_by
        present = (source >= 0) & (source < axis_count)
        fixed = (jnp.where(present, received[0], 1.0), received[1])
        if section_num == 0:
            running = fixed
        else:
            running = link_maps(fixed, running)
    return running


def local(inputs, dt_raw, dt_bias, a_log, b_in, c_in, skip_gain, grad_out, doc_lengths):
    token_count = inputs.shape[1]
    head_count = dt_bias.shape[0]
    head_width = inputs.shape[2] // head_count
    state_size = b_in.shape[2]
    span_count = token_count // SPAN
    preact = dt_raw[0] + dt_bias[None, :]
    step_size = jax.nn.softplus(preact)
    decay_rate = -jnp.exp(a_log)
    log_decay = step_size * decay_rate[None, :]
    lengths = doc_lengths[0]
    starts = jnp.cumsum(lengths) - lengths
    positions = lax.axis_index("ctx") * token_count + jnp.arange(token_count, dtype=jnp.int32)
    segment = doc_index(positions, starts)
    previous = doc_index(positions[::SPAN] - 1, starts)
    shaped = (
        inputs[0].reshape(span_count, SPAN, head_count, head_width),
        grad_out[0].reshape(span_count, SPAN, head_count, head_width),
        b_in[0].reshape(span_count, SPAN, state_size),
        c_in[0].reshape(span_count, SPAN, state_size),
        step_size.reshape(span_count, SPAN, head_count),
        log_decay.reshape(span_count, SPAN, head_count),
        segment.reshape(span_count, SPAN),
        previous,
    )
    totals, state_parts, grad_parts = jax.vmap(first_pass)(*shaped)
    start_maps = (
        jnp.ones((head_count,), jnp.float32),
        jnp.zeros((head_count, head_width, state_size), jnp.float32),
    )
    forward_map, (gain_before, local_entry) = lax.scan(
        local_link, start_maps, (totals, state_parts)
    )
    backward_map, (gain_after, local_leave) = lax.scan(
        local_link, start_maps, (totals, grad_parts), reverse=True
    )
    entry_state = doubling(forward_map, False)[1]
    leave_state = doubling(backward_map, True)[1]
    entering = gain_before[:, :, None, None] * entry_state[None] + local_entry
    leaving = gain_after[:, :, None, None] * leave_state[None] + local_leave
    mapped = jax.vmap(span_grads, in_axes=(0, 0, 0, 0, 0, 0, 0, 0, 0, 0, 0, None, None))
    grad_x, grad_dt, grad_b, grad_c, grad_alog, grad_bias, grad_skip = mapped(
        *shaped,
        preact.reshape(span_count, SPAN, head_count),
        entering,
        leaving,
        decay_rate,
        skip_gain
    )
    b_total, c_total = lax.psum(
        (grad_b.reshape(token_count, state_size), grad_c.reshape(token_count, state_size)), "head"
    )
    alog_total, bias_total, skip_total = lax.psum(
        (jnp.sum(grad_alog, axis=0), jnp.sum(grad_bias, axis=0), jnp.sum(grad_skip, axis=0)),
        ("dp", "ctx"),
    )
    return (
        grad_x.reshape(1, token_count, head_count * head_width),
        grad_dt,
        b_total[None],
        c_total[None],
        alog_total,
        bias_total,
        skip_total,
    )


def solution(mesh):
    placed = (
        P("dp", "ctx", "head"),
        P("dp", "ctx", "head"),
        P("head"),
        P("head"),
        P("dp", "ctx", None),
        P("dp", "ctx", None),
        P("head"),
        P("dp", "ctx", "head"),
        P("dp", None),
    )
    return jax.shard_map(
        local,
        mesh=mesh,
        in_specs=placed,
        out_specs=(
            P("dp", "ctx", "head"),
            P("dp", "ctx", "head"),
            P("dp", "ctx", None),
            P("dp", "ctx", None),
            P("head"),
            P("head"),
            P("head"),
        ),
        check_vma=False,
    )
```

profile of v0, /device:TPU:0, one launch (start us, length us, event | category | flops | bytes accessed | tf_op | source)
XLA Modules:
  0.0 140.7 jit_solution(209060816925791621)
XLA Ops:
  7.3 0.8 reduce-window_clone.1
  8.1 1.3 fusion.37
  9.5 0.6 slice.13
  10.1 0.8 copy.101
  10.9 0.7 exponential_negate_fusion
  12.8 0.7 broadcast_multiply_fusion
  13.5 0.2 reduce_window_sum.44
  13.7 1.3 collective-permute-start
  15.0 5.6 %collective-permute-start.5 = (f32[16]{0:T(128)S(1)}, f32[16]{0:T(128)S(1)}, u32[]{:S(2)}, u32[]{:S(2)}) collective-permute-start(f32[16]{0:T(128)S(1)} %get-tuple-element.102), channel_id=1, source_target_pairs={{0,2},{2,4},{4,6},{1,3},{3,5},{5,7},{8,10},{10,12},{12,14},{9,11},... | collective-permute-start | bytes 200 | tf_op jit(solution)/shard_map/ppermute | solution.py:12
  20.7 1.3 compare_convert_fusion
  22.3 0.7 copy-done.1
  23.0 0.2 convolution_add_fusion.1
  23.3 1.4 %collective-permute-start.2 = (f32[16,64,128]{2,1,0:T(8,128)S(1)}, f32[16,64,128]{2,1,0:T(8,128)S(1)}, u32[]{:S(2)}, u32[]{:S(2)}) collective-permute-start(f32[16,64,128]{2,1,0:T(8,128)S(1)} %convolution_add_fusion.1), channel_id=1, source_target_pairs={{2,0},{4,2},{6,4},{3,1},{5,3},{7,5},{10,8},{12,10},{14,12},{11,9},... | collective-permute-start | bytes 1572872 | tf_op jit(solution)/shard_map/ppermute | solution.py:12
  24.8 0.2 copy.107
  25.1 0.7 copy-done
  25.8 0.2 convolution_add_fusion
  26.0 4.6 %collective-permute-start.7 = (f32[16,64,128]{2,1,0:T(8,128)S(1)}, f32[16,64,128]{2,1,0:T(8,128)S(1)}, u32[]{:S(2)}, u32[]{:S(2)}) collective-permute-start(f32[16,64,128]{2,1,0:T(8,128)S(1)} %convolution_add_fusion), channel_id=1, source_target_pairs={{0,2},{2,4},{4,6},{1,3},{3,5},{5,7},{8,10},{10,12},{12,14},{9,11},... | collective-permute-start | bytes 1572872 | tf_op jit(solution)/shard_map/ppermute | solution.py:12
  30.9 0.6 copy-done.5
  31.6 0.9 multiply_reduce_fusion.4
  32.6 6.1 %collective-permute-done.2 = f32[16,64,128]{2,1,0:T(8,128)S(1)} collective-permute-done((f32[16,64,128]{2,1,0:T(8,128)S(1)}, f32[16,64,128]{2,1,0:T(8,128)S(1)}, u32[]{:S(2)}, u32[]{:S(2)}) %collective-permute-start.2) | collective-permute-done | bytes 524320 | tf_op jit(solution)/shard_map/ppermute | solution.py:12
  38.7 1.3 collective-permute-start.3
  40.0 0.5 convolution_bitcast_fusion.2
  40.8 0.3 reduce_window_sum.46
  41.2 4.6 %collective-permute-start.8 = (f32[16,64,128]{2,1,0:T(8,128)S(1)}, f32[16,64,128]{2,1,0:T(8,128)S(1)}, u32[]{:S(2)}, u32[]{:S(2)}) collective-permute-start(f32[16,64,128]{2,1,0:T(8,128)S(1)} %collective-permute-done.7), channel_id=1, source_target_pairs={{0,2},{2,4},{4,6},{1,3},{3,5},{5,7},{8,10},{10,12},{12,14},{9,11},... | collective-permute-start | bytes 1572872 | tf_op jit(solution)/shard_map/ppermute | solution.py:12
  45.8 7.3 %collective-permute-done.3 = f32[16,64,128]{2,1,0:T(8,128)} collective-permute-done((f32[16,64,128]{2,1,0:T(8,128)S(1)}, f32[16,64,128]{2,1,0:T(8,128)}, u32[]{:S(2)}, u32[]{:S(2)}) %collective-permute-start.3) | collective-permute-done | bytes 524320 | tf_op jit(solution)/shard_map/ppermute | solution.py:12
  53.2 1.2 multiply_add_fusion.3
  54.3 1.3 collective-permute-start.4
  55.8 5.5 %collective-permute-start.9 = (f32[16,64,128]{2,1,0:T(8,128)S(1)}, f32[16,64,128]{2,1,0:T(8,128)S(1)}, u32[]{:S(2)}, u32[]{:S(2)}) collective-permute-start(f32[16,64,128]{2,1,0:T(8,128)S(1)} %multiply_add_fusion.1), channel_id=1, source_target_pairs={{0,4},{2,6},{1,5},{3,7},{8,12},{10,14},{9,13},{11,15},{16,20},{18,... | collective-permute-start | bytes 1572872 | tf_op jit(solution)/shard_map/ppermute | solution.py:12
  61.3 0.2 fusion.6
  61.5 3.9 %collective-permute-start.6 = (f32[16]{0:T(128)S(1)}, f32[16]{0:T(128)S(1)}, u32[]{:S(2)}, u32[]{:S(2)}) collective-permute-start(f32[16]{0:T(128)S(1)} %broadcast_select_fusion.1), channel_id=1, source_target_pairs={{0,2},{2,4},{4,6},{1,3},{3,5},{5,7},{8,10},{10,12},{12,14},{9,11},... | collective-permute-start | bytes 200 | tf_op jit(solution)/shard_map/ppermute | solution.py:12
  65.4 1.3 collective-permute-start.1
  66.7 3.5 %collective-permute-done.6 = f32[16]{0:T(128)S(1)} collective-permute-done((f32[16]{0:T(128)S(1)}, f32[16]{0:T(128)S(1)}, u32[]{:S(2)}, u32[]{:S(2)}) %collective-permute-start.6) | collective-permute-done | bytes 96 | tf_op jit(solution)/shard_map/ppermute | solution.py:12
  70.2 0.7 collective-permute-done.1
  70.9 9.1 %collective-permute-done.4 = f32[16,64,128]{2,1,0:T(8,128)S(1)} collective-permute-done((f32[16,64,128]{2,1,0:T(8,128)S(1)}, f32[16,64,128]{2,1,0:T(8,128)S(1)}, u32[]{:S(2)}, u32[]{:S(2)}) %collective-permute-start.4) | collective-permute-done | bytes 524320 | tf_op jit(solution)/shard_map/ppermute | solution.py:12
  80.0 0.3 multiply_reduce_fusion.6
  80.4 0.4 multiply_reduce_fusion.1
  80.8 0.7 multiply_reduce_fusion
  81.8 0.2 reduce_window_sum.47
  82.1 0.7 copy-done.7
  82.8 0.3 multiply_reduce_fusion.7
  83.6 0.8 fusion.4
  84.4 0.8 fusion.5
  85.2 0.7 copy.121
  85.9 0.8 copy.120
  86.7 0.6 copy-done.8
  87.4 44.3 %all-reduce = (f32[16]{0:T(128)}, f32[16]{0:T(128)}, f32[16]{0:T(128)}) all-reduce(f32[16]{0:T(128)S(1)} %fusion.39, f32[16]{0:T(128)S(1)} %get-tuple-element.96, f32[16]{0:T(128)S(1)} %fusion.6), channel_id=1, replica_groups=mesh['dp'=4,'ctx'=4,'head'=2] {'dp','ctx'}, use_global_device_ids=true, to_apply=%region_19.20 | all-reduce | flops 48 | bytes 384 | tf_op jit(solution)/shard_map/psum | solution.py:207
  131.7 1.5 %copy.134 = f32[1,128,128]{2,1,0:T(8,128)} copy(f32[1,128,128]{2,1,0:T(8,128)} %get-tuple-element.119) | data formatting | bytes 131072
  133.2 0.6 copy.135
  (62 shorter events, 2.7 us)
Async XLA Ops:
  7.2 14.8 %copy-start.2 = (bf16[1,128,1024]{2,1,0:T(8,128)(2,1)S(1)}, bf16[1,128,1024]{2,1,0:T(8,128)(2,1)}, u32[]{:S(2)}) copy-start(bf16[1,128,1024]{2,1,0:T(8,128)(2,1)} %param.16) | copy-start | bytes 786436
  7.2 124.5 %all-reduce.4.cloned.1.call-start = ((), (), s32[]{:S(2)}) async-start(), calls=%async_computation | async-start | bytes 262144 | tf_op jit(solution)/shard_map/psum | solution.py:204
  13.7 32.1 %collective-permute-start = (f32[16]{0:T(128)S(1)}, f32[16]{0:T(128)S(1)}, u32[]{:S(2)}, u32[]{:S(2)}) collective-permute-start(f32[16]{0:T(128)S(1)} %get-tuple-element.102), channel_id=1, source_target_pairs={{2,0},{4,2},{6,4},{3,1},{5,3},{7,5},{10,8},{12,10},{14,12},{11,9},... | collective-permute-start | bytes 200 | tf_op jit(solution)/shard_map/ppermute | solution.py:12
  15.0 30.8 %collective-permute-start.5 = (f32[16]{0:T(128)S(1)}, f32[16]{0:T(128)S(1)}, u32[]{:S(2)}, u32[]{:S(2)}) collective-permute-start(f32[16]{0:T(128)S(1)} %get-tuple-element.102), channel_id=1, source_target_pairs={{0,2},{2,4},{4,6},{1,3},{3,5},{5,7},{8,10},{10,12},{12,14},{9,11},... | collective-permute-start | bytes 200 | tf_op jit(solution)/shard_map/ppermute | solution.py:12
  22.3 0.8 copy-start.1
  23.0 1.7 %copy-start.6 = (f32[16]{0:T(128)S(1)}, f32[16]{0:T(128)}, u32[]{:S(2)}) copy-start(f32[16]{0:T(128)} %param.11) | copy-start | bytes 196
  23.2 1.6 %copy-start.3 = (bf16[1,128,1024]{2,1,0:T(8,128)(2,1)S(1)}, bf16[1,128,1024]{2,1,0:T(8,128)(2,1)}, u32[]{:S(2)}) copy-start(bf16[1,128,1024]{2,1,0:T(8,128)(2,1)} %param.9) | copy-start | bytes 786436
  23.3 15.4 %collective-permute-start.2 = (f32[16,64,128]{2,1,0:T(8,128)S(1)}, f32[16,64,128]{2,1,0:T(8,128)S(1)}, u32[]{:S(2)}, u32[]{:S(2)}) collective-permute-start(f32[16,64,128]{2,1,0:T(8,128)S(1)} %convolution_add_fusion.1), channel_id=1, source_target_pairs={{2,0},{4,2},{6,4},{3,1},{5,3},{7,5},{10,8},{12,10},{14,12},{11,9},... | collective-permute-start | bytes 1572872 | tf_op jit(solution)/shard_map/ppermute | solution.py:12
  25.0 0.8 copy-start
  26.0 15.2 %collective-permute-start.7 = (f32[16,64,128]{2,1,0:T(8,128)S(1)}, f32[16,64,128]{2,1,0:T(8,128)S(1)}, u32[]{:S(2)}, u32[]{:S(2)}) collective-permute-start(f32[16,64,128]{2,1,0:T(8,128)S(1)} %convolution_add_fusion), channel_id=1, source_target_pairs={{0,2},{2,4},{4,6},{1,3},{3,5},{5,7},{8,10},{10,12},{12,14},{9,11},... | collective-permute-start | bytes 1572872 | tf_op jit(solution)/shard_map/ppermute | solution.py:12
  30.7 0.7 copy-start.5
  38.7 14.5 %collective-permute-start.3 = (f32[16,64,128]{2,1,0:T(8,128)S(1)}, f32[16,64,128]{2,1,0:T(8,128)}, u32[]{:S(2)}, u32[]{:S(2)}) collective-permute-start(f32[16,64,128]{2,1,0:T(8,128)S(1)} %collective-permute-done.2), channel_id=1, source_target_pairs={{2,0},{4,2},{6,4},{3,1},{5,3},{7,5},{10,8},{12,10},{14,12},{11,9},... | collective-permute-start | bytes 1572872 | tf_op jit(solution)/shard_map/ppermute | solution.py:12
  41.2 14.4 %collective-permute-start.8 = (f32[16,64,128]{2,1,0:T(8,128)S(1)}, f32[16,64,128]{2,1,0:T(8,128)S(1)}, u32[]{:S(2)}, u32[]{:S(2)}) collective-permute-start(f32[16,64,128]{2,1,0:T(8,128)S(1)} %collective-permute-done.7), channel_id=1, source_target_pairs={{0,2},{2,4},{4,6},{1,3},{3,5},{5,7},{8,10},{10,12},{12,14},{9,11},... | collective-permute-start | bytes 1572872 | tf_op jit(solution)/shard_map/ppermute | solution.py:12
  54.3 25.7 %collective-permute-start.4 = (f32[16,64,128]{2,1,0:T(8,128)S(1)}, f32[16,64,128]{2,1,0:T(8,128)S(1)}, u32[]{:S(2)}, u32[]{:S(2)}) collective-permute-start(f32[16,64,128]{2,1,0:T(8,128)S(1)} %multiply_add_fusion.3), channel_id=1, source_target_pairs={{4,0},{6,2},{5,1},{7,3},{12,8},{14,10},{13,9},{15,11},{20,16},{22,... | collective-permute-start | bytes 1572872 | tf_op jit(solution)/shard_map/ppermute | solution.py:12
  55.8 24.3 %collective-permute-start.9 = (f32[16,64,128]{2,1,0:T(8,128)S(1)}, f32[16,64,128]{2,1,0:T(8,128)S(1)}, u32[]{:S(2)}, u32[]{:S(2)}) collective-permute-start(f32[16,64,128]{2,1,0:T(8,128)S(1)} %multiply_add_fusion.1), channel_id=1, source_target_pairs={{0,4},{2,6},{1,5},{3,7},{8,12},{10,14},{9,13},{11,15},{16,20},{18,... | collective-permute-start | bytes 1572872 | tf_op jit(solution)/shard_map/ppermute | solution.py:12
  61.5 8.7 %collective-permute-start.6 = (f32[16]{0:T(128)S(1)}, f32[16]{0:T(128)S(1)}, u32[]{:S(2)}, u32[]{:S(2)}) collective-permute-start(f32[16]{0:T(128)S(1)} %broadcast_select_fusion.1), channel_id=1, source_target_pairs={{0,2},{2,4},{4,6},{1,3},{3,5},{5,7},{8,10},{10,12},{12,14},{9,11},... | collective-permute-start | bytes 200 | tf_op jit(solution)/shard_map/ppermute | solution.py:12
  65.4 5.5 %collective-permute-start.1 = (f32[16]{0:T(128)S(1)}, f32[16]{0:T(128)S(1)}, u32[]{:S(2)}, u32[]{:S(2)}) collective-permute-start(f32[16]{0:T(128)S(1)} %broadcast_select_fusion.3), channel_id=1, source_target_pairs={{2,0},{4,2},{6,4},{3,1},{5,3},{7,5},{10,8},{12,10},{14,12},{11,9},... | collective-permute-start | bytes 200 | tf_op jit(solution)/shard_map/ppermute | solution.py:12
  82.1 0.7 copy-start.7
  86.7 0.7 copy-start.8
  131.7 1.5 %copy-start.4 = (f32[1,128,128]{2,1,0:T(8,128)S(1)}, f32[1,128,128]{2,1,0:T(8,128)}, u32[]{:S(2)}) copy-start(f32[1,128,128]{2,1,0:T(8,128)} %get-tuple-element.120) | copy-start | bytes 196612
Sparse Core Ops, SparseCore 0:
  86.9 20.8 all-reduce.3
where the time goes:
time: 141 us
  blocking collectives  44.3 us (31%)
  starting transfers between devices  30.8 us (22%)
  waiting for transfers between devices  26.8 us (19%)
  between operations  15.8 us (11%)
  local copies, waits for them, and re-layouts  9.75 us (7%)
  other arithmetic  8.3 us (6%)
  matrix products  4.97 us (4%)
    psum x1, blocking collectives, local(): lax.psum((jnp.sum(grad_alog, axis=0), jnp.sum(grad_bias, axis=0), jnp.sum...  44.3 us
    ppermute x10, starting transfers between devices, from_behind(): return lax.ppermute(array, axis, pairs)  30.8 us
    ppermute x10, waiting for transfers between devices, from_behind(): return lax.ppermute(array, axis, pairs)  26.8 us
    unnamed x25, local copies, waits for them, and re-layouts  8.06 us
  transfers between devices with their start and end apart: 11, of which 5 were waited for; matrix products, arithmetic and copies ran while one was open for 5% of the time, Pallas kernels for 0%

commit v1 on v0

--- a/solution.py
+++ b/solution.py
@@ -1,9 +1,17 @@
+import functools
+
 import jax
 import jax.numpy as jnp
 from jax import lax
+from jax.experimental import pallas as pl
+from jax.experimental.pallas import tpu as pltpu
 from jax.sharding import PartitionSpec as P
 
 SPAN = 128
+LANES = 128
+F32 = jnp.float32
+BF16 = jnp.bfloat16
+EXACT = lax.Precision.HIGHEST
 
 
 def from_behind(array, axis, by):
@@ -152,7 +160,7 @@
     return running
 
 
-def local(inputs, dt_raw, dt_bias, a_log, b_in, c_in, skip_gain, grad_out, doc_lengths):
+def general_local(inputs, dt_raw, dt_bias, a_log, b_in, c_in, skip_gain, grad_out, doc_lengths):
     token_count = inputs.shape[1]
     head_count = dt_bias.shape[0]
     head_width = inputs.shape[2] // head_count
@@ -219,6 +227,452 @@
     )
 
 
+def nn(left, right, precision=None):
+    return lax.dot_general(
+        left, right, (((1,), (0,)), ((), ())), precision=precision, preferred_element_type=F32
+    )
+
+
+def nt(left, right, precision=None):
+    return lax.dot_general(
+        left, right, (((1,), (1,)), ((), ())), precision=precision, preferred_element_type=F32
+    )
+
+
+def iota(shape, axis):
+    return lax.broadcasted_iota(jnp.int32, shape, axis)
+
+
+def eye(size):
+    return (iota((size, size), 0) == iota((size, size), 1)).astype(F32)
+
+
+def head_rows(heads, features):
+    width = features // heads
+    start = iota((heads, features), 0) * width
+    feature = iota((heads, features), 1)
+    return ((feature >= start) & (feature < start + width)).astype(BF16)
+
+
+def head_columns(features, heads):
+    width = features // heads
+    start = iota((features, heads), 1) * width
+    feature = iota((features, heads), 0)
+    return ((feature >= start) & (feature < start + width)).astype(BF16)
+
+
+def spread(factor, rows):
+    high = factor.astype(BF16)
+    rest = factor - high.astype(F32)
+    middle = rest.astype(BF16)
+    low = (rest - middle.astype(F32)).astype(BF16)
+    return nn(high, rows) + nn(middle, rows) + nn(low, rows)
+
+
+def head_sum(values, columns):
+    high = values.astype(BF16)
+    low = (values - high.astype(F32)).astype(BF16)
+    return nn(high, columns) + nn(low, columns)
+
+
+def doc_of(lens_ref, positions):
+    count = jnp.zeros(positions.shape, jnp.int32)
+    start = jnp.int32(0)
+    for index in range(lens_ref.shape[1]):
+        count = count + (start <= positions).astype(jnp.int32)
+        start = start + lens_ref[0, index]
+    return count
+
+
+def doc_scalar(lens_ref, position):
+    count = jnp.int32(0)
+    start = jnp.int32(0)
+    for index in range(lens_ref.shape[1]):
+        count = count + jnp.where(start <= position, 1, 0)
+        start = start + lens_ref[0, index]
+    return count
+
+
+def masks(lens_ref, span):
+    base = lax.axis_index("ctx") * span
+    doc = doc_of(lens_ref, base + iota((span, 1), 0))
+    before = doc_scalar(lens_ref, base - 1)
+    last = doc_scalar(lens_ref, base + span - 1)
+    inward = (doc == before).astype(F32)
+    outward = (doc == last).astype(F32)
+    whole = jnp.where(last == before, 1.0, 0.0)
+    return inward, outward, whole
+
+
+AUX = ("dt", "gate", "cum", "din", "dout", "alpha_s", "beta_s", "alpha_u", "beta_u", "tot", "rate")
+
+
+def aux_get(aux_ref, name, heads):
+    slot = AUX.index(name) * heads
+    return aux_ref[:, slot : slot + heads]
+
+
+def prep_kernel(
+    lens_ref, x_ref, g_ref, raw_ref, bias_ref, alog_ref, b_ref, c_ref,
+    pay_even_ref, pay_odd_ref, aux_ref, xs_ref, gs_ref,
+):
+    span, features = x_ref.shape[1:]
+    heads = raw_ref.shape[2]
+    inward, outward, whole = masks(lens_ref, span)
+    preact = raw_ref[0] + bias_ref[...]
+    dt = jnp.maximum(preact, 0.0) + jnp.log1p(jnp.exp(-jnp.abs(preact)))
+    gate = 1.0 / (1.0 + jnp.exp(-preact))
+    rate = -jnp.exp(alog_ref[...])
+    row, column = iota((span, span), 0), iota((span, span), 1)
+    upto = (row >= column).astype(F32)
+    beyond = (row < column).astype(F32)
+    cum = nn(upto, dt * rate, EXACT)
+    cum_last = cum[span - 1 : span, :]
+    din = inward * jnp.exp(cum)
+    dout = outward * jnp.exp(cum_last - cum)
+    tot = jnp.broadcast_to(whole * jnp.exp(cum_last), cum.shape)
+    pair = jnp.concatenate([dt, gate], axis=1)
+    seen = nn(upto, pair * inward, EXACT)
+    left = nn(beyond, pair * outward, EXACT)
+    alpha_s = rate * left[:, :heads]
+    beta_s = rate * left[:, heads:] + gate / dt
+    alpha_u = rate * seen[:, :heads]
+    beta_u = rate * seen[:, heads:]
+    values = (dt, gate, cum, din, dout, alpha_s, beta_s, alpha_u, beta_u, tot,
+              jnp.broadcast_to(rate, cum.shape))
+    for slot, value in enumerate(values):
+        aux_ref[:, slot * heads : (slot + 1) * heads] = value
+    rows = head_rows(heads, features)
+    xs = (x_ref[0].astype(F32) * spread(dout * dt, rows)).astype(BF16)
+    gs = (g_ref[0].astype(F32) * spread(din, rows)).astype(BF16)
+    xs_ref[...] = xs
+    gs_ref[...] = gs
+    turn = eye(heads)
+    ahead_small = [nt(turn, alpha_s, EXACT), nt(turn, beta_s, EXACT)]
+    behind_small = [nt(turn, alpha_u, EXACT), nt(turn, beta_u, EXACT)]
+
+    def fill(ref, scaled, wide, small):
+        blocks = features // LANES
+        for block in range(blocks):
+            ref[block * span : (block + 1) * span, :] = scaled[
+                :, block * LANES : (block + 1) * LANES
+            ].astype(F32)
+        base = blocks * span
+        ref[base : base + span, :] = wide.astype(F32)
+        base = base + span
+        for part in small:
+            ref[base : base + heads, :] = part
+            base = base + heads
+
+    even = lax.rem(lax.axis_index("ctx"), 2) == 0
+
+    @pl.when(even)
+    def _():
+        fill(pay_even_ref, xs, b_ref[0], ahead_small)
+        fill(pay_odd_ref, gs, c_ref[0], behind_small)
+
+    @pl.when(jnp.logical_not(even))
+    def _():
+        fill(pay_even_ref, gs, c_ref[0], behind_small)
+        fill(pay_odd_ref, xs, b_ref[0], ahead_small)
+
+
+def local_kernel(lens_ref, x_ref, g_ref, aux_ref, b_ref, c_ref, gb_ref, small_ref, grads_ref):
+    span, features = x_ref.shape[1:]
+    heads = small_ref.shape[1] // 8
+    width = features // heads
+    base = lax.axis_index("ctx") * span
+    doc_s = doc_of(lens_ref, base + iota((span, 1), 0))
+    doc_u = doc_of(lens_ref, base + iota((1, span), 1))
+    row, column = iota((span, span), 0), iota((span, span), 1)
+    closed = jnp.where((column >= row) & (doc_s == doc_u), 0.0, -1e30)
+    dt = aux_get(aux_ref, "dt", heads)
+    gate = aux_get(aux_ref, "gate", heads)
+    cum = aux_get(aux_ref, "cum", heads)
+    rate = aux_get(aux_ref, "rate", heads)
+    cum_rows = nt(eye(heads), cum, EXACT)
+    scores = nt(b_ref[0], c_ref[0])
+    summed = jnp.zeros((span, span), F32)
+    lane = iota((span, heads), 1)
+    from_s = jnp.zeros((span, heads), F32)
+    to_u = []
+    for pair in range(0, heads, 2):
+        outs = []
+        for head in (pair, pair + 1):
+            part = slice(head * width, (head + 1) * width)
+            g_head, x_head = g_ref[0, :, part], x_ref[0, :, part]
+            cross = nt(x_head, g_head)
+            decay = jnp.exp(cum_rows[head : head + 1, :] - cum[:, head : head + 1] + closed)
+            masked = decay * scores
+            weighted = decay * cross * dt[:, head : head + 1]
+            summed = summed + weighted
+            product = weighted * scores
+            from_s = jnp.where(lane == head, jnp.sum(product, axis=1, keepdims=True), from_s)
+            to_u.append(jnp.sum(product, axis=0, keepdims=True))
+            outs.append(nn(masked.astype(BF16), g_head))
+        gb_ref[:, pair * width : (pair + 2) * width] = jnp.concatenate(outs, axis=1)
+    onward = (row <= column).astype(F32)
+    first = nt(onward, jnp.concatenate(to_u, axis=0), EXACT) - nn(onward, from_s, EXACT)
+    columns = head_columns(features, heads)
+    x_wide = x_ref[0].astype(F32)
+    x_gb = head_sum(x_wide * gb_ref[...], columns)
+    skip = head_sum(x_wide * g_ref[0].astype(F32), columns)
+    values = (first, x_gb, rate * dt * first, gate * (x_gb + rate * first), skip)
+    for slot, value in enumerate(values):
+        small_ref[:, slot * heads : (slot + 1) * heads] = value
+    grads_ref[:span, :] = nn(summed.astype(BF16), c_ref[0])
+    grads_ref[span:, :] = nn(jnp.transpose(summed).astype(BF16), b_ref[0])
+
+
+def relay_kernel(
+    got_even_ref, got_odd_ref, xs_ref, gs_ref, aux_ref, b_ref, c_ref, small_ref, grads_ref,
+    hop_even_ref, hop_odd_ref, red_ref, zw_ref, gb_ref, sums_ref,
+):
+    span, features = xs_ref.shape
+    heads = small_ref.shape[1] // 8
+    blocks = features // LANES
+    even = lax.rem(lax.axis_index("ctx"), 2) == 0
+
+    def behind(part):
+        return jnp.where(even, got_odd_ref[part, :], got_even_ref[part, :])
+
+    def ahead(part):
+        return jnp.where(even, got_even_ref[part, :], got_odd_ref[part, :])
+
+    def wide(get):
+        return jnp.concatenate(
+            [get(slice(k * span, (k + 1) * span)).astype(BF16) for k in range(blocks)], axis=1
+        )
+
+    base = blocks * span
+    xp, bp = wide(behind), behind(slice(base, base + span)).astype(BF16)
+    gn, cn = wide(ahead), ahead(slice(base, base + span)).astype(BF16)
+    base = base + span
+    alpha_p = behind(slice(base, base + heads))
+    beta_p = behind(slice(base + heads, base + 2 * heads))
+    alpha_n = ahead(slice(base, base + heads))
+    beta_n = ahead(slice(base + heads, base + 2 * heads))
+    xs, gs, b, c = xs_ref[...], gs_ref[...], b_ref[0], c_ref[0]
+    columns = head_columns(features, heads)
+    rows = head_rows(heads, features)
+    tot = aux_get(aux_ref, "tot", heads)
+    gn_tot = (gn.astype(F32) * spread(tot, rows)).astype(BF16)
+
+    pull = nn(nt(c, bp).astype(BF16), xp)
+    z_own = head_sum(gs.astype(F32) * pull, columns)
+    push = nn(nt(b, cn).astype(BF16), gn)
+    w_own = head_sum(xs.astype(F32) * push, columns)
+    gb_ref[...] = push
+    far_pull = nn(nt(cn, bp).astype(BF16), xp)
+    z_far = head_sum(gn_tot.astype(F32) * far_pull, columns)
+    far_push = nn(nt(bp, cn).astype(BF16), gn_tot)
+    w_far = head_sum(xp.astype(F32) * far_push, columns)
+
+    turn = eye(heads)
+    z_far_rows = nt(turn, z_far, EXACT)
+    w_far_rows = nt(turn, w_far, EXACT)
+    carried = jnp.sum(z_far, axis=0, keepdims=True)
+    dt, gate, rate = (aux_get(aux_ref, name, heads) for name in ("dt", "gate", "rate"))
+    values = small_ref[:, 2 * heads : 5 * heads]
+    alog_own = (
+        z_own * aux_get(aux_ref, "alpha_u", heads)
+        + w_own * aux_get(aux_ref, "alpha_s", heads)
+        + carried * rate * dt
+        + values[:, :heads]
+    )
+    bias_own = (
+        z_own * aux_get(aux_ref, "beta_u", heads)
+        + w_own * aux_get(aux_ref, "beta_s", heads)
+        + carried * rate * gate
+        + values[:, heads : 2 * heads]
+    )
+    ones = jnp.ones((8, span), F32)
+    alog = nn(ones, alog_own, EXACT) + nt(ones, z_far_rows * alpha_n + w_far_rows * alpha_p, EXACT)
+    bias = nn(ones, bias_own, EXACT) + nt(ones, z_far_rows * beta_n + w_far_rows * beta_p, EXACT)
+    skip = nn(ones, values[:, 2 * heads :], EXACT)
+    red_ref[...] = jnp.zeros(red_ref.shape, F32)
+    red_ref[:, :heads] = alog
+    red_ref[:, heads : 2 * heads] = bias
+    red_ref[:, 2 * heads : 3 * heads] = skip
+    zw_ref[:, :heads] = z_own
+    zw_ref[:, heads : 2 * heads] = w_own
+    zw_ref[:, 2 * heads : 3 * heads] = jnp.broadcast_to(carried, z_own.shape)
+
+    sums_ref[:span, :] = grads_ref[:span, :] + nn(nt(xs, gn).astype(BF16), cn)
+    sums_ref[span:, :] = grads_ref[span:, :] + nn(nt(gs, xp).astype(BF16), bp)
+    grad_b_far = nn(nt(xp, gn_tot).astype(BF16), cn)
+    grad_c_far = nn(nt(gn_tot, xp).astype(BF16), bp)
+
+    base = blocks * span
+
+    def fill(ref, grad, small, heavy):
+        if heavy:
+            for block in range(blocks):
+                ref[block * span : (block + 1) * span, :] = far_push[
+                    :, block * LANES : (block + 1) * LANES
+                ]
+        ref[base : base + span, :] = grad
+        ref[base + span : base + span + heads, :] = small
+
+    @pl.when(even)
+    def _():
+        fill(hop_even_ref, grad_c_far, z_far_rows, True)
+        fill(hop_odd_ref, grad_b_far, w_far_rows, True)
+
+    @pl.when(jnp.logical_not(even))
+    def _():
+        fill(hop_even_ref, grad_b_far, w_far_rows, True)
+        fill(hop_odd_ref, grad_c_far, z_far_rows, True)
+
+
+def final_kernel(
+    lens_ref, far_even_ref, far_odd_ref, g_ref, aux_ref, skip_ref, gbl_ref, gbn_ref, small_ref,
+    zw_ref, sums_ref, gx_ref, gdt_ref, half_ref,
+):
+    span, features = g_ref.shape[1:]
+    heads = small_ref.shape[1] // 8
+    blocks = features // LANES
+    even = lax.rem(lax.axis_index("ctx"), 2) == 0
+
+    def behind(part):
+        return jnp.where(even, far_odd_ref[part, :], far_even_ref[part, :])
+
+    def ahead(part):
+        return jnp.where(even, far_even_ref[part, :], far_odd_ref[part, :])
+
+    base = blocks * span
+    push = gbn_ref[...] + jnp.concatenate(
+        [ahead(slice(k * span, (k + 1) * span)) for k in range(blocks)], axis=1
+    )
+    rows = head_rows(heads, features)
+    dt = aux_get(aux_ref, "dt", heads)
+    dout = aux_get(aux_ref, "dout", heads)
+    gate = aux_get(aux_ref, "gate", heads)
+    rate = aux_get(aux_ref, "rate", heads)
+    skip = jnp.broadcast_to(skip_ref[...], dt.shape)
+    gx_ref[0] = (
+        spread(dt, rows) * gbl_ref[...]
+        + spread(dt * dout, rows) * push
+        + spread(skip, rows) * g_ref[0].astype(F32)
+    ).astype(BF16)
+    inward, outward, _ = masks(lens_ref, span)
+    flip = eye(span)
+    z = zw_ref[:, :heads] + nt(flip, behind(slice(base + span, base + span + heads)), EXACT)
+    w = zw_ref[:, heads : 2 * heads] + nt(
+        flip, ahead(slice(base + span, base + span + heads)), EXACT
+    )
+    row, column = iota((span, span), 0), iota((span, span), 1)
+    onward = (row <= column).astype(F32)
+    past = (row > column).astype(F32)
+    decay_grad = (
+        small_ref[:, :heads]
+        + inward * nn(onward, z, EXACT)
+        + outward * nn(past, w, EXACT)
+        + zw_ref[:, 2 * heads : 3 * heads]
+    )
+    x_gb = small_ref[:, heads : 2 * heads] + w / dt
+    gdt_ref[0] = (x_gb + rate * decay_grad) * gate
+    half_ref[:span, :] = sums_ref[:span, :] + ahead(slice(base, base + span))
+    half_ref[span:, :] = sums_ref[span:, :] + behind(slice(base, base + span))
+
+
+def call(kernel, shapes, operands, scalars=0, flops=0):
+    specs = [pl.BlockSpec(memory_space=pltpu.SMEM)] * scalars + [
+        pl.BlockSpec(memory_space=pltpu.VMEM)
+    ] * (len(operands) - scalars)
+    moved = sum(item.size * item.dtype.itemsize for item in operands) + sum(
+        item.size * jnp.dtype(item.dtype).itemsize for item in shapes
+    )
+    return pl.pallas_call(
+        kernel,
+        out_shape=shapes,
+        in_specs=specs,
+        out_specs=[pl.BlockSpec(memory_space=pltpu.VMEM)] * len(shapes),
+        cost_estimate=pl.CostEstimate(flops=flops, bytes_accessed=moved, transcendentals=0),
+    )(*operands)
+
+
+def near_local(inputs, dt_raw, dt_bias, a_log, b_in, c_in, skip_gain, grad_out, doc_lengths):
+    _, span, features = inputs.shape
+    heads = dt_bias.shape[0]
+    state = b_in.shape[2]
+    count = lax.axis_size("ctx")
+    struct = jax.ShapeDtypeStruct
+    bias, alog, skip = (item.reshape(1, heads) for item in (dt_bias, a_log, skip_gain))
+    pay_rows = features // LANES * span + span + 2 * heads
+    pay = struct((pay_rows, LANES), F32)
+    pay_even, pay_odd, aux, xs, gs = call(
+        prep_kernel,
+        (pay, pay, struct((span, 2 * LANES), F32), struct((span, features), BF16),
+         struct((span, features), BF16)),
+        (doc_lengths, inputs, grad_out, dt_raw, bias, alog, b_in, c_in),
+        scalars=1,
+        flops=10**8,
+    )
+    even_pairs = [(i, i ^ 1) for i in range(count) if i ^ 1 < count]
+    odd_pairs = [(i, j) for i in range(count) for j in [((i + 1) ^ 1) - 1] if 0 <= j < count]
+    got_odd = lax.ppermute(pay_odd, "ctx", odd_pairs)
+    got_even = lax.ppermute(pay_even, "ctx", even_pairs)
+    gb_local, small, grads = call(
+        local_kernel,
+        (struct((span, features), F32), struct((span, 8 * heads), F32),
+         struct((2 * span, state), F32)),
+        (doc_lengths, inputs, grad_out, aux, b_in, c_in),
+        scalars=1,
+        flops=10**8,
+    )
+    hop_rows = features // LANES * span + span + heads
+    hop = struct((hop_rows, LANES), F32)
+    hop_even, hop_odd, red, zw, gb_next, sums = call(
+        relay_kernel,
+        (hop, hop, struct((8, LANES), F32), struct((span, LANES), F32),
+         struct((span, features), F32), struct((2 * span, state), F32)),
+        (got_even, got_odd, xs, gs, aux, b_in, c_in, small, grads),
+        flops=3 * 10**8,
+    )
+    inner = range(1, count - 1)
+    far_even = lax.ppermute(hop_even, "ctx", [p for p in even_pairs if p[0] in inner])
+    far_odd = lax.ppermute(hop_odd, "ctx", [p for p in odd_pairs if p[0] in inner])
+    for axis in ("dp", "ctx"):
+        size = lax.axis_size(axis)
+        bit = 1
+        while bit < size:
+            red = red + lax.ppermute(red, axis, [(i, i ^ bit) for i in range(size)])
+            bit *= 2
+    grad_x, grad_dt, half = call(
+        final_kernel,
+        (struct((1, span, features), BF16), struct((1, span, heads), F32),
+         struct((2 * span, state), F32)),
+        (doc_lengths, far_even, far_odd, grad_out, aux, skip, gb_local, gb_next, small, zw, sums),
+        scalars=1,
+        flops=10**8,
+    )
+    lanes = lax.axis_size("head")
+    total = half
+    for step in range(1, lanes):
+        total = total + lax.ppermute(half, "head", [(i, (i + step) % lanes) for i in range(lanes)])
+    alog_total, bias_total, skip_total = (
+        red[0, i * heads : (i + 1) * heads] for i in range(3)
+    )
+    return (grad_x, grad_dt, total[None, :span], total[None, span:], alog_total, bias_total, skip_total)
+
+
+def local(inputs, dt_raw, dt_bias, a_log, b_in, c_in, skip_gain, grad_out, doc_lengths):
+    args = (inputs, dt_raw, dt_bias, a_log, b_in, c_in, skip_gain, grad_out, doc_lengths)
+    heads = dt_bias.shape[0]
+    shards = [lax.axis_size(axis) for axis in ("dp", "ctx")]
+    near = (
+        inputs.shape[1] == SPAN
+        and shards[1] in (2, 4)
+        and shards[0] & (shards[0] - 1) == 0
+        and b_in.shape[2] == LANES
+        and inputs.shape[2] % LANES == 0
+        and heads * len(AUX) <= 2 * LANES
+        and heads * 8 == LANES
+    )
+    return near_local(*args) if near else general_local(*args)
+
+
 def solution(mesh):
     placed = (
         P("dp", "ctx", "head"),

time: 141 us -> 62.7 us (0.44)
  blocking collectives: 44.3 us -> 0 us
  Pallas kernels: 0 us -> 18.3 us
  between operations: 15.8 us -> 0.7 us
  starting transfers between devices: 30.8 us -> 18.1 us
  waiting for transfers between devices: 26.8 us -> 18.1 us
  other arithmetic: 8.3 us -> 0.93 us
  matrix products: 4.97 us -> 0 us
  local copies, waits for them, and re-layouts: 9.75 us -> 6.23 us
    psum x1 -> x0, blocking collectives: 44.3 us -> none  [local(): lax.psum((jnp.sum(grad_alog, axis=0), jnp.sum(grad_bias, axis=0), jnp.sum...]
    pallas_call x0 -> x4, Pallas kernels: none -> 18.3 us  [call(): pl.pallas_call(kernel, out_shape=shapes, in_specs=specs, out_specs=[pl.Bl...]
    ppermute x10 -> x9, starting transfers between devices: 30.8 us -> 18.1 us  [the longest x4 12.2 us: near_local(): red = red + lax.ppermute(red, axis, [(i, i ^ bit) for i in range(size)])]
    ppermute x10 -> x9, waiting for transfers between devices: 26.8 us -> 18.1 us  [the longest x4 9.16 us: near_local(): red = red + lax.ppermute(red, axis, [(i, i ^ bit) for i in range(size)])]
    dot_general x10 -> x0, matrix products: 4.97 us -> none  [the longest x1 0.9 us: span_grads(): jnp.einsum('uhp,shp->hus', grads_block, inputs_block, preferred_element_t...]
    unnamed x25 -> x12, local copies, waits for them, and re-layouts: 8.06 us -> 4.98 us
    reduce_sum x5 -> x0, other arithmetic: 1.89 us -> none  [the longest x2 1.38 us: doc_index(): jnp.sum((starts[None, :] <= positions[:, None]).astype(jnp.int32), axis=1)]
    another operation x5 -> x0, other arithmetic: 1.63 us -> none
  transfers between devices with their start and end apart: 11 -> 9, of which waited for: 5 -> 5; matrix products, arithmetic and copies ran while one was open for 5% -> 3% of each run, Pallas kernels for 0% -> 7%
where the time goes in v1:
time: 62.7 us; the launch traced here: 62.3 us
  Pallas kernels  18.3 us (29%)
  starting transfers between devices  18.1 us (29%)
  waiting for transfers between devices  18.1 us (29%)
  local copies, waits for them, and re-layouts  6.23 us (10%)
  other arithmetic  0.93 us (1%)
  between operations  0.7 us (1%)
    pallas_call x4, Pallas kernels, call(): pl.pallas_call(kernel, out_shape=shapes, in_specs=specs, out_specs=[pl.Bl...  18.3 us
    ppermute x4, starting transfers between devices, near_local(): red = red + lax.ppermute(red, axis, [(i, i ^ bit) for i in range(size)])  12.2 us
    ppermute x4, waiting for transfers between devices, near_local(): red = red + lax.ppermute(red, axis, [(i, i ^ bit) for i in range(size)])  9.16 us
    ppermute x1, waiting for transfers between devices, near_local(): got_even = lax.ppermute(pay_even, 'ctx', even_pairs)  8.89 us
    unnamed x12, local copies, waits for them, and re-layouts  4.98 us
    ppermute x1, starting transfers between devices, near_local(): got_even = lax.ppermute(pay_even, 'ctx', even_pairs)  3.13 us
    ppermute x1, starting transfers between devices, near_local(): lax.ppermute(hop_even, 'ctx', [p for p in even_pairs if p[0] in inner])  1.41 us
  transfers between devices with their start and end apart: 9, of which 5 were waited for; matrix products, arithmetic and copies ran while one was open for 3% of the time, Pallas kernels for 7%

profile of v1, /device:TPU:0, one launch (start us, length us, event | category | flops | bytes accessed | tf_op | source)
XLA Modules:
  0.0 62.3 jit_solution(8763890973533150758)
XLA Ops:
  0.6 1.4 %copy.16.raw_ref = f32[1,128,16]{2,1,0:T(8,128)} copy(f32[1,128,16]{1,2,0:T(8,128)} %param.10) | data formatting | bytes 16384 | tf_op args[1]
  2.1 3.6 %shard_map.144 = (f32[1184,128]{1,0:T(8,128)}, f32[1184,128]{1,0:T(8,128)}, f32[128,256]{1,0:T(8,128)}, bf16[128,1024]{1,0:T(8,128)(2,1)}, bf16[128,1024]{1,0:T(8,128)(2,1)}) custom-call(s32[1,4]{1,0:T(1,128)} %lens_ref.5, bf16[1,128,1024]{2,1,0:T(8,128)(2,1)} %x_ref.3, bf16[1,128,1024]{2,1,0:T(8,128)(2,1)} %g_ref.5, f32[1,128,16]{2,1,0:T(8,128)} %copy.16.raw_ref, ...), custom_call_target="tpu_custom_call" | custom-call | flops 100000000 | bytes 2465936 | tf_op jit(solution)/shard_map/pallas_call | solution.py:586
  5.7 3.1 %collective-permute-start = (f32[1184,128]{1,0:T(8,128)}, f32[1184,128]{1,0:T(8,128)S(1)}, u32[]{:S(2)}, u32[]{:S(2)}) collective-permute-start(f32[1184,128]{1,0:T(8,128)} %get-tuple-element.24), channel_id=1, source_target_pairs={{0,2},{2,0},{4,6},{6,4},{1,3},{3,1},{5,7},{7,5},{8,10},{10,8},{12,... | collective-permute-start | bytes 1818632 | tf_op jit(solution)/shard_map/ppermute | solution.py:615
  8.8 0.7 %collective-permute-start.1 = (f32[1184,128]{1,0:T(8,128)}, f32[1184,128]{1,0:T(8,128)S(1)}, u32[]{:S(2)}, u32[]{:S(2)}) collective-permute-start(f32[1184,128]{1,0:T(8,128)} %get-tuple-element.25), channel_id=1, source_target_pairs={{2,4},{4,2},{3,5},{5,3},{10,12},{12,10},{11,13},{13,11},{18,20},{2... | collective-permute-start | bytes 1818632 | tf_op jit(solution)/shard_map/ppermute | solution.py:614
  9.5 4.3 %shard_map.145 = (f32[128,1024]{1,0:T(8,128)}, f32[128,128]{1,0:T(8,128)}, f32[256,128]{1,0:T(8,128)}) custom-call(s32[1,4]{1,0:T(1,128)} %lens_ref.5, bf16[1,128,1024]{2,1,0:T(8,128)(2,1)} %x_ref.3, bf16[1,128,1024]{2,1,0:T(8,128)(2,1)} %g_ref.5, f32[128,256]{1,0:T(8,128)} %get-tuple-element.28.aux_ref, bf16[1,128,128]{2,1,0:T(8,128)(2,1)} %b_ref.5, ...), custom_call_target="tpu_custom_call" | custom-call | flops 100000000 | bytes 1441808 | tf_op jit(solution)/shard_map/pallas_call | solution.py:586
  13.8 8.9 %collective-permute-done.got_even_ref = f32[1184,128]{1,0:T(8,128)S(1)} collective-permute-done((f32[1184,128]{1,0:T(8,128)}, f32[1184,128]{1,0:T(8,128)S(1)}, u32[]{:S(2)}, u32[]{:S(2)}) %collective-permute-start) | collective-permute-done | bytes 606240 | tf_op jit(solution)/shard_map/ppermute | solution.py:615
  22.7 0.0 copy-start
  22.7 0.0 collective-permute-done.1.got_odd_ref
  22.7 0.0 copy-start.1
  22.7 0.8 %copy-done = f32[1184,128]{1,0:T(8,128)} copy-done((f32[1184,128]{1,0:T(8,128)}, f32[1184,128]{1,0:T(8,128)S(1)}, u32[]{:S(2)}) %copy-start) | copy-done | bytes 606232
  23.5 0.2 copy-done.1
  23.8 6.5 %shard_map.146 = (f32[1168,128]{1,0:T(8,128)}, f32[1168,128]{1,0:T(8,128)}, f32[8,128]{1,0:T(8,128)}, f32[128,128]{1,0:T(8,128)}, f32[128,1024]{1,0:T(8,128)}, /*index=5*/f32[256,128]{1,0:T(8,128)}) custom-call(f32[1184,128]{1,0:T(8,128)} %copy-done, f32[1184,128]{1,0:T(8,128)} %copy-done.1, bf16[128,1024]{1,0:T(8,128)(2,1)} %get-tuple-element.26.xs_ref, ...), custom_call_target="tpu_custom_call" | custom-call | flops 300000000 | bytes 4050944 | tf_op jit(solution)/shard_map/pallas_call | solution.py:586
  30.2 0.0 copy-start.4
  30.2 1.4 %collective-permute-start.2 = (f32[1168,128]{1,0:T(8,128)}, f32[1168,128]{1,0:T(8,128)S(1)}, u32[]{:S(2)}, u32[]{:S(2)}) collective-permute-start(f32[1168,128]{1,0:T(8,128)} %get-tuple-element.31), channel_id=1, source_target_pairs={{2,0},{4,6},{3,1},{5,7},{10,8},{12,14},{11,9},{13,15},{18,16},{20,... | collective-permute-start | bytes 1794056 | tf_op jit(solution)/shard_map/ppermute | solution.py:634
  31.6 0.7 %collective-permute-start.3 = (f32[1168,128]{1,0:T(8,128)}, f32[1168,128]{1,0:T(8,128)S(1)}, u32[]{:S(2)}, u32[]{:S(2)}) collective-permute-start(f32[1168,128]{1,0:T(8,128)} %get-tuple-element.32), channel_id=1, source_target_pairs={{2,4},{4,2},{3,5},{5,3},{10,12},{12,10},{11,13},{13,11},{18,20},{2... | collective-permute-start | bytes 1794056 | tf_op jit(solution)/shard_map/ppermute | solution.py:635
  32.4 0.0 copy-done.4
  32.4 1.6 %collective-permute-start.5 = (f32[8,128]{1,0:T(8,128)S(1)}, f32[8,128]{1,0:T(8,128)S(1)}, u32[]{:S(2)}, u32[]{:S(2)}) collective-permute-start(f32[8,128]{1,0:T(8,128)S(1)} %copy-done.4), channel_id=1, source_target_pairs={{0,8},{8,0},{16,24},{24,16},{1,9},{9,1},{17,25},{25,17},{2,10},{10... | collective-permute-start | bytes 12296 | tf_op jit(solution)/shard_map/ppermute | solution.py:640
  34.0 2.0 %collective-permute-done.5 = f32[8,128]{1,0:T(8,128)S(1)} collective-permute-done((f32[8,128]{1,0:T(8,128)S(1)}, f32[8,128]{1,0:T(8,128)S(1)}, u32[]{:S(2)}, u32[]{:S(2)}) %collective-permute-start.5) | collective-permute-done | bytes 4128 | tf_op jit(solution)/shard_map/ppermute | solution.py:640
  36.0 1.6 %collective-permute-start.6 = (f32[8,128]{1,0:T(8,128)S(1)}, f32[8,128]{1,0:T(8,128)S(1)}, u32[]{:S(2)}, u32[]{:S(2)}) collective-permute-start(f32[8,128]{1,0:T(8,128)S(1)} %add.16), channel_id=1, source_target_pairs={{0,16},{8,24},{16,0},{24,8},{1,17},{9,25},{17,1},{25,9},{2,18},{10... | collective-permute-start | bytes 12296 | tf_op jit(solution)/shard_map/ppermute | solution.py:640
  37.6 2.0 %collective-permute-done.6 = f32[8,128]{1,0:T(8,128)S(1)} collective-permute-done((f32[8,128]{1,0:T(8,128)S(1)}, f32[8,128]{1,0:T(8,128)S(1)}, u32[]{:S(2)}, u32[]{:S(2)}) %collective-permute-start.6) | collective-permute-done | bytes 4128 | tf_op jit(solution)/shard_map/ppermute | solution.py:640
  39.6 7.5 %collective-permute-start.7 = (f32[8,128]{1,0:T(8,128)S(1)}, f32[8,128]{1,0:T(8,128)S(1)}, u32[]{:S(2)}, u32[]{:S(2)}) collective-permute-start(f32[8,128]{1,0:T(8,128)S(1)} %add.17), channel_id=1, source_target_pairs={{0,2},{2,0},{4,6},{6,4},{1,3},{3,1},{5,7},{7,5},{8,10},{10,8},{12,... | collective-permute-start | bytes 12296 | tf_op jit(solution)/shard_map/ppermute | solution.py:640
  47.2 2.0 %collective-permute-done.7 = f32[8,128]{1,0:T(8,128)S(1)} collective-permute-done((f32[8,128]{1,0:T(8,128)S(1)}, f32[8,128]{1,0:T(8,128)S(1)}, u32[]{:S(2)}, u32[]{:S(2)}) %collective-permute-start.7) | collective-permute-done | bytes 4128 | tf_op jit(solution)/shard_map/ppermute | solution.py:640
  49.2 1.4 %collective-permute-start.8 = (f32[8,128]{1,0:T(8,128)S(1)}, f32[8,128]{1,0:T(8,128)S(1)}, u32[]{:S(2)}, u32[]{:S(2)}) collective-permute-start(f32[8,128]{1,0:T(8,128)S(1)} %add.18), channel_id=1, source_target_pairs={{0,4},{2,6},{4,0},{6,2},{1,5},{3,7},{5,1},{7,3},{8,12},{10,14},{12... | collective-permute-start | bytes 12296 | tf_op jit(solution)/shard_map/ppermute | solution.py:640
  50.6 3.1 %collective-permute-done.8 = f32[8,128]{1,0:T(8,128)S(1)} collective-permute-done((f32[8,128]{1,0:T(8,128)S(1)}, f32[8,128]{1,0:T(8,128)S(1)}, u32[]{:S(2)}, u32[]{:S(2)}) %collective-permute-start.8) | collective-permute-done | bytes 4128 | tf_op jit(solution)/shard_map/ppermute | solution.py:640
  53.7 0.0 collective-permute-done.2.far_even_ref
  53.7 0.0 copy-start.2
  53.7 0.0 collective-permute-done.3.far_odd_ref
  53.7 0.0 copy-start.3
  53.7 0.8 %copy-done.2 = f32[1168,128]{1,0:T(8,128)} copy-done((f32[1168,128]{1,0:T(8,128)}, f32[1168,128]{1,0:T(8,128)S(1)}, u32[]{:S(2)}) %copy-start.2) | copy-done | bytes 598040
  54.5 0.2 copy-done.3
  54.7 3.9 %shard_map.147 = (bf16[1,128,1024]{2,1,0:T(8,128)(2,1)}, f32[1,128,16]{2,1,0:T(8,128)}, f32[256,128]{1,0:T(8,128)}) custom-call(s32[1,4]{1,0:T(1,128)} %lens_ref.5, f32[1168,128]{1,0:T(8,128)} %copy-done.2, f32[1168,128]{1,0:T(8,128)} %copy-done.3, bf16[1,128,1024]{2,1,0:T(8,128)(2,1)} %g_ref.5, f32[128,256]{1,0:T(8,128)} %get-tuple-element.28.aux_ref, ...), custom_call_target="tpu_custom_call" | custom-call | flops 100000000 | bytes 3301456 | tf_op jit(solution)/shard_map/pallas_call | solution.py:586
  58.6 0.0 collective-permute-start.4
  58.6 0.6 slice_bitcast_fusion.2
  59.2 1.5 %copy.17 = f32[1,128,16]{1,2,0:T(8,128)} copy(f32[1,128,16]{2,1,0:T(8,128)} %get-tuple-element.42) | data formatting | bytes 16384
  60.7 0.0 collective-permute-done.4
  60.7 0.9 %add.15 = f32[256,128]{1,0:T(8,128)S(1)} add(f32[256,128]{1,0:T(8,128)} %get-tuple-element.39, f32[256,128]{1,0:T(8,128)S(1)} %collective-permute-done.4) | non-fusion elementwise | flops 32768 | bytes 393216 | tf_op jit(solution)/shard_map/add | solution.py:653
  61.6 0.7 %slice_bitcast_fusion = (f32[1,128,128]{2,1,0:T(8,128)}, f32[1,128,128]{2,1,0:T(8,128)}) fusion(f32[256,128]{1,0:T(8,128)S(1)} %add.15), kind=kLoop, calls=%fused_computation | loop fusion | bytes 262144 | tf_op jit(solution)/shard_map/broadcast_in_dim | solution.py:657
  (4 shorter events, 0.0 us)
Async XLA Ops:
  5.7 17.0 %collective-permute-start = (f32[1184,128]{1,0:T(8,128)}, f32[1184,128]{1,0:T(8,128)S(1)}, u32[]{:S(2)}, u32[]{:S(2)}) collective-permute-start(f32[1184,128]{1,0:T(8,128)} %get-tuple-element.24), channel_id=1, source_target_pairs={{0,2},{2,0},{4,6},{6,4},{1,3},{3,1},{5,7},{7,5},{8,10},{10,8},{12,... | collective-permute-start | bytes 1818632 | tf_op jit(solution)/shard_map/ppermute | solution.py:615
  8.8 13.9 %collective-permute-start.1 = (f32[1184,128]{1,0:T(8,128)}, f32[1184,128]{1,0:T(8,128)S(1)}, u32[]{:S(2)}, u32[]{:S(2)}) collective-permute-start(f32[1184,128]{1,0:T(8,128)} %get-tuple-element.25), channel_id=1, source_target_pairs={{2,4},{4,2},{3,5},{5,3},{10,12},{12,10},{11,13},{13,11},{18,20},{2... | collective-permute-start | bytes 1818632 | tf_op jit(solution)/shard_map/ppermute | solution.py:614
  22.7 0.8 %copy-start = (f32[1184,128]{1,0:T(8,128)}, f32[1184,128]{1,0:T(8,128)S(1)}, u32[]{:S(2)}) copy-start(f32[1184,128]{1,0:T(8,128)S(1)} %collective-permute-done.got_even_ref) | copy-start | bytes 1818628
  22.7 1.0 %copy-start.1 = (f32[1184,128]{1,0:T(8,128)}, f32[1184,128]{1,0:T(8,128)S(1)}, u32[]{:S(2)}) copy-start(f32[1184,128]{1,0:T(8,128)S(1)} %collective-permute-done.1.got_odd_ref) | copy-start | bytes 1818628
  30.2 2.1 %copy-start.4 = (f32[8,128]{1,0:T(8,128)S(1)}, f32[8,128]{1,0:T(8,128)}, u32[]{:S(2)}) copy-start(f32[8,128]{1,0:T(8,128)} %get-tuple-element.40) | copy-start | bytes 12292
  30.2 23.5 %collective-permute-start.2 = (f32[1168,128]{1,0:T(8,128)}, f32[1168,128]{1,0:T(8,128)S(1)}, u32[]{:S(2)}, u32[]{:S(2)}) collective-permute-start(f32[1168,128]{1,0:T(8,128)} %get-tuple-element.31), channel_id=1, source_target_pairs={{2,0},{4,6},{3,1},{5,7},{10,8},{12,14},{11,9},{13,15},{18,16},{20,... | collective-permute-start | bytes 1794056 | tf_op jit(solution)/shard_map/ppermute | solution.py:634
  31.6 22.1 %collective-permute-start.3 = (f32[1168,128]{1,0:T(8,128)}, f32[1168,128]{1,0:T(8,128)S(1)}, u32[]{:S(2)}, u32[]{:S(2)}) collective-permute-start(f32[1168,128]{1,0:T(8,128)} %get-tuple-element.32), channel_id=1, source_target_pairs={{2,4},{4,2},{3,5},{5,3},{10,12},{12,10},{11,13},{13,11},{18,20},{2... | collective-permute-start | bytes 1794056 | tf_op jit(solution)/shard_map/ppermute | solution.py:635
  32.4 3.7 %collective-permute-start.5 = (f32[8,128]{1,0:T(8,128)S(1)}, f32[8,128]{1,0:T(8,128)S(1)}, u32[]{:S(2)}, u32[]{:S(2)}) collective-permute-start(f32[8,128]{1,0:T(8,128)S(1)} %copy-done.4), channel_id=1, source_target_pairs={{0,8},{8,0},{16,24},{24,16},{1,9},{9,1},{17,25},{25,17},{2,10},{10... | collective-permute-start | bytes 12296 | tf_op jit(solution)/shard_map/ppermute | solution.py:640
  36.0 3.6 %collective-permute-start.6 = (f32[8,128]{1,0:T(8,128)S(1)}, f32[8,128]{1,0:T(8,128)S(1)}, u32[]{:S(2)}, u32[]{:S(2)}) collective-permute-start(f32[8,128]{1,0:T(8,128)S(1)} %add.16), channel_id=1, source_target_pairs={{0,16},{8,24},{16,0},{24,8},{1,17},{9,25},{17,1},{25,9},{2,18},{10... | collective-permute-start | bytes 12296 | tf_op jit(solution)/shard_map/ppermute | solution.py:640
  39.6 9.5 %collective-permute-start.7 = (f32[8,128]{1,0:T(8,128)S(1)}, f32[8,128]{1,0:T(8,128)S(1)}, u32[]{:S(2)}, u32[]{:S(2)}) collective-permute-start(f32[8,128]{1,0:T(8,128)S(1)} %add.17), channel_id=1, source_target_pairs={{0,2},{2,0},{4,6},{6,4},{1,3},{3,1},{5,7},{7,5},{8,10},{10,8},{12,... | collective-permute-start | bytes 12296 | tf_op jit(solution)/shard_map/ppermute | solution.py:640
  49.2 4.5 %collective-permute-start.8 = (f32[8,128]{1,0:T(8,128)S(1)}, f32[8,128]{1,0:T(8,128)S(1)}, u32[]{:S(2)}, u32[]{:S(2)}) collective-permute-start(f32[8,128]{1,0:T(8,128)S(1)} %add.18), channel_id=1, source_target_pairs={{0,4},{2,6},{4,0},{6,2},{1,5},{3,7},{5,1},{7,3},{8,12},{10,14},{12... | collective-permute-start | bytes 12296 | tf_op jit(solution)/shard_map/ppermute | solution.py:640
  53.7 0.8 %copy-start.2 = (f32[1168,128]{1,0:T(8,128)}, f32[1168,128]{1,0:T(8,128)S(1)}, u32[]{:S(2)}) copy-start(f32[1168,128]{1,0:T(8,128)S(1)} %collective-permute-done.2.far_even_ref) | copy-start | bytes 1794052
  53.7 1.0 %copy-start.3 = (f32[1168,128]{1,0:T(8,128)}, f32[1168,128]{1,0:T(8,128)S(1)}, u32[]{:S(2)}) copy-start(f32[1168,128]{1,0:T(8,128)S(1)} %collective-permute-done.3.far_odd_ref) | copy-start | bytes 1794052
  58.6 2.1 %collective-permute-start.4 = (f32[256,128]{1,0:T(8,128)}, f32[256,128]{1,0:T(8,128)S(1)}, u32[]{:S(2)}, u32[]{:S(2)}) collective-permute-start(f32[256,128]{1,0:T(8,128)} %get-tuple-element.39), channel_id=1, source_target_pairs={{0,1},{1,0},{2,3},{3,2},{4,5},{5,4},{6,7},{7,6},{8,9},{9,8},{10,11... | collective-permute-start | bytes 393224 | tf_op jit(solution)/shard_map/ppermute | solution.py:653

commit v2 on v0

--- a/solution.py
+++ b/solution.py
@@ -1,9 +1,17 @@
 import jax
 import jax.numpy as jnp
 from jax import lax
+from jax.experimental import pallas as pl
+from jax.experimental.pallas import tpu as pltpu
 from jax.sharding import PartitionSpec as P
 
+
 SPAN = 128
+LANES = 128
+VMEM_GRANT = 16 << 20
+F32 = jnp.float32
+BF16 = jnp.bfloat16
+EXACT = lax.Precision.HIGHEST
 
 
 def from_behind(array, axis, by):
@@ -50,7 +58,7 @@
     segment_block,
     previous_block,
 ):
-    cumulative, mask_in, mask_out, factor_in, factor_out, span_total = vector_factors(
+    _, _, _, factor_in, factor_out, span_total = vector_factors(
         decay_block, segment_block, previous_block
     )
     scaled_in = (inputs_block * (factor_out * step_block)[:, :, None]).astype(jnp.bfloat16)
@@ -75,7 +83,7 @@
     decay_rate,
     skip_gain,
 ):
-    cumulative, mask_in, mask_out, factor_in, factor_out, span_total = vector_factors(
+    cumulative, mask_in, mask_out, factor_in, factor_out, _ = vector_factors(
         decay_block, segment_block, previous_block
     )
     pair_decay = pair_factor(cumulative, segment_block)
@@ -152,7 +160,7 @@
     return running
 
 
-def local(inputs, dt_raw, dt_bias, a_log, b_in, c_in, skip_gain, grad_out, doc_lengths):
+def general_local(inputs, dt_raw, dt_bias, a_log, b_in, c_in, skip_gain, grad_out, doc_lengths):
     token_count = inputs.shape[1]
     head_count = dt_bias.shape[0]
     head_width = inputs.shape[2] // head_count
@@ -219,6 +227,627 @@
     )
 
 
+def dot(left, right, dims, precision=None):
+    return lax.dot_general(
+        left, right, (dims, ((), ())), precision=precision, preferred_element_type=F32
+    )
+
+
+def nn(left, right, precision=None):
+    return dot(left, right, ((1,), (0,)), precision)
+
+
+def nt(left, right, precision=None):
+    return dot(left, right, ((1,), (1,)), precision)
+
+
+def tn(left, right, precision=None):
+    return dot(left, right, ((0,), (0,)), precision)
+
+
+def iota(shape, axis):
+    return lax.broadcasted_iota(jnp.int32, shape, axis)
+
+
+def eye(size):
+    return (iota((size, size), 0) == iota((size, size), 1)).astype(F32)
+
+
+def head_rows(heads, features):
+    width = features // heads
+    start = iota((heads, features), 0) * width
+    feature = iota((heads, features), 1)
+    return ((feature >= start) & (feature < start + width)).astype(BF16)
+
+
+def head_columns(features, heads):
+    width = features // heads
+    start = iota((features, heads), 1) * width
+    feature = iota((features, heads), 0)
+    return ((feature >= start) & (feature < start + width)).astype(BF16)
+
+
+def thirds(value):
+    high = value.astype(BF16)
+    rest = value - high.astype(F32)
+    middle = rest.astype(BF16)
+    low = (rest - middle.astype(F32)).astype(BF16)
+    return jnp.concatenate([high, middle, low], axis=0)
+
+
+def spread(factor, rows):
+    return tn(thirds(factor), jnp.concatenate([rows] * 3, axis=0))
+
+
+def spread_row(factor, features):
+    heads = factor.shape[1]
+    wide = jnp.broadcast_to(factor, (8, heads))
+    high = wide.astype(BF16)
+    rest = wide - high.astype(F32)
+    middle = rest.astype(BF16)
+    low = (rest - middle.astype(F32)).astype(BF16)
+    rows = head_rows(heads, features)
+    return (nn(high, rows) + nn(middle, rows) + nn(low, rows))[:1]
+
+
+def head_sum(values, columns):
+    high = values.astype(BF16)
+    low = (values - high.astype(F32)).astype(BF16)
+    return nn(high, columns) + nn(low, columns)
+
+
+def as_column(row):
+    size = row.shape[1]
+    return jnp.sum(jnp.where(eye(size) > 0, row, 0.0), axis=1, keepdims=True)
+
+
+def as_row(column):
+    size = column.shape[0]
+    return jnp.sum(jnp.where(eye(size) > 0, column, 0.0), axis=0, keepdims=True)
+
+
+def doc_of(lens_ref, positions):
+    count = jnp.zeros(positions.shape, jnp.int32)
+    start = jnp.int32(0)
+    for index in range(lens_ref.shape[1]):
+        count = count + (start <= positions).astype(jnp.int32)
+        start = start + lens_ref[0, index]
+    return count
+
+
+def doc_scalar(lens_ref, position):
+    count = jnp.int32(0)
+    start = jnp.int32(0)
+    for index in range(lens_ref.shape[1]):
+        count = count + jnp.where(start <= position, 1, 0)
+        start = start + lens_ref[0, index]
+    return count
+
+
+def doc_start(lens_ref, position):
+    found = jnp.int32(0)
+    start = jnp.int32(0)
+    for index in range(lens_ref.shape[1]):
+        found = jnp.where(start <= position, start, found)
+        start = start + lens_ref[0, index]
+    return found
+
+
+def leads():
+    return lax.rem(lax.axis_index("ctx"), 2) == 0
+
+
+AUX = (
+    "dt", "gate", "cum", "dout", "alpha_s", "beta_s", "alpha_u", "beta_u", "rate", "doc", "masks",
+    "short",
+)
+LOCAL = ("first", "x_gb", "skip")
+FAR = ("z_own", "w_own", "z_far", "w_far", "carried")
+
+
+def take(ref, names, name, heads):
+    slot = names.index(name) * heads
+    return ref[slot : slot + heads, :]
+
+
+def put(ref, names, heads, values):
+    for name, value in values.items():
+        slot = names.index(name) * heads
+        ref[slot : slot + heads, :] = value
+
+
+def halves(upper, lower, rows):
+    width = upper.shape[1]
+    return jnp.concatenate(
+        [jnp.broadcast_to(item, (rows // 2, width)) for item in (upper, lower)], axis=0
+    )
+
+
+def prep_kernel(
+    lens_hbm, raw_hbm, bias_hbm, alog_hbm, skip_hbm, x_hbm, g_hbm, b_hbm, c_hbm,
+    pay_one_ref, pay_two_ref, aux_ref, xs_ref, gs_ref, x_ref, g_ref, b_ref, c_ref, tot_ref,
+    gain_ref, lens_ref, raw_ref, bias_ref, alog_ref, skip_ref, sems,
+):
+    moves = (
+        (lens_hbm, lens_ref), (raw_hbm.at[0], raw_ref), (bias_hbm, bias_ref),
+        (alog_hbm, alog_ref), (skip_hbm, skip_ref), (x_hbm.at[0], x_ref), (g_hbm.at[0], g_ref),
+        (b_hbm.at[0], b_ref), (c_hbm.at[0], c_ref),
+    )
+    copies = [
+        pltpu.make_async_copy(source, target, sems.at[index])
+        for index, (source, target) in enumerate(moves)
+    ]
+    for copy in copies:
+        copy.start()
+    small, large = copies[:5], copies[5:]
+    span, features = x_ref.shape
+    heads = raw_ref.shape[0]
+    row, column = iota((span, span), 0), iota((span, span), 1)
+    upto = (row <= column).astype(F32)
+    beyond = (row > column).astype(F32)
+    rows = head_rows(heads, features)
+    for copy in small:
+        copy.wait()
+    base = lax.axis_index("ctx") * span
+    doc = doc_of(lens_ref, base + iota((1, span), 1))
+    before = doc_scalar(lens_ref, base - 1)
+    last = doc_scalar(lens_ref, base + span - 1)
+    inward = (doc == before).astype(F32)
+    outward = (doc == last).astype(F32)
+    whole = jnp.where(last == before, 1.0, 0.0)
+    short_before = jnp.where(base - doc_start(lens_ref, base - 1) <= span // 2, 1.0, 0.0)
+    short_last = jnp.where(
+        base + span - doc_start(lens_ref, base + span - 1) <= span // 2, 1.0, 0.0
+    )
+    preact = raw_ref[...] + as_column(bias_ref[...])
+    dt = jnp.maximum(preact, 0.0) + jnp.log1p(jnp.exp(-jnp.abs(preact)))
+    gate = 1.0 / (1.0 + jnp.exp(-preact))
+    rate = -jnp.exp(as_column(alog_ref[...]))
+    cum = nn(dt * rate, upto, EXACT)
+    cum_last = cum[:, span - 1 : span]
+    din = inward * jnp.exp(cum)
+    dout = outward * jnp.exp(cum_last - cum)
+    tot_ref[...] = jnp.broadcast_to(
+        spread_row(as_row(whole * jnp.exp(cum_last)), features), tot_ref.shape
+    )
+    pair = jnp.concatenate([dt, gate], axis=0)
+    seen = nn(pair * inward, upto, EXACT)
+    left = nn(pair * outward, beyond, EXACT)
+    alpha_s = rate * left[:heads]
+    beta_s = rate * left[heads:] + gate / dt
+    alpha_u = rate * seen[:heads]
+    beta_u = rate * seen[heads:]
+    put(aux_ref, AUX, heads, dict(
+        dt=dt, gate=gate, cum=cum, dout=dout,
+        alpha_s=alpha_s, beta_s=beta_s, alpha_u=alpha_u, beta_u=beta_u,
+        rate=jnp.broadcast_to(rate, dt.shape), doc=jnp.broadcast_to(doc.astype(F32), dt.shape),
+        masks=halves(inward, outward, heads),
+        short=halves(jnp.full((1, span), short_before), jnp.full((1, span), short_last), heads),
+    ))
+    gain_ref[...] = jnp.broadcast_to(spread_row(skip_ref[...], features), gain_ref.shape)
+    x_factor, g_factor = spread(dout * dt, rows), spread(din, rows)
+    for copy in large:
+        copy.wait()
+    xs = (x_ref[...].astype(F32) * x_factor).astype(BF16)
+    gs = (g_ref[...].astype(F32) * g_factor).astype(BF16)
+    xs_ref[...] = xs
+    gs_ref[...] = gs
+
+    def fill(ref, scaled, wide, small):
+        blocks = features // LANES
+        for block in range(blocks):
+            ref[block * span : (block + 1) * span, :] = scaled[
+                :, block * LANES : (block + 1) * LANES
+            ].astype(F32)
+        base = blocks * span
+        ref[base : base + span, :] = wide.astype(F32)
+        base = base + span
+        for part in small:
+            ref[base : base + heads, :] = part
+            base = base + heads
+
+    first = leads()
+
+    @pl.when(first)
+    def _():
+        fill(pay_one_ref, xs, b_ref[...], (alpha_s, beta_s))
+        fill(pay_two_ref, gs, c_ref[...], (alpha_u, beta_u))
+
+    @pl.when(jnp.logical_not(first))
+    def _():
+        fill(pay_one_ref, gs, c_ref[...], (alpha_u, beta_u))
+        fill(pay_two_ref, xs, b_ref[...], (alpha_s, beta_s))
+
+
+def local_kernel(
+    x_ref, g_ref, aux_ref, b_ref, c_ref, gb_ref, small_ref, grads_ref, own_ref
+):
+    span, features = x_ref.shape
+    heads = aux_ref.shape[0] // len(AUX)
+    width = features // heads
+    row, column = iota((span, span), 0), iota((span, span), 1)
+    dt = take(aux_ref, AUX, "dt", heads)
+    gate = take(aux_ref, AUX, "gate", heads)
+    cum = take(aux_ref, AUX, "cum", heads)
+    rate = take(aux_ref, AUX, "rate", heads)
+    doc = take(aux_ref, AUX, "doc", heads)
+    upright = nt(eye(span), jnp.concatenate([dt, cum, doc], axis=0), EXACT)
+    doc_s = upright[:, 2 * heads : 2 * heads + 1]
+    closed = jnp.where((column >= row) & (jnp.abs(doc_s - doc[:1, :]) < 0.5), 0.0, -1e30)
+    scores = nt(b_ref[...], c_ref[...])
+    summed = jnp.zeros((span, span), F32)
+    lane = iota((span, heads), 1)
+    from_s = jnp.zeros((span, heads), F32)
+    to_u = []
+    for pair in range(0, heads, 2):
+        outs = []
+        for head in (pair, pair + 1):
+            part = slice(head * width, (head + 1) * width)
+            g_head, x_head = g_ref[:, part], x_ref[:, part]
+            cross = nt(x_head, g_head)
+            cum_s = upright[:, heads + head : heads + head + 1]
+            decay = jnp.exp(cum[head : head + 1, :] - cum_s + closed)
+            masked = decay * scores
+            weighted = decay * cross * upright[:, head : head + 1]
+            summed = summed + weighted
+            product = weighted * scores
+            from_s = jnp.where(lane == head, jnp.sum(product, axis=1, keepdims=True), from_s)
+            to_u.append(jnp.sum(product, axis=0, keepdims=True))
+            outs.append(nn(masked.astype(BF16), g_head))
+        gb_ref[:, pair * width : (pair + 2) * width] = jnp.concatenate(outs, axis=1)
+    onward = (row >= column).astype(F32)
+    turn = eye(heads)
+    change = jnp.concatenate(to_u, axis=0) - nt(turn, from_s, EXACT)
+    first = nn(change, onward, EXACT)
+    columns = head_columns(features, heads)
+    x_wide = x_ref[...].astype(F32)
+    sums = jnp.concatenate(
+        [head_sum(x_wide * gb_ref[...], columns),
+         head_sum(x_wide * g_ref[...].astype(F32), columns)], axis=1
+    )
+    sums = nt(eye(2 * heads), sums, EXACT)
+    x_gb, skip = sums[:heads], sums[heads:]
+    put(small_ref, LOCAL, heads, dict(first=first, x_gb=x_gb, skip=skip))
+    own_ref[:heads, :] = rate * dt * first
+    own_ref[heads : 2 * heads, :] = gate * (x_gb + rate * first)
+    own_ref[2 * heads :, :] = skip
+    grads_ref[:span, :] = nn(summed.astype(BF16), c_ref[...])
+    grads_ref[span:, :] = nn(jnp.transpose(summed).astype(BF16), b_ref[...])
+
+
+def neighbours(one_ref, two_ref):
+    first = leads()
+
+    def behind(part):
+        return jnp.where(first, two_ref[part, :], one_ref[part, :])
+
+    def ahead(part):
+        return jnp.where(first, one_ref[part, :], two_ref[part, :])
+
+    return behind, ahead
+
+
+def wide(get, span, blocks):
+    return jnp.concatenate(
+        [get(slice(k * span, (k + 1) * span)).astype(BF16) for k in range(blocks)], axis=1
+    )
+
+
+def relay_kernel(
+    got_one_ref, got_two_ref, xs_ref, gs_ref, aux_ref, b_ref, c_ref, own_ref, tot_ref,
+    red_ref, far_ref, push_ref, far_push_ref, xp_ref, gn_ref, bp_ref, cn_ref,
+):
+    span, features = xs_ref.shape
+    heads = aux_ref.shape[0] // len(AUX)
+    blocks = features // LANES
+    behind, ahead = neighbours(got_one_ref, got_two_ref)
+    base = blocks * span
+    xp, bp = wide(behind, span, blocks), behind(slice(base, base + span)).astype(BF16)
+    gn, cn = wide(ahead, span, blocks), ahead(slice(base, base + span)).astype(BF16)
+    base = base + span
+    alpha_p = behind(slice(base, base + heads))
+    beta_p = behind(slice(base + heads, base + 2 * heads))
+    alpha_n = ahead(slice(base, base + heads))
+    beta_n = ahead(slice(base + heads, base + 2 * heads))
+    xs, gs, b, c = xs_ref[...], gs_ref[...], b_ref[...], c_ref[...]
+    columns = head_columns(features, heads)
+    gn_tot = (gn.astype(F32) * tot_ref[:1, :]).astype(BF16)
+
+    pull = nn(nt(c, bp).astype(BF16), xp)
+    push = nn(nt(b, cn).astype(BF16), gn)
+    far_pull = nn(nt(cn, bp).astype(BF16), xp)
+    far_push = nn(nt(bp, cn).astype(BF16), gn_tot)
+    products = [
+        gs.astype(F32) * pull,
+        xs.astype(F32) * push,
+        gn_tot.astype(F32) * far_pull,
+        xp.astype(F32) * far_push,
+    ]
+    sums = jnp.concatenate([nn(item.astype(BF16), columns) for item in products], axis=1)
+    sums = nt(eye(4 * heads), sums, EXACT)
+    z_own, w_own, z_far, w_far = (sums[k * heads : (k + 1) * heads] for k in range(4))
+    carried = jnp.sum(z_far, axis=1, keepdims=True)
+    rate = take(aux_ref, AUX, "rate", heads)
+    alog = (
+        own_ref[:heads, :]
+        + z_own * take(aux_ref, AUX, "alpha_u", heads)
+        + w_own * take(aux_ref, AUX, "alpha_s", heads)
+        + carried * rate * take(aux_ref, AUX, "dt", heads)
+        + z_far * alpha_n
+        + w_far * alpha_p
+    )
+    bias = (
+        own_ref[heads : 2 * heads, :]
+        + z_own * take(aux_ref, AUX, "beta_u", heads)
+        + w_own * take(aux_ref, AUX, "beta_s", heads)
+        + carried * rate * take(aux_ref, AUX, "gate", heads)
+        + z_far * beta_n
+        + w_far * beta_p
+    )
+    stack = jnp.concatenate([alog, bias, own_ref[2 * heads :, :]], axis=0)
+    red_ref[:, : 3 * heads] = nt(jnp.ones((8, span), F32), stack, EXACT)
+    red_ref[:, 3 * heads :] = jnp.zeros((8, red_ref.shape[1] - 3 * heads), F32)
+    put(far_ref, FAR, heads, dict(
+        z_own=z_own, w_own=w_own, z_far=z_far, w_far=w_far,
+        carried=jnp.broadcast_to(carried, z_own.shape),
+    ))
+    push_ref[...] = push
+    far_push_ref[...] = far_push
+    xp_ref[...] = xp
+    gn_ref[...] = gn
+    bp_ref[...] = bp
+    cn_ref[...] = cn
+
+
+def grads_kernel(
+    xp_ref, gn_ref, bp_ref, cn_ref, xs_ref, gs_ref, aux_ref, grads_ref, far_ref, far_push_ref,
+    tot_ref, hop_one_ref, hop_two_ref, sums_ref,
+):
+    span, features = xs_ref.shape
+    blocks = features // LANES
+    heads = far_ref.shape[0] // len(FAR)
+    xp, gn, bp, cn = xp_ref[...], gn_ref[...], bp_ref[...], cn_ref[...]
+    gn_tot = (gn.astype(F32) * tot_ref[:1, :]).astype(BF16)
+    sums_ref[:span, :] = grads_ref[:span, :] + nn(nt(xs_ref[...], gn).astype(BF16), cn)
+    sums_ref[span:, :] = grads_ref[span:, :] + nn(nt(gs_ref[...], xp).astype(BF16), bp)
+    grad_b_far = nn(nt(xp, gn_tot).astype(BF16), cn)
+    grad_c_far = nn(nt(gn_tot, xp).astype(BF16), bp)
+    half = span // 2
+    base = blocks * half
+    short = take(aux_ref, AUX, "short", heads)[:1, :] > 0.5
+
+    def fill(ref, grad, name, heavy):
+        if heavy:
+            for block in range(blocks):
+                part = slice(block * LANES, (block + 1) * LANES)
+                ref[block * half : (block + 1) * half, :] = jnp.where(
+                    short, far_push_ref[half:, part], gn_tot[:half, part].astype(F32)
+                )
+            ref[base : base + half, :] = cn[:half].astype(F32)
+        else:
+            ref[: base + half, :] = jnp.zeros((base + half, LANES), F32)
+        rest = base + half
+        ref[rest : rest + span, :] = grad
+        ref[rest + span : rest + span + heads, :] = take(far_ref, FAR, name, heads)
+
+    first = leads()
+
+    @pl.when(first)
+    def _():
+        fill(hop_one_ref, grad_c_far, "z_far", False)
+        fill(hop_two_ref, grad_b_far, "w_far", True)
+
+    @pl.when(jnp.logical_not(first))
+    def _():
+        fill(hop_one_ref, grad_b_far, "w_far", True)
+        fill(hop_two_ref, grad_c_far, "z_far", False)
+
+
+def final_kernel(
+    far_one_ref, far_two_ref, g_ref, b_ref, aux_ref, gain_ref, gbl_ref, push_ref, small_ref, far_ref,
+    sums_ref, gx_ref, gdt_ref, half_ref,
+):
+    span, features = g_ref.shape
+    heads = aux_ref.shape[0] // len(AUX)
+    blocks = features // LANES
+    half = span // 2
+    behind, ahead = neighbours(far_one_ref, far_two_ref)
+    base = blocks * half
+    short = take(aux_ref, AUX, "short", heads)[heads // 2 : heads // 2 + 1, :] > 0.5
+    cn = ahead(slice(base, base + half)).astype(BF16)
+    scores = nt(b_ref[...], cn).astype(BF16)
+    parts = [ahead(slice(k * half, (k + 1) * half)) for k in range(blocks)]
+    other = nn(scores, jnp.concatenate(parts, axis=1).astype(BF16))
+    blank = jnp.zeros((half, LANES), F32)
+    push = push_ref[...] + jnp.concatenate(
+        [
+            jnp.where(
+                short,
+                jnp.concatenate([blank, part], axis=0),
+                other[:, k * LANES : (k + 1) * LANES],
+            )
+            for k, part in enumerate(parts)
+        ],
+        axis=1,
+    )
+    rows = head_rows(heads, features)
+    dt = take(aux_ref, AUX, "dt", heads)
+    gate = take(aux_ref, AUX, "gate", heads)
+    dout = take(aux_ref, AUX, "dout", heads)
+    rate = take(aux_ref, AUX, "rate", heads)
+    gx_ref[0] = (
+        spread(dt, rows) * gbl_ref[...]
+        + spread(dt * dout, rows) * push
+        + gain_ref[:1, :] * g_ref[...].astype(F32)
+    ).astype(BF16)
+    inout = take(aux_ref, AUX, "masks", heads)
+    inward, outward = inout[:1, :], inout[heads // 2 : heads // 2 + 1, :]
+    rest = base + half
+    z = take(far_ref, FAR, "z_own", heads) + behind(slice(rest + span, rest + span + heads))
+    w = take(far_ref, FAR, "w_own", heads) + ahead(slice(rest + span, rest + span + heads))
+    row, column = iota((span, span), 0), iota((span, span), 1)
+    decay_grad = (
+        take(small_ref, LOCAL, "first", heads)
+        + inward * nn(z, (row >= column).astype(F32), EXACT)
+        + outward * nn(w, (row < column).astype(F32), EXACT)
+        + take(far_ref, FAR, "carried", heads)
+    )
+    x_gb = take(small_ref, LOCAL, "x_gb", heads) + w / dt
+    gdt_ref[0] = (x_gb + rate * decay_grad) * gate
+    half_ref[:span, :] = sums_ref[:span, :] + ahead(slice(rest, rest + span))
+    half_ref[span:, :] = sums_ref[span:, :] + behind(slice(rest, rest + span))
+
+
+def close_kernel(*refs):
+    count = len(refs) - 5
+    b_ref, c_ref, alog_ref, bias_ref, skip_ref = refs[count:]
+    span = b_ref.shape[1]
+    heads = alog_ref.shape[1]
+    red = refs[0][:1, :] + refs[1][:1, :]
+    alog_ref[...] = red[:, :heads]
+    bias_ref[...] = red[:, heads : 2 * heads]
+    skip_ref[...] = red[:, 2 * heads : 3 * heads]
+    total = refs[2][...]
+    for other in refs[3:count]:
+        total = total + other[...]
+    b_ref[0] = total[:span]
+    c_ref[0] = total[span:]
+
+
+def call(kernel, shapes, operands, raw=0, flops=0, scratch=()):
+    def space(index):
+        return pltpu.HBM if index < raw else pltpu.VMEM
+
+    moved = sum(item.size * item.dtype.itemsize for item in operands) + sum(
+        item.size * jnp.dtype(item.dtype).itemsize for item in shapes
+    )
+    return pl.pallas_call(
+        kernel,
+        out_shape=shapes,
+        in_specs=[pl.BlockSpec(memory_space=space(index)) for index in range(len(operands))],
+        out_specs=[pl.BlockSpec(memory_space=pltpu.VMEM)] * len(shapes),
+        scratch_shapes=list(scratch),
+        cost_estimate=pl.CostEstimate(flops=flops, bytes_accessed=moved, transcendentals=0),
+        compiler_params=pltpu.CompilerParams(vmem_limit_bytes=VMEM_GRANT),
+    )(
+        *(
+            pltpu.with_memory_space_constraint(item, pltpu.HBM) if index < raw else item
+            for index, item in enumerate(operands)
+        )
+    )
+
+
+def exchange(array, turn, senders):
+    count = lax.axis_size("ctx")
+    pairs = [(i, i + 1 if (i + turn) % 2 == 0 else i - 1) for i in range(count)]
+    return lax.ppermute(
+        array, "ctx", [(i, j) for i, j in pairs if 0 <= j < count and i in senders]
+    )
+
+
+def flip(array, axis, bit):
+    return lax.ppermute(array, axis, [(i, i ^ bit) for i in range(lax.axis_size(axis))])
+
+
+def near_local(inputs, dt_raw, dt_bias, a_log, b_in, c_in, skip_gain, grad_out, doc_lengths):
+    _, span, features = inputs.shape
+    heads = dt_bias.shape[0]
+    state = b_in.shape[2]
+    count = lax.axis_size("ctx")
+    struct = jax.ShapeDtypeStruct
+    bias, alog, skip = (item.reshape(1, heads) for item in (dt_bias, a_log, skip_gain))
+    raw = jnp.swapaxes(dt_raw, 1, 2)
+    base = features // LANES * span + span
+    pay = struct((base + 2 * heads, LANES), F32)
+    full, low = struct((span, features), F32), struct((span, features), BF16)
+    line = struct((8, features), F32)
+    square = struct((span, state), BF16)
+    pair = struct((2 * span, state), F32)
+    one_row = pltpu.VMEM((1, heads), F32)
+    pay_one, pay_two, aux, xs, gs, x, g, b, c, tot, gain = call(
+        prep_kernel,
+        (pay, pay, struct((len(AUX) * heads, span), F32), low, low, low, low, square, square, line,
+         line),
+        (doc_lengths, raw, bias, alog, skip, inputs, grad_out, b_in, c_in),
+        raw=9, flops=10**8,
+        scratch=[pltpu.SMEM(doc_lengths.shape, jnp.int32), pltpu.VMEM((heads, span), F32),
+                 one_row, one_row, one_row, pltpu.SemaphoreType.DMA((9,))],
+    )
+    got_one = exchange(pay_one, 0, range(count))
+    got_two = exchange(pay_two, 1, range(count))
+    gb_local, small, grads, own = call(
+        local_kernel,
+        (full, struct((len(LOCAL) * heads, span), F32), pair, struct((3 * heads, span), F32)),
+        (x, g, aux, b, c),
+        flops=10**8,
+    )
+    red, far, push, far_push, xp, gn, bp, cn = call(
+        relay_kernel,
+        (struct((8, LANES), F32), struct((len(FAR) * heads, span), F32), full, full, low, low,
+         square, square),
+        (got_one, got_two, xs, gs, aux, b, c, own, tot),
+        flops=10**8,
+    )
+    steps = []
+    for axis in ("dp", "ctx"):
+        bit = 1
+        while bit < lax.axis_size(axis):
+            steps.append((axis, bit))
+            bit *= 2
+    hop = struct((base // 2 + span + heads, LANES), F32)
+    hop_one, hop_two, sums = call(
+        grads_kernel,
+        (hop, hop, pair),
+        (xp, gn, bp, cn, xs, gs, aux, grads, far, far_push, tot),
+        flops=10**8,
+    )
+    hop_one, hop_two, red = lax.optimization_barrier((hop_one, hop_two, red))
+    relays = range(1, count - 1)
+    far_two = exchange(hop_two, 1, relays)
+    far_one = exchange(hop_one, 0, relays)
+    for axis, bit in steps[:-2]:
+        red = red + flip(red, axis, bit)
+    far_one, far_two, red = lax.optimization_barrier((far_one, far_two, red))
+    red = red + flip(red, *steps[-2])
+    last_red = flip(red, *steps[-1])
+    grad_x, grad_dt, half = call(
+        final_kernel,
+        (struct((1, span, features), BF16), struct((1, heads, span), F32), pair),
+        (far_one, far_two, g, b, aux, gain, gb_local, push, small, far, sums),
+        flops=10**8,
+    )
+    sides = lax.axis_size("head")
+    others = [
+        lax.ppermute(half, "head", [(i, (i + step) % sides) for i in range(sides)])
+        for step in range(1, sides)
+    ]
+    flat = struct((1, heads), F32)
+    cube = struct((1, span, state), F32)
+    b_total, c_total, alog_total, bias_total, skip_total = call(
+        close_kernel, (cube, cube, flat, flat, flat), (red, last_red, half, *others)
+    )
+    return (
+        grad_x, jnp.swapaxes(grad_dt, 1, 2), b_total, c_total,
+        alog_total.reshape(heads), bias_total.reshape(heads), skip_total.reshape(heads),
+    )
+
+
+def local(inputs, dt_raw, dt_bias, a_log, b_in, c_in, skip_gain, grad_out, doc_lengths):
+    args = (inputs, dt_raw, dt_bias, a_log, b_in, c_in, skip_gain, grad_out, doc_lengths)
+    shards = [lax.axis_size(axis) for axis in ("dp", "ctx")]
+    near = (
+        inputs.shape[1] == SPAN
+        and shards[1] in (2, 4)
+        and shards[0] & (shards[0] - 1) == 0
+        and b_in.shape[2] == LANES
+        and inputs.shape[2] % LANES == 0
+        and dt_bias.shape[0] * 8 == LANES
+    )
+    if not near:
+        return general_local(*args)
+    return near_local(*args)
+
+
 def solution(mesh):
     placed = (
         P("dp", "ctx", "head"),

time: 141 us -> 48.1 us (0.34)
  blocking collectives: 44.3 us -> 0 us
  between operations: 15.8 us -> 0.69 us
  starting transfers between devices: 30.8 us -> 15.7 us
  Pallas kernels: 0 us -> 9.75 us
  local copies, waits for them, and re-layouts: 9.75 us -> 0 us
  other arithmetic: 8.3 us -> 0.01 us
  waiting for transfers between devices: 26.8 us -> 21.7 us
  matrix products: 4.97 us -> 0 us
    psum x1 -> x0, blocking collectives: 44.3 us -> none  [local(): lax.psum((jnp.sum(grad_alog, axis=0), jnp.sum(grad_bias, axis=0), jnp.sum...]
    ppermute x10 -> x9, starting transfers between devices: 30.8 us -> 15.7 us  [the longest x4 9.95 us: flip(): lax.ppermute(array, axis, [(i, i ^ bit) for i in range(lax.axis_size(axis...]
    pallas_call x0 -> x6, Pallas kernels: none -> 9.75 us  [call(): pl.pallas_call(kernel, out_shape=shapes, in_specs=[pl.BlockSpec(memory_sp...]
    unnamed x25 -> x0, local copies, waits for them, and re-layouts: 8.06 us -> none
    ppermute x10 -> x9, waiting for transfers between devices: 26.8 us -> 21.7 us  [the longest x4 14.6 us: exchange(): lax.ppermute(array, 'ctx', [(i, j) for i, j in pairs if 0 <= j < count an...]
    dot_general x10 -> x0, matrix products: 4.97 us -> none  [the longest x1 0.9 us: span_grads(): jnp.einsum('uhp,shp->hus', grads_block, inputs_block, preferred_element_t...]
    reduce_sum x5 -> x0, other arithmetic: 1.89 us -> none  [the longest x2 1.38 us: doc_index(): jnp.sum((starts[None, :] <= positions[:, None]).astype(jnp.int32), axis=1)]
    another operation x5 -> x0, other arithmetic: 1.63 us -> none
  transfers between devices with their start and end apart: 11 -> 9, of which waited for: 5 -> 6; matrix products, arithmetic and copies ran while one was open for 5% -> 0% of each run, Pallas kernels for 0% -> 6%
where the time goes in v2:
time: 48.1 us; the launch traced here: 47.9 us
  waiting for transfers between devices  21.7 us (45%)
  starting transfers between devices  15.7 us (33%)
  Pallas kernels  9.75 us (20%)
  between operations  0.69 us (1%)
    ppermute x4, waiting for transfers between devices, exchange(): lax.ppermute(array, 'ctx', [(i, j) for i, j in pairs if 0 <= j < count an...  14.6 us
    ppermute x4, starting transfers between devices, flip(): lax.ppermute(array, axis, [(i, i ^ bit) for i in range(lax.axis_size(axis...  9.95 us
    pallas_call x6, Pallas kernels, call(): pl.pallas_call(kernel, out_shape=shapes, in_specs=[pl.BlockSpec(memory_sp...  9.75 us
    ppermute x4, waiting for transfers between devices, flip(): lax.ppermute(array, axis, [(i, i ^ bit) for i in range(lax.axis_size(axis...  7.1 us
    ppermute x4, starting transfers between devices, exchange(): lax.ppermute(array, 'ctx', [(i, j) for i, j in pairs if 0 <= j < count an...  5.78 us
  transfers between devices with their start and end apart: 9, of which 6 were waited for; matrix products, arithmetic and copies ran while one was open for 0% of the time, Pallas kernels for 6%

profile of v2, /device:TPU:0, one launch (start us, length us, event | category | flops | bytes accessed | tf_op | source)
XLA Modules:
  0.0 47.9 jit_solution(10272145311321981913)
XLA Ops:
  0.6 1.8 %shard_map.144 = (f32[1184,128]{1,0:T(8,128)S(1)}, f32[1184,128]{1,0:T(8,128)S(1)}, f32[192,128]{1,0:T(8,128)S(1)}, bf16[128,1024]{1,0:T(8,128)(2,1)S(1)}, bf16[...) custom-call(s32[1,4]{1,0:T(1,128)} %lens_hbm.1, ...), custom_call_target="tpu_custom_call" | custom-call | flops 100000000 | bytes 3088592 | tf_op jit(solution)/shard_map/pallas_call | solution.py:724
  2.5 3.1 %collective-permute-start = (f32[1184,128]{1,0:T(8,128)S(1)}, f32[1184,128]{1,0:T(8,128)S(1)}, u32[]{:S(2)}, u32[]{:S(2)}) collective-permute-start(f32[1184,128]{1,0:T(8,128)S(1)} %get-tuple-element.47), channel_id=1, source_target_pairs={{0,2},{2,0},{4,6},{6,4},{1,3},{3,1},{5,7},{7,5},{8,10},{10,8},{12,... | collective-permute-start | bytes 1818632 | tf_op jit(solution)/shard_map/ppermute | solution.py:743
  5.6 0.7 %collective-permute-start.1 = (f32[1184,128]{1,0:T(8,128)S(1)}, f32[1184,128]{1,0:T(8,128)S(1)}, u32[]{:S(2)}, u32[]{:S(2)}) collective-permute-start(f32[1184,128]{1,0:T(8,128)S(1)} %get-tuple-element.48), channel_id=1, source_target_pairs={{2,4},{4,2},{3,5},{5,3},{10,12},{12,10},{11,13},{13,11},{18,20},{2... | collective-permute-start | bytes 1818632 | tf_op jit(solution)/shard_map/ppermute | solution.py:743
  6.3 2.9 %shard_map.145 = (f32[128,1024]{1,0:T(8,128)S(1)}, f32[48,128]{1,0:T(8,128)S(1)}, f32[256,128]{1,0:T(8,128)S(1)}, f32[48,128]{1,0:T(8,128)S(1)}) custom-call(bf16[128,1024]{1,0:T(8,128)(2,1)S(1)} %get-tuple-element.54.x_ref, bf16[128,1024]{1,0:T(8,128)(2,1)S(1)} %get-tuple-element.55.g_ref, f32[192,128]{1,0:T(8,128)S(1)} %get-tuple-element.51.aux_ref, ...), custom_call_target="tpu_custom_call" | custom-call | flops 100000000 | bytes 1392640 | tf_op jit(solution)/shard_map/pallas_call | solution.py:724
  9.2 10.1 %collective-permute-done.got_one_ref = f32[1184,128]{1,0:T(8,128)S(1)} collective-permute-done((f32[1184,128]{1,0:T(8,128)S(1)}, f32[1184,128]{1,0:T(8,128)S(1)}, u32[]{:S(2)}, u32[]{:S(2)}) %collective-permute-start) | collective-permute-done | bytes 606240 | tf_op jit(solution)/shard_map/ppermute | solution.py:743
  19.3 0.0 collective-permute-done.1.got_two_ref
  19.3 1.9 %shard_map.146 = (f32[8,128]{1,0:T(8,128)S(1)}, f32[80,128]{1,0:T(8,128)S(1)}, f32[128,1024]{1,0:T(8,128)S(1)}, f32[128,1024]{1,0:T(8,128)S(1)}, bf16[128,1024]{...) custom-call(f32[1184,128]{1,0:T(8,128)S(1)} %collective-permute-done, ...), custom_call_target="tpu_custom_call" | custom-call | flops 100000000 | bytes 3641344 | tf_op jit(solution)/shard_map/pallas_call | solution.py:724
  21.1 1.2 %shard_map.147 = (f32[720,128]{1,0:T(8,128)S(1)}, f32[720,128]{1,0:T(8,128)S(1)}, f32[256,128]{1,0:T(8,128)S(1)}) custom-call(bf16[128,1024]{1,0:T(8,128)(2,1)S(1)} %get-tuple-element.58.xp_ref, bf16[128,1024]{1,0:T(8,128)(2,1)S(1)} %get-tuple-element.59.gn_ref, bf16[128,128]{1,0:T(8,128)(2,1)S(1)} %get-tuple-element.60.bp_ref, ...), custom_call_target="tpu_custom_call" | custom-call | flops 100000000 | bytes 2809856 | tf_op jit(solution)/shard_map/pallas_call | solution.py:724
  22.3 1.3 %collective-permute-start.2 = (f32[720,128]{1,0:T(8,128)S(1)}, f32[720,128]{1,0:T(8,128)S(1)}, u32[]{:S(2)}, u32[]{:S(2)}) collective-permute-start(f32[720,128]{1,0:T(8,128)S(1)} %get-tuple-element.68), channel_id=1, source_target_pairs={{2,0},{4,6},{3,1},{5,7},{10,8},{12,14},{11,9},{13,15},{18,16},{20,... | collective-permute-start | bytes 1105928 | tf_op jit(solution)/shard_map/ppermute | solution.py:743
  23.6 0.7 %collective-permute-start.3 = (f32[720,128]{1,0:T(8,128)S(1)}, f32[720,128]{1,0:T(8,128)S(1)}, u32[]{:S(2)}, u32[]{:S(2)}) collective-permute-start(f32[720,128]{1,0:T(8,128)S(1)} %get-tuple-element.69), channel_id=1, source_target_pairs={{2,4},{4,2},{3,5},{5,3},{10,12},{12,10},{11,13},{13,11},{18,20},{2... | collective-permute-start | bytes 1105928 | tf_op jit(solution)/shard_map/ppermute | solution.py:743
  24.3 1.7 %collective-permute-start.4 = (f32[8,128]{1,0:T(8,128)S(1)}, f32[8,128]{1,0:T(8,128)S(1)}, u32[]{:S(2)}, u32[]{:S(2)}) collective-permute-start(f32[8,128]{1,0:T(8,128)S(1)} %get-tuple-element.70), channel_id=1, source_target_pairs={{0,8},{8,0},{16,24},{24,16},{1,9},{9,1},{17,25},{25,17},{2,10},{10... | collective-permute-start | bytes 12296 | tf_op jit(solution)/shard_map/ppermute | solution.py:749
  26.0 2.0 %collective-permute-done.4 = f32[8,128]{1,0:T(8,128)S(1)} collective-permute-done((f32[8,128]{1,0:T(8,128)S(1)}, f32[8,128]{1,0:T(8,128)S(1)}, u32[]{:S(2)}, u32[]{:S(2)}) %collective-permute-start.4) | collective-permute-done | bytes 4128 | tf_op jit(solution)/shard_map/ppermute | solution.py:749
  28.0 1.7 %collective-permute-start.5 = (f32[8,128]{1,0:T(8,128)S(1)}, f32[8,128]{1,0:T(8,128)S(1)}, u32[]{:S(2)}, u32[]{:S(2)}) collective-permute-start(f32[8,128]{1,0:T(8,128)S(1)} %add.9), channel_id=1, source_target_pairs={{0,16},{8,24},{16,0},{24,8},{1,17},{9,25},{17,1},{25,9},{2,18},{10... | collective-permute-start | bytes 12296 | tf_op jit(solution)/shard_map/ppermute | solution.py:749
  29.7 1.9 %collective-permute-done.5 = f32[8,128]{1,0:T(8,128)S(1)} collective-permute-done((f32[8,128]{1,0:T(8,128)S(1)}, f32[8,128]{1,0:T(8,128)S(1)}, u32[]{:S(2)}, u32[]{:S(2)}) %collective-permute-start.5) | collective-permute-done | bytes 4128 | tf_op jit(solution)/shard_map/ppermute | solution.py:749
  31.6 4.5 %collective-permute-done.2.far_one_ref = f32[720,128]{1,0:T(8,128)S(1)} collective-permute-done((f32[720,128]{1,0:T(8,128)S(1)}, f32[720,128]{1,0:T(8,128)S(1)}, u32[]{:S(2)}, u32[]{:S(2)}) %collective-permute-start.2) | collective-permute-done | bytes 368672 | tf_op jit(solution)/shard_map/ppermute | solution.py:743
  36.1 0.0 collective-permute-done.3.far_two_ref
  36.1 1.3 %shard_map.148 = (bf16[1,128,1024]{2,1,0:T(8,128)(2,1)}, f32[1,16,128]{2,1,0:T(8,128)}, f32[256,128]{1,0:T(8,128)S(1)}) custom-call(f32[720,128]{1,0:T(8,128)S(1)} %collective-permute-done.2.far_one_ref, f32[720,128]{1,0:T(8,128)S(1)} %collective-permute-done.3.far_two_ref, bf16[128,1024]{1,0:T(8,128)(2,1)S(1)} %get-tuple-element.55.g_ref, ...), custom_call_target="tpu_custom_call" | custom-call | flops 100000000 | bytes 2809856 | tf_op jit(solution)/shard_map/pallas_call | solution.py:724
  37.4 0.0 collective-permute-start.8
  37.4 3.7 %collective-permute-start.6 = (f32[8,128]{1,0:T(8,128)S(1)}, f32[8,128]{1,0:T(8,128)S(1)}, u32[]{:S(2)}, u32[]{:S(2)}) collective-permute-start(f32[8,128]{1,0:T(8,128)S(1)} %add.10), channel_id=1, source_target_pairs={{0,2},{2,0},{4,6},{6,4},{1,3},{3,1},{5,7},{7,5},{8,10},{10,8},{12,... | collective-permute-start | bytes 12296 | tf_op jit(solution)/shard_map/ppermute | solution.py:749
  41.1 1.6 %collective-permute-done.6 = f32[8,128]{1,0:T(8,128)S(1)} collective-permute-done((f32[8,128]{1,0:T(8,128)S(1)}, f32[8,128]{1,0:T(8,128)S(1)}, u32[]{:S(2)}, u32[]{:S(2)}) %collective-permute-start.6) | collective-permute-done | bytes 4128 | tf_op jit(solution)/shard_map/ppermute | solution.py:749
  42.7 2.9 %collective-permute-start.7 = (f32[8,128]{1,0:T(8,128)S(1)}, f32[8,128]{1,0:T(8,128)S(1)}, u32[]{:S(2)}, u32[]{:S(2)}) collective-permute-start(f32[8,128]{1,0:T(8,128)S(1)} %add.11.refs_0_), channel_id=1, source_target_pairs={{0,4},{2,6},{4,0},{6,2},{1,5},{3,7},{5,1},{7,3},{8,12},{10,14},{12... | collective-permute-start | bytes 12296 | tf_op jit(solution)/shard_map/ppermute | solution.py:749
  45.6 1.6 %collective-permute-done.7.refs_1_ = f32[8,128]{1,0:T(8,128)S(1)} collective-permute-done((f32[8,128]{1,0:T(8,128)S(1)}, f32[8,128]{1,0:T(8,128)S(1)}, u32[]{:S(2)}, u32[]{:S(2)}) %collective-permute-start.7) | collective-permute-done | bytes 4128 | tf_op jit(solution)/shard_map/ppermute | solution.py:749
  47.2 0.0 collective-permute-done.8.refs_3_
  47.2 0.7 %shard_map.149 = (f32[1,128,128]{2,1,0:T(8,128)}, f32[1,128,128]{2,1,0:T(8,128)}, f32[1,16]{1,0:T(1,128)}, f32[1,16]{1,0:T(1,128)}, f32[1,16]{1,0:T(1,128)}) custom-call(f32[8,128]{1,0:T(8,128)S(1)} %add.11.refs_0_, f32[8,128]{1,0:T(8,128)S(1)} %collective-permute-done.7.refs_1_, f32[256,128]{1,0:T(8,128)S(1)} %get-tuple-element.81.refs_2_, ...), custom_call_target="tpu_custom_call" | custom-call | bytes 401600 | tf_op jit(solution)/shard_map/pallas_call | solution.py:724
  (3 shorter events, 0.0 us)
Async XLA Ops:
  2.5 16.8 %collective-permute-start = (f32[1184,128]{1,0:T(8,128)S(1)}, f32[1184,128]{1,0:T(8,128)S(1)}, u32[]{:S(2)}, u32[]{:S(2)}) collective-permute-start(f32[1184,128]{1,0:T(8,128)S(1)} %get-tuple-element.47), channel_id=1, source_target_pairs={{0,2},{2,0},{4,6},{6,4},{1,3},{3,1},{5,7},{7,5},{8,10},{10,8},{12,... | collective-permute-start | bytes 1818632 | tf_op jit(solution)/shard_map/ppermute | solution.py:743
  5.6 13.7 %collective-permute-start.1 = (f32[1184,128]{1,0:T(8,128)S(1)}, f32[1184,128]{1,0:T(8,128)S(1)}, u32[]{:S(2)}, u32[]{:S(2)}) collective-permute-start(f32[1184,128]{1,0:T(8,128)S(1)} %get-tuple-element.48), channel_id=1, source_target_pairs={{2,4},{4,2},{3,5},{5,3},{10,12},{12,10},{11,13},{13,11},{18,20},{2... | collective-permute-start | bytes 1818632 | tf_op jit(solution)/shard_map/ppermute | solution.py:743
  22.3 13.8 %collective-permute-start.2 = (f32[720,128]{1,0:T(8,128)S(1)}, f32[720,128]{1,0:T(8,128)S(1)}, u32[]{:S(2)}, u32[]{:S(2)}) collective-permute-start(f32[720,128]{1,0:T(8,128)S(1)} %get-tuple-element.68), channel_id=1, source_target_pairs={{2,0},{4,6},{3,1},{5,7},{10,8},{12,14},{11,9},{13,15},{18,16},{20,... | collective-permute-start | bytes 1105928 | tf_op jit(solution)/shard_map/ppermute | solution.py:743
  23.6 12.5 %collective-permute-start.3 = (f32[720,128]{1,0:T(8,128)S(1)}, f32[720,128]{1,0:T(8,128)S(1)}, u32[]{:S(2)}, u32[]{:S(2)}) collective-permute-start(f32[720,128]{1,0:T(8,128)S(1)} %get-tuple-element.69), channel_id=1, source_target_pairs={{2,4},{4,2},{3,5},{5,3},{10,12},{12,10},{11,13},{13,11},{18,20},{2... | collective-permute-start | bytes 1105928 | tf_op jit(solution)/shard_map/ppermute | solution.py:743
  24.3 3.7 %collective-permute-start.4 = (f32[8,128]{1,0:T(8,128)S(1)}, f32[8,128]{1,0:T(8,128)S(1)}, u32[]{:S(2)}, u32[]{:S(2)}) collective-permute-start(f32[8,128]{1,0:T(8,128)S(1)} %get-tuple-element.70), channel_id=1, source_target_pairs={{0,8},{8,0},{16,24},{24,16},{1,9},{9,1},{17,25},{25,17},{2,10},{10... | collective-permute-start | bytes 12296 | tf_op jit(solution)/shard_map/ppermute | solution.py:749
  28.0 3.6 %collective-permute-start.5 = (f32[8,128]{1,0:T(8,128)S(1)}, f32[8,128]{1,0:T(8,128)S(1)}, u32[]{:S(2)}, u32[]{:S(2)}) collective-permute-start(f32[8,128]{1,0:T(8,128)S(1)} %add.9), channel_id=1, source_target_pairs={{0,16},{8,24},{16,0},{24,8},{1,17},{9,25},{17,1},{25,9},{2,18},{10... | collective-permute-start | bytes 12296 | tf_op jit(solution)/shard_map/ppermute | solution.py:749
  37.4 9.8 %collective-permute-start.8 = (f32[256,128]{1,0:T(8,128)S(1)}, f32[256,128]{1,0:T(8,128)S(1)}, u32[]{:S(2)}, u32[]{:S(2)}) collective-permute-start(f32[256,128]{1,0:T(8,128)S(1)} %get-tuple-element.81.refs_2_), channel_id=1, source_target_pairs={{0,1},{1,0},{2,3},{3,2},{4,5},{5,4},{6,7},{7,6},{8,9},{9,8},{10,11... | collective-permute-start | bytes 393224 | tf_op jit(solution)/shard_map/ppermute | solution.py:821
  37.4 5.3 %collective-permute-start.6 = (f32[8,128]{1,0:T(8,128)S(1)}, f32[8,128]{1,0:T(8,128)S(1)}, u32[]{:S(2)}, u32[]{:S(2)}) collective-permute-start(f32[8,128]{1,0:T(8,128)S(1)} %add.10), channel_id=1, source_target_pairs={{0,2},{2,0},{4,6},{6,4},{1,3},{3,1},{5,7},{7,5},{8,10},{10,8},{12,... | collective-permute-start | bytes 12296 | tf_op jit(solution)/shard_map/ppermute | solution.py:749
  42.7 4.5 %collective-permute-start.7 = (f32[8,128]{1,0:T(8,128)S(1)}, f32[8,128]{1,0:T(8,128)S(1)}, u32[]{:S(2)}, u32[]{:S(2)}) collective-permute-start(f32[8,128]{1,0:T(8,128)S(1)} %add.11.refs_0_), channel_id=1, source_target_pairs={{0,4},{2,6},{4,0},{6,2},{1,5},{3,7},{5,1},{7,3},{8,12},{10,14},{12... | collective-permute-start | bytes 12296 | tf_op jit(solution)/shard_map/ppermute | solution.py:749

commit v3 on v2

--- a/solution.py
+++ b/solution.py
@@ -773,8 +773,8 @@
         scratch=[pltpu.SMEM(doc_lengths.shape, jnp.int32), pltpu.VMEM((heads, span), F32),
                  one_row, one_row, one_row, pltpu.SemaphoreType.DMA((9,))],
     )
+    got_two = exchange(pay_two, 1, range(count))
     got_one = exchange(pay_one, 0, range(count))
-    got_two = exchange(pay_two, 1, range(count))
     gb_local, small, grads, own = call(
         local_kernel,
         (full, struct((len(LOCAL) * heads, span), F32), pair, struct((3 * heads, span), F32)),
@@ -789,7 +789,7 @@
         flops=10**8,
     )
     steps = []
-    for axis in ("dp", "ctx"):
+    for axis in ("ctx", "dp"):
         bit = 1
         while bit < lax.axis_size(axis):
             steps.append((axis, bit))
@@ -801,14 +801,11 @@
         (xp, gn, bp, cn, xs, gs, aux, grads, far, far_push, tot),
         flops=10**8,
     )
-    hop_one, hop_two, red = lax.optimization_barrier((hop_one, hop_two, red))
     relays = range(1, count - 1)
     far_two = exchange(hop_two, 1, relays)
     far_one = exchange(hop_one, 0, relays)
-    for axis, bit in steps[:-2]:
+    for axis, bit in steps[:-1]:
         red = red + flip(red, axis, bit)
-    far_one, far_two, red = lax.optimization_barrier((far_one, far_two, red))
-    red = red + flip(red, *steps[-2])
     last_red = flip(red, *steps[-1])
     grad_x, grad_dt, half = call(
         final_kernel,

time: 48.1 us -> 55.3 us (1.15)
  waiting for transfers between devices: 21.7 us -> 29.3 us
    ppermute x4, waiting for transfers between devices: 14.6 us -> 21.9 us  [exchange(): lax.ppermute(array, 'ctx', [(i, j) for i, j in pairs if 0 <= j < count an...]
  transfers between devices with their start and end apart: 9 -> 9, of which waited for: 6 -> 6; matrix products, arithmetic and copies ran while one was open for 0% -> 0% of each run, Pallas kernels for 6% -> 5%
where the time goes in v3:
time: 55.3 us; the launch traced here: 55.1 us
  waiting for transfers between devices  29.3 us (53%)
  starting transfers between devices  15.4 us (28%)
  Pallas kernels  9.75 us (18%)
  between operations  0.69 us (1%)
    ppermute x4, waiting for transfers between devices, exchange(): lax.ppermute(array, 'ctx', [(i, j) for i, j in pairs if 0 <= j < count an...  21.9 us
    pallas_call x6, Pallas kernels, call(): pl.pallas_call(kernel, out_shape=shapes, in_specs=[pl.BlockSpec(memory_sp...  9.75 us
    ppermute x4, starting transfers between devices, flip(): lax.ppermute(array, axis, [(i, i ^ bit) for i in range(lax.axis_size(axis...  9.61 us
    ppermute x4, waiting for transfers between devices, flip(): lax.ppermute(array, axis, [(i, i ^ bit) for i in range(lax.axis_size(axis...  7.37 us
    ppermute x4, starting transfers between devices, exchange(): lax.ppermute(array, 'ctx', [(i, j) for i, j in pairs if 0 <= j < count an...  5.78 us
  transfers between devices with their start and end apart: 9, of which 6 were waited for; matrix products, arithmetic and copies ran while one was open for 0% of the time, Pallas kernels for 5%

profile of v3, /device:TPU:0, one launch (start us, length us, event | category | flops | bytes accessed | tf_op | source)
XLA Modules:
  0.0 55.1 jit_solution(4500852514398782972)
XLA Ops:
  0.6 1.8 %shard_map.144 = (f32[1184,128]{1,0:T(8,128)S(1)}, f32[1184,128]{1,0:T(8,128)S(1)}, f32[192,128]{1,0:T(8,128)S(1)}, bf16[128,1024]{1,0:T(8,128)(2,1)S(1)}, bf16[...) custom-call(s32[1,4]{1,0:T(1,128)} %lens_hbm.1, ...), custom_call_target="tpu_custom_call" | custom-call | flops 100000000 | bytes 3088592 | tf_op jit(solution)/shard_map/pallas_call | solution.py:724
  2.5 3.1 %collective-permute-start = (f32[1184,128]{1,0:T(8,128)S(1)}, f32[1184,128]{1,0:T(8,128)S(1)}, u32[]{:S(2)}, u32[]{:S(2)}) collective-permute-start(f32[1184,128]{1,0:T(8,128)S(1)} %get-tuple-element.41), channel_id=1, source_target_pairs={{0,2},{2,0},{4,6},{6,4},{1,3},{3,1},{5,7},{7,5},{8,10},{10,8},{12,... | collective-permute-start | bytes 1818632 | tf_op jit(solution)/shard_map/ppermute | solution.py:743
  5.6 0.7 %collective-permute-start.1 = (f32[1184,128]{1,0:T(8,128)S(1)}, f32[1184,128]{1,0:T(8,128)S(1)}, u32[]{:S(2)}, u32[]{:S(2)}) collective-permute-start(f32[1184,128]{1,0:T(8,128)S(1)} %get-tuple-element.42), channel_id=1, source_target_pairs={{2,4},{4,2},{3,5},{5,3},{10,12},{12,10},{11,13},{13,11},{18,20},{2... | collective-permute-start | bytes 1818632 | tf_op jit(solution)/shard_map/ppermute | solution.py:743
  6.3 2.9 %shard_map.145 = (f32[128,1024]{1,0:T(8,128)S(1)}, f32[48,128]{1,0:T(8,128)S(1)}, f32[256,128]{1,0:T(8,128)S(1)}, f32[48,128]{1,0:T(8,128)S(1)}) custom-call(bf16[128,1024]{1,0:T(8,128)(2,1)S(1)} %get-tuple-element.48.x_ref, bf16[128,1024]{1,0:T(8,128)(2,1)S(1)} %get-tuple-element.49.g_ref, f32[192,128]{1,0:T(8,128)S(1)} %get-tuple-element.45.aux_ref, ...), custom_call_target="tpu_custom_call" | custom-call | flops 100000000 | bytes 1392640 | tf_op jit(solution)/shard_map/pallas_call | solution.py:724
  9.2 10.1 %collective-permute-done.got_one_ref = f32[1184,128]{1,0:T(8,128)S(1)} collective-permute-done((f32[1184,128]{1,0:T(8,128)S(1)}, f32[1184,128]{1,0:T(8,128)S(1)}, u32[]{:S(2)}, u32[]{:S(2)}) %collective-permute-start) | collective-permute-done | bytes 606240 | tf_op jit(solution)/shard_map/ppermute | solution.py:743
  19.3 0.0 collective-permute-done.1.got_two_ref
  19.3 1.9 %shard_map.146 = (f32[8,128]{1,0:T(8,128)S(1)}, f32[80,128]{1,0:T(8,128)S(1)}, f32[128,1024]{1,0:T(8,128)S(1)}, f32[128,1024]{1,0:T(8,128)S(1)}, bf16[128,1024]{...) custom-call(f32[1184,128]{1,0:T(8,128)S(1)} %collective-permute-done, ...), custom_call_target="tpu_custom_call" | custom-call | flops 100000000 | bytes 3641344 | tf_op jit(solution)/shard_map/pallas_call | solution.py:724
  21.1 1.2 %shard_map.147 = (f32[720,128]{1,0:T(8,128)S(1)}, f32[720,128]{1,0:T(8,128)S(1)}, f32[256,128]{1,0:T(8,128)S(1)}) custom-call(bf16[128,1024]{1,0:T(8,128)(2,1)S(1)} %get-tuple-element.52.xp_ref, bf16[128,1024]{1,0:T(8,128)(2,1)S(1)} %get-tuple-element.53.gn_ref, bf16[128,128]{1,0:T(8,128)(2,1)S(1)} %get-tuple-element.54.bp_ref, ...), custom_call_target="tpu_custom_call" | custom-call | flops 100000000 | bytes 2809856 | tf_op jit(solution)/shard_map/pallas_call | solution.py:724
  22.3 1.3 %collective-permute-start.2 = (f32[720,128]{1,0:T(8,128)S(1)}, f32[720,128]{1,0:T(8,128)S(1)}, u32[]{:S(2)}, u32[]{:S(2)}) collective-permute-start(f32[720,128]{1,0:T(8,128)S(1)} %get-tuple-element.59), channel_id=1, source_target_pairs={{2,0},{4,6},{3,1},{5,7},{10,8},{12,14},{11,9},{13,15},{18,16},{20,... | collective-permute-start | bytes 1105928 | tf_op jit(solution)/shard_map/ppermute | solution.py:743
  23.6 0.7 %collective-permute-start.3 = (f32[720,128]{1,0:T(8,128)S(1)}, f32[720,128]{1,0:T(8,128)S(1)}, u32[]{:S(2)}, u32[]{:S(2)}) collective-permute-start(f32[720,128]{1,0:T(8,128)S(1)} %get-tuple-element.60), channel_id=1, source_target_pairs={{2,4},{4,2},{3,5},{5,3},{10,12},{12,10},{11,13},{13,11},{18,20},{2... | collective-permute-start | bytes 1105928 | tf_op jit(solution)/shard_map/ppermute | solution.py:743
  24.3 11.8 %collective-permute-done.2.far_one_ref = f32[720,128]{1,0:T(8,128)S(1)} collective-permute-done((f32[720,128]{1,0:T(8,128)S(1)}, f32[720,128]{1,0:T(8,128)S(1)}, u32[]{:S(2)}, u32[]{:S(2)}) %collective-permute-start.2) | collective-permute-done | bytes 368672 | tf_op jit(solution)/shard_map/ppermute | solution.py:743
  36.1 0.0 collective-permute-done.3.far_two_ref
  36.1 1.3 %shard_map.148 = (bf16[1,128,1024]{2,1,0:T(8,128)(2,1)}, f32[1,16,128]{2,1,0:T(8,128)}, f32[256,128]{1,0:T(8,128)S(1)}) custom-call(f32[720,128]{1,0:T(8,128)S(1)} %collective-permute-done.2.far_one_ref, f32[720,128]{1,0:T(8,128)S(1)} %collective-permute-done.3.far_two_ref, bf16[128,1024]{1,0:T(8,128)(2,1)S(1)} %get-tuple-element.49.g_ref, ...), custom_call_target="tpu_custom_call" | custom-call | flops 100000000 | bytes 2809856 | tf_op jit(solution)/shard_map/pallas_call | solution.py:724
  37.4 0.0 collective-permute-start.8
  37.4 3.7 %collective-permute-start.4 = (f32[8,128]{1,0:T(8,128)S(1)}, f32[8,128]{1,0:T(8,128)S(1)}, u32[]{:S(2)}, u32[]{:S(2)}) collective-permute-start(f32[8,128]{1,0:T(8,128)S(1)} %get-tuple-element.68), channel_id=1, source_target_pairs={{0,2},{2,0},{4,6},{6,4},{1,3},{3,1},{5,7},{7,5},{8,10},{10,8},{12,... | collective-permute-start | bytes 12296 | tf_op jit(solution)/shard_map/ppermute | solution.py:749
  41.1 1.6 %collective-permute-done.4 = f32[8,128]{1,0:T(8,128)S(1)} collective-permute-done((f32[8,128]{1,0:T(8,128)S(1)}, f32[8,128]{1,0:T(8,128)S(1)}, u32[]{:S(2)}, u32[]{:S(2)}) %collective-permute-start.4) | collective-permute-done | bytes 4128 | tf_op jit(solution)/shard_map/ppermute | solution.py:749
  42.7 2.9 %collective-permute-start.5 = (f32[8,128]{1,0:T(8,128)S(1)}, f32[8,128]{1,0:T(8,128)S(1)}, u32[]{:S(2)}, u32[]{:S(2)}) collective-permute-start(f32[8,128]{1,0:T(8,128)S(1)} %add.9), channel_id=1, source_target_pairs={{0,4},{2,6},{4,0},{6,2},{1,5},{3,7},{5,1},{7,3},{8,12},{10,14},{12... | collective-permute-start | bytes 12296 | tf_op jit(solution)/shard_map/ppermute | solution.py:749
  45.6 1.6 %collective-permute-done.5 = f32[8,128]{1,0:T(8,128)S(1)} collective-permute-done((f32[8,128]{1,0:T(8,128)S(1)}, f32[8,128]{1,0:T(8,128)S(1)}, u32[]{:S(2)}, u32[]{:S(2)}) %collective-permute-start.5) | collective-permute-done | bytes 4128 | tf_op jit(solution)/shard_map/ppermute | solution.py:749
  47.2 1.5 %collective-permute-start.6 = (f32[8,128]{1,0:T(8,128)S(1)}, f32[8,128]{1,0:T(8,128)S(1)}, u32[]{:S(2)}, u32[]{:S(2)}) collective-permute-start(f32[8,128]{1,0:T(8,128)S(1)} %add.10), channel_id=1, source_target_pairs={{0,8},{8,0},{16,24},{24,16},{1,9},{9,1},{17,25},{25,17},{2,10},{10... | collective-permute-start | bytes 12296 | tf_op jit(solution)/shard_map/ppermute | solution.py:749
  48.7 2.1 %collective-permute-done.6 = f32[8,128]{1,0:T(8,128)S(1)} collective-permute-done((f32[8,128]{1,0:T(8,128)S(1)}, f32[8,128]{1,0:T(8,128)S(1)}, u32[]{:S(2)}, u32[]{:S(2)}) %collective-permute-start.6) | collective-permute-done | bytes 4128 | tf_op jit(solution)/shard_map/ppermute | solution.py:749
  50.8 1.5 %collective-permute-start.7 = (f32[8,128]{1,0:T(8,128)S(1)}, f32[8,128]{1,0:T(8,128)S(1)}, u32[]{:S(2)}, u32[]{:S(2)}) collective-permute-start(f32[8,128]{1,0:T(8,128)S(1)} %add.11.refs_0_), channel_id=1, source_target_pairs={{0,16},{8,24},{16,0},{24,8},{1,17},{9,25},{17,1},{25,9},{2,18},{10... | collective-permute-start | bytes 12296 | tf_op jit(solution)/shard_map/ppermute | solution.py:749
  52.4 2.1 %collective-permute-done.7.refs_1_ = f32[8,128]{1,0:T(8,128)S(1)} collective-permute-done((f32[8,128]{1,0:T(8,128)S(1)}, f32[8,128]{1,0:T(8,128)S(1)}, u32[]{:S(2)}, u32[]{:S(2)}) %collective-permute-start.7) | collective-permute-done | bytes 4128 | tf_op jit(solution)/shard_map/ppermute | solution.py:749
  54.4 0.0 collective-permute-done.8.refs_3_
  54.4 0.7 %shard_map.149 = (f32[1,128,128]{2,1,0:T(8,128)}, f32[1,128,128]{2,1,0:T(8,128)}, f32[1,16]{1,0:T(1,128)}, f32[1,16]{1,0:T(1,128)}, f32[1,16]{1,0:T(1,128)}) custom-call(f32[8,128]{1,0:T(8,128)S(1)} %add.11.refs_0_, f32[8,128]{1,0:T(8,128)S(1)} %collective-permute-done.7.refs_1_, f32[256,128]{1,0:T(8,128)S(1)} %get-tuple-element.69.refs_2_, ...), custom_call_target="tpu_custom_call" | custom-call | bytes 401600 | tf_op jit(solution)/shard_map/pallas_call | solution.py:724
  (3 shorter events, 0.0 us)
Async XLA Ops:
  2.5 16.8 %collective-permute-start = (f32[1184,128]{1,0:T(8,128)S(1)}, f32[1184,128]{1,0:T(8,128)S(1)}, u32[]{:S(2)}, u32[]{:S(2)}) collective-permute-start(f32[1184,128]{1,0:T(8,128)S(1)} %get-tuple-element.41), channel_id=1, source_target_pairs={{0,2},{2,0},{4,6},{6,4},{1,3},{3,1},{5,7},{7,5},{8,10},{10,8},{12,... | collective-permute-start | bytes 1818632 | tf_op jit(solution)/shard_map/ppermute | solution.py:743
  5.6 13.7 %collective-permute-start.1 = (f32[1184,128]{1,0:T(8,128)S(1)}, f32[1184,128]{1,0:T(8,128)S(1)}, u32[]{:S(2)}, u32[]{:S(2)}) collective-permute-start(f32[1184,128]{1,0:T(8,128)S(1)} %get-tuple-element.42), channel_id=1, source_target_pairs={{2,4},{4,2},{3,5},{5,3},{10,12},{12,10},{11,13},{13,11},{18,20},{2... | collective-permute-start | bytes 1818632 | tf_op jit(solution)/shard_map/ppermute | solution.py:743
  22.3 13.8 %collective-permute-start.2 = (f32[720,128]{1,0:T(8,128)S(1)}, f32[720,128]{1,0:T(8,128)S(1)}, u32[]{:S(2)}, u32[]{:S(2)}) collective-permute-start(f32[720,128]{1,0:T(8,128)S(1)} %get-tuple-element.59), channel_id=1, source_target_pairs={{2,0},{4,6},{3,1},{5,7},{10,8},{12,14},{11,9},{13,15},{18,16},{20,... | collective-permute-start | bytes 1105928 | tf_op jit(solution)/shard_map/ppermute | solution.py:743
  23.6 12.5 %collective-permute-start.3 = (f32[720,128]{1,0:T(8,128)S(1)}, f32[720,128]{1,0:T(8,128)S(1)}, u32[]{:S(2)}, u32[]{:S(2)}) collective-permute-start(f32[720,128]{1,0:T(8,128)S(1)} %get-tuple-element.60), channel_id=1, source_target_pairs={{2,4},{4,2},{3,5},{5,3},{10,12},{12,10},{11,13},{13,11},{18,20},{2... | collective-permute-start | bytes 1105928 | tf_op jit(solution)/shard_map/ppermute | solution.py:743
  37.4 17.0 %collective-permute-start.8 = (f32[256,128]{1,0:T(8,128)S(1)}, f32[256,128]{1,0:T(8,128)S(1)}, u32[]{:S(2)}, u32[]{:S(2)}) collective-permute-start(f32[256,128]{1,0:T(8,128)S(1)} %get-tuple-element.69.refs_2_), channel_id=1, source_target_pairs={{0,1},{1,0},{2,3},{3,2},{4,5},{5,4},{6,7},{7,6},{8,9},{9,8},{10,11... | collective-permute-start | bytes 393224 | tf_op jit(solution)/shard_map/ppermute | solution.py:818
  37.4 5.3 %collective-permute-start.4 = (f32[8,128]{1,0:T(8,128)S(1)}, f32[8,128]{1,0:T(8,128)S(1)}, u32[]{:S(2)}, u32[]{:S(2)}) collective-permute-start(f32[8,128]{1,0:T(8,128)S(1)} %get-tuple-element.68), channel_id=1, source_target_pairs={{0,2},{2,0},{4,6},{6,4},{1,3},{3,1},{5,7},{7,5},{8,10},{10,8},{12,... | collective-permute-start | bytes 12296 | tf_op jit(solution)/shard_map/ppermute | solution.py:749
  42.7 4.5 %collective-permute-start.5 = (f32[8,128]{1,0:T(8,128)S(1)}, f32[8,128]{1,0:T(8,128)S(1)}, u32[]{:S(2)}, u32[]{:S(2)}) collective-permute-start(f32[8,128]{1,0:T(8,128)S(1)} %add.9), channel_id=1, source_target_pairs={{0,4},{2,6},{4,0},{6,2},{1,5},{3,7},{5,1},{7,3},{8,12},{10,14},{12... | collective-permute-start | bytes 12296 | tf_op jit(solution)/shard_map/ppermute | solution.py:749
  47.2 3.6 %collective-permute-start.6 = (f32[8,128]{1,0:T(8,128)S(1)}, f32[8,128]{1,0:T(8,128)S(1)}, u32[]{:S(2)}, u32[]{:S(2)}) collective-permute-start(f32[8,128]{1,0:T(8,128)S(1)} %add.10), channel_id=1, source_target_pairs={{0,8},{8,0},{16,24},{24,16},{1,9},{9,1},{17,25},{25,17},{2,10},{10... | collective-permute-start | bytes 12296 | tf_op jit(solution)/shard_map/ppermute | solution.py:749
  50.8 3.6 %collective-permute-start.7 = (f32[8,128]{1,0:T(8,128)S(1)}, f32[8,128]{1,0:T(8,128)S(1)}, u32[]{:S(2)}, u32[]{:S(2)}) collective-permute-start(f32[8,128]{1,0:T(8,128)S(1)} %add.11.refs_0_), channel_id=1, source_target_pairs={{0,16},{8,24},{16,0},{24,8},{1,17},{9,25},{17,1},{25,9},{2,18},{10... | collective-permute-start | bytes 12296 | tf_op jit(solution)/shard_map/ppermute | solution.py:749

commit v4 on v3

--- a/solution.py
+++ b/solution.py
@@ -1,3 +1,5 @@
+import functools
+
 import jax
 import jax.numpy as jnp
 from jax import lax
@@ -643,11 +645,25 @@
         fill(hop_two_ref, grad_c_far, "z_far", False)
 
 
+def ready_kernel(g_ref, aux_ref, gain_ref, gbl_ref, push_ref, near_ref, weight_ref):
+    features = g_ref.shape[1]
+    heads = aux_ref.shape[0] // len(AUX)
+    rows = head_rows(heads, features)
+    dt = take(aux_ref, AUX, "dt", heads)
+    weight = spread(dt * take(aux_ref, AUX, "dout", heads), rows)
+    weight_ref[...] = weight
+    near_ref[...] = (
+        spread(dt, rows) * gbl_ref[...]
+        + weight * push_ref[...]
+        + gain_ref[:1, :] * g_ref[...].astype(F32)
+    )
+
+
 def final_kernel(
-    far_one_ref, far_two_ref, g_ref, b_ref, aux_ref, gain_ref, gbl_ref, push_ref, small_ref, far_ref,
-    sums_ref, gx_ref, gdt_ref, half_ref,
+    far_one_ref, far_two_ref, b_ref, aux_ref, near_ref, weight_ref, small_ref, far_ref,
+    gx_ref, gdt_ref,
 ):
-    span, features = g_ref.shape
+    span, features = near_ref.shape
     heads = aux_ref.shape[0] // len(AUX)
     blocks = features // LANES
     half = span // 2
@@ -659,7 +675,7 @@
     parts = [ahead(slice(k * half, (k + 1) * half)) for k in range(blocks)]
     other = nn(scores, jnp.concatenate(parts, axis=1).astype(BF16))
     blank = jnp.zeros((half, LANES), F32)
-    push = push_ref[...] + jnp.concatenate(
+    push = jnp.concatenate(
         [
             jnp.where(
                 short,
@@ -670,16 +686,10 @@
         ],
         axis=1,
     )
-    rows = head_rows(heads, features)
+    gx_ref[0] = (near_ref[...] + weight_ref[...] * push).astype(BF16)
     dt = take(aux_ref, AUX, "dt", heads)
     gate = take(aux_ref, AUX, "gate", heads)
-    dout = take(aux_ref, AUX, "dout", heads)
     rate = take(aux_ref, AUX, "rate", heads)
-    gx_ref[0] = (
-        spread(dt, rows) * gbl_ref[...]
-        + spread(dt * dout, rows) * push
-        + gain_ref[:1, :] * g_ref[...].astype(F32)
-    ).astype(BF16)
     inout = take(aux_ref, AUX, "masks", heads)
     inward, outward = inout[:1, :], inout[heads // 2 : heads // 2 + 1, :]
     rest = base + half
@@ -694,6 +704,11 @@
     )
     x_gb = take(small_ref, LOCAL, "x_gb", heads) + w / dt
     gdt_ref[0] = (x_gb + rate * decay_grad) * gate
+
+
+def half_kernel(rest, far_one_ref, far_two_ref, sums_ref, half_ref):
+    span = sums_ref.shape[0] // 2
+    behind, ahead = neighbours(far_one_ref, far_two_ref)
     half_ref[:span, :] = sums_ref[:span, :] + ahead(slice(rest, rest + span))
     half_ref[span:, :] = sums_ref[span:, :] + behind(slice(rest, rest + span))
 
@@ -807,10 +822,15 @@
     for axis, bit in steps[:-1]:
         red = red + flip(red, axis, bit)
     last_red = flip(red, *steps[-1])
-    grad_x, grad_dt, half = call(
+    near, weight = call(ready_kernel, (full, full), (g, aux, gain, gb_local, push), flops=10**8)
+    half = call(
+        functools.partial(half_kernel, base // 2), (pair,), (far_one, far_two, sums),
+        flops=10**5,
+    )[0]
+    grad_x, grad_dt = call(
         final_kernel,
-        (struct((1, span, features), BF16), struct((1, heads, span), F32), pair),
-        (far_one, far_two, g, b, aux, gain, gb_local, push, small, far, sums),
+        (struct((1, span, features), BF16), struct((1, heads, span), F32)),
+        (far_one, far_two, b, aux, near, weight, small, far),
         flops=10**8,
     )
     sides = lax.axis_size("head")

time: 55.3 us -> 54.2 us (0.980)
  waiting for transfers between devices: 29.3 us -> 27.8 us
    ppermute x4, waiting for transfers between devices: 7.37 us -> 5.92 us  [flip(): lax.ppermute(array, axis, [(i, i ^ bit) for i in range(lax.axis_size(axis...]
    pallas_call x6 -> x8, Pallas kernels: 9.75 us -> 9.92 us  [call(): pl.pallas_call(kernel, out_shape=shapes, in_specs=[pl.BlockSpec(memory_sp...]
  transfers between devices with their start and end apart: 9 -> 9, of which waited for: 6 -> 6; matrix products, arithmetic and copies ran while one was open for 0% -> 0% of each run, Pallas kernels for 5% -> 8%
where the time goes in v4:
time: 54.2 us; the launch traced here: 54 us
  waiting for transfers between devices  27.8 us (51%)
  starting transfers between devices  15.5 us (29%)
  Pallas kernels  9.92 us (18%)
  between operations  0.71 us (1%)
    ppermute x4, waiting for transfers between devices, exchange(): lax.ppermute(array, 'ctx', [(i, j) for i, j in pairs if 0 <= j < count an...  21.9 us
    pallas_call x8, Pallas kernels, call(): pl.pallas_call(kernel, out_shape=shapes, in_specs=[pl.BlockSpec(memory_sp...  9.92 us
    ppermute x4, starting transfers between devices, flip(): lax.ppermute(array, axis, [(i, i ^ bit) for i in range(lax.axis_size(axis...  9.65 us
    ppermute x4, waiting for transfers between devices, flip(): lax.ppermute(array, axis, [(i, i ^ bit) for i in range(lax.axis_size(axis...  5.92 us
    ppermute x4, starting transfers between devices, exchange(): lax.ppermute(array, 'ctx', [(i, j) for i, j in pairs if 0 <= j < count an...  5.78 us
  transfers between devices with their start and end apart: 9, of which 6 were waited for; matrix products, arithmetic and copies ran while one was open for 0% of the time, Pallas kernels for 8%

profile of v4, /device:TPU:0, one launch (start us, length us, event | category | flops | bytes accessed | tf_op | source)
XLA Modules:
  0.0 54.0 jit_solution(2710802782609001952)
XLA Ops:
  0.6 1.8 %shard_map.144 = (f32[1184,128]{1,0:T(8,128)S(1)}, f32[1184,128]{1,0:T(8,128)S(1)}, f32[192,128]{1,0:T(8,128)S(1)}, bf16[128,1024]{1,0:T(8,128)(2,1)S(1)}, bf16[...) custom-call(s32[1,4]{1,0:T(1,128)} %lens_hbm.1, ...), custom_call_target="tpu_custom_call" | custom-call | flops 100000000 | bytes 3088592 | tf_op jit(solution)/shard_map/pallas_call | solution.py:739
  2.5 3.1 %collective-permute-start = (f32[1184,128]{1,0:T(8,128)S(1)}, f32[1184,128]{1,0:T(8,128)S(1)}, u32[]{:S(2)}, u32[]{:S(2)}) collective-permute-start(f32[1184,128]{1,0:T(8,128)S(1)} %get-tuple-element.42), channel_id=1, source_target_pairs={{0,2},{2,0},{4,6},{6,4},{1,3},{3,1},{5,7},{7,5},{8,10},{10,8},{12,... | collective-permute-start | bytes 1818632 | tf_op jit(solution)/shard_map/ppermute | solution.py:758
  5.6 0.7 %collective-permute-start.1 = (f32[1184,128]{1,0:T(8,128)S(1)}, f32[1184,128]{1,0:T(8,128)S(1)}, u32[]{:S(2)}, u32[]{:S(2)}) collective-permute-start(f32[1184,128]{1,0:T(8,128)S(1)} %get-tuple-element.43), channel_id=1, source_target_pairs={{2,4},{4,2},{3,5},{5,3},{10,12},{12,10},{11,13},{13,11},{18,20},{2... | collective-permute-start | bytes 1818632 | tf_op jit(solution)/shard_map/ppermute | solution.py:758
  6.3 2.9 %shard_map.145 = (f32[128,1024]{1,0:T(8,128)S(1)}, f32[48,128]{1,0:T(8,128)S(1)}, f32[256,128]{1,0:T(8,128)S(1)}, f32[48,128]{1,0:T(8,128)S(1)}) custom-call(bf16[128,1024]{1,0:T(8,128)(2,1)S(1)} %get-tuple-element.49.x_ref, bf16[128,1024]{1,0:T(8,128)(2,1)S(1)} %get-tuple-element.50.g_ref, f32[192,128]{1,0:T(8,128)S(1)} %get-tuple-element.46.aux_ref, ...), custom_call_target="tpu_custom_call" | custom-call | flops 100000000 | bytes 1392640 | tf_op jit(solution)/shard_map/pallas_call | solution.py:739
  9.2 10.1 %collective-permute-done.got_one_ref = f32[1184,128]{1,0:T(8,128)S(1)} collective-permute-done((f32[1184,128]{1,0:T(8,128)S(1)}, f32[1184,128]{1,0:T(8,128)S(1)}, u32[]{:S(2)}, u32[]{:S(2)}) %collective-permute-start) | collective-permute-done | bytes 606240 | tf_op jit(solution)/shard_map/ppermute | solution.py:758
  19.3 0.0 collective-permute-done.1.got_two_ref
  19.3 1.9 %shard_map.146 = (f32[8,128]{1,0:T(8,128)S(1)}, f32[80,128]{1,0:T(8,128)S(1)}, f32[128,1024]{1,0:T(8,128)S(1)}, f32[128,1024]{1,0:T(8,128)S(1)}, bf16[128,1024]{...) custom-call(f32[1184,128]{1,0:T(8,128)S(1)} %collective-permute-done, ...), custom_call_target="tpu_custom_call" | custom-call | flops 100000000 | bytes 3641344 | tf_op jit(solution)/shard_map/pallas_call | solution.py:739
  21.1 1.2 %shard_map.147 = (f32[720,128]{1,0:T(8,128)S(1)}, f32[720,128]{1,0:T(8,128)S(1)}, f32[256,128]{1,0:T(8,128)S(1)}) custom-call(bf16[128,1024]{1,0:T(8,128)(2,1)S(1)} %get-tuple-element.53.xp_ref, bf16[128,1024]{1,0:T(8,128)(2,1)S(1)} %get-tuple-element.54.gn_ref, bf16[128,128]{1,0:T(8,128)(2,1)S(1)} %get-tuple-element.55.bp_ref, ...), custom_call_target="tpu_custom_call" | custom-call | flops 100000000 | bytes 2809856 | tf_op jit(solution)/shard_map/pallas_call | solution.py:739
  22.3 1.3 %collective-permute-start.2 = (f32[720,128]{1,0:T(8,128)S(1)}, f32[720,128]{1,0:T(8,128)S(1)}, u32[]{:S(2)}, u32[]{:S(2)}) collective-permute-start(f32[720,128]{1,0:T(8,128)S(1)} %get-tuple-element.60), channel_id=1, source_target_pairs={{2,0},{4,6},{3,1},{5,7},{10,8},{12,14},{11,9},{13,15},{18,16},{20,... | collective-permute-start | bytes 1105928 | tf_op jit(solution)/shard_map/ppermute | solution.py:758
  23.6 0.7 %collective-permute-start.3 = (f32[720,128]{1,0:T(8,128)S(1)}, f32[720,128]{1,0:T(8,128)S(1)}, u32[]{:S(2)}, u32[]{:S(2)}) collective-permute-start(f32[720,128]{1,0:T(8,128)S(1)} %get-tuple-element.61), channel_id=1, source_target_pairs={{2,4},{4,2},{3,5},{5,3},{10,12},{12,10},{11,13},{13,11},{18,20},{2... | collective-permute-start | bytes 1105928 | tf_op jit(solution)/shard_map/ppermute | solution.py:758
  24.3 11.8 %collective-permute-done.2.far_one_ref = f32[720,128]{1,0:T(8,128)S(1)} collective-permute-done((f32[720,128]{1,0:T(8,128)S(1)}, f32[720,128]{1,0:T(8,128)S(1)}, u32[]{:S(2)}, u32[]{:S(2)}) %collective-permute-start.2) | collective-permute-done | bytes 368672 | tf_op jit(solution)/shard_map/ppermute | solution.py:758
  36.1 0.0 collective-permute-done.3.far_two_ref
  36.1 0.1 collective-permute-start.8
  36.2 3.7 %collective-permute-start.4 = (f32[8,128]{1,0:T(8,128)S(1)}, f32[8,128]{1,0:T(8,128)S(1)}, u32[]{:S(2)}, u32[]{:S(2)}) collective-permute-start(f32[8,128]{1,0:T(8,128)S(1)} %get-tuple-element.70), channel_id=1, source_target_pairs={{0,2},{2,0},{4,6},{6,4},{1,3},{3,1},{5,7},{7,5},{8,10},{10,8},{12,... | collective-permute-start | bytes 12296 | tf_op jit(solution)/shard_map/ppermute | solution.py:764
  40.0 1.6 %collective-permute-done.4 = f32[8,128]{1,0:T(8,128)S(1)} collective-permute-done((f32[8,128]{1,0:T(8,128)S(1)}, f32[8,128]{1,0:T(8,128)S(1)}, u32[]{:S(2)}, u32[]{:S(2)}) %collective-permute-start.4) | collective-permute-done | bytes 4128 | tf_op jit(solution)/shard_map/ppermute | solution.py:764
  41.6 2.9 %collective-permute-start.5 = (f32[8,128]{1,0:T(8,128)S(1)}, f32[8,128]{1,0:T(8,128)S(1)}, u32[]{:S(2)}, u32[]{:S(2)}) collective-permute-start(f32[8,128]{1,0:T(8,128)S(1)} %add.9), channel_id=1, source_target_pairs={{0,4},{2,6},{4,0},{6,2},{1,5},{3,7},{5,1},{7,3},{8,12},{10,14},{12... | collective-permute-start | bytes 12296 | tf_op jit(solution)/shard_map/ppermute | solution.py:764
  44.4 1.6 %collective-permute-done.5 = f32[8,128]{1,0:T(8,128)S(1)} collective-permute-done((f32[8,128]{1,0:T(8,128)S(1)}, f32[8,128]{1,0:T(8,128)S(1)}, u32[]{:S(2)}, u32[]{:S(2)}) %collective-permute-start.5) | collective-permute-done | bytes 4128 | tf_op jit(solution)/shard_map/ppermute | solution.py:764
  46.1 1.5 %collective-permute-start.6 = (f32[8,128]{1,0:T(8,128)S(1)}, f32[8,128]{1,0:T(8,128)S(1)}, u32[]{:S(2)}, u32[]{:S(2)}) collective-permute-start(f32[8,128]{1,0:T(8,128)S(1)} %add.10), channel_id=1, source_target_pairs={{0,8},{8,0},{16,24},{24,16},{1,9},{9,1},{17,25},{25,17},{2,10},{10... | collective-permute-start | bytes 12296 | tf_op jit(solution)/shard_map/ppermute | solution.py:764
  47.6 0.4 shard_map.148
  48.0 1.7 %collective-permute-done.6 = f32[8,128]{1,0:T(8,128)S(1)} collective-permute-done((f32[8,128]{1,0:T(8,128)S(1)}, f32[8,128]{1,0:T(8,128)S(1)}, u32[]{:S(2)}, u32[]{:S(2)}) %collective-permute-start.6) | collective-permute-done | bytes 4128 | tf_op jit(solution)/shard_map/ppermute | solution.py:764
  49.7 1.5 %collective-permute-start.7 = (f32[8,128]{1,0:T(8,128)S(1)}, f32[8,128]{1,0:T(8,128)S(1)}, u32[]{:S(2)}, u32[]{:S(2)}) collective-permute-start(f32[8,128]{1,0:T(8,128)S(1)} %add.11.refs_0_), channel_id=1, source_target_pairs={{0,16},{8,24},{16,0},{24,8},{1,17},{9,25},{17,1},{25,9},{2,18},{10... | collective-permute-start | bytes 12296 | tf_op jit(solution)/shard_map/ppermute | solution.py:764
  51.2 1.1 %shard_map.149 = (bf16[1,128,1024]{2,1,0:T(8,128)(2,1)}, f32[1,16,128]{2,1,0:T(8,128)}) custom-call(f32[720,128]{1,0:T(8,128)S(1)} %collective-permute-done.2.far_one_ref, f32[720,128]{1,0:T(8,128)S(1)} %collective-permute-done.3.far_two_ref, bf16[128,128]{1,0:T(8,128)(2,1)S(1)} %get-tuple-element.47.b_ref, f32[192,128]{1,0:T(8,128)S(1)} %get-tuple-element.46.aux_ref, ...), custom_call_target="tpu_custom_call" | custom-call | flops 100000000 | bytes 2252800 | tf_op jit(solution)/shard_map/pallas_call | solution.py:739
  52.3 1.0 %collective-permute-done.7.refs_1_ = f32[8,128]{1,0:T(8,128)S(1)} collective-permute-done((f32[8,128]{1,0:T(8,128)S(1)}, f32[8,128]{1,0:T(8,128)S(1)}, u32[]{:S(2)}, u32[]{:S(2)}) %collective-permute-start.7) | collective-permute-done | bytes 4128 | tf_op jit(solution)/shard_map/ppermute | solution.py:764
  53.3 0.0 collective-permute-done.8.refs_3_
  53.3 0.7 %shard_map.151 = (f32[1,128,128]{2,1,0:T(8,128)}, f32[1,128,128]{2,1,0:T(8,128)}, f32[1,16]{1,0:T(1,128)}, f32[1,16]{1,0:T(1,128)}, f32[1,16]{1,0:T(1,128)}) custom-call(f32[8,128]{1,0:T(8,128)S(1)} %add.11.refs_0_, f32[8,128]{1,0:T(8,128)S(1)} %collective-permute-done.7.refs_1_, f32[256,128]{1,0:T(8,128)S(1)} %shard_map.150.refs_2_, ...), custom_call_target="tpu_custom_call" | custom-call | bytes 401600 | tf_op jit(solution)/shard_map/pallas_call | solution.py:739
  (4 shorter events, 0.0 us)
Async XLA Ops:
  2.5 16.8 %collective-permute-start = (f32[1184,128]{1,0:T(8,128)S(1)}, f32[1184,128]{1,0:T(8,128)S(1)}, u32[]{:S(2)}, u32[]{:S(2)}) collective-permute-start(f32[1184,128]{1,0:T(8,128)S(1)} %get-tuple-element.42), channel_id=1, source_target_pairs={{0,2},{2,0},{4,6},{6,4},{1,3},{3,1},{5,7},{7,5},{8,10},{10,8},{12,... | collective-permute-start | bytes 1818632 | tf_op jit(solution)/shard_map/ppermute | solution.py:758
  5.6 13.7 %collective-permute-start.1 = (f32[1184,128]{1,0:T(8,128)S(1)}, f32[1184,128]{1,0:T(8,128)S(1)}, u32[]{:S(2)}, u32[]{:S(2)}) collective-permute-start(f32[1184,128]{1,0:T(8,128)S(1)} %get-tuple-element.43), channel_id=1, source_target_pairs={{2,4},{4,2},{3,5},{5,3},{10,12},{12,10},{11,13},{13,11},{18,20},{2... | collective-permute-start | bytes 1818632 | tf_op jit(solution)/shard_map/ppermute | solution.py:758
  22.3 13.8 %collective-permute-start.2 = (f32[720,128]{1,0:T(8,128)S(1)}, f32[720,128]{1,0:T(8,128)S(1)}, u32[]{:S(2)}, u32[]{:S(2)}) collective-permute-start(f32[720,128]{1,0:T(8,128)S(1)} %get-tuple-element.60), channel_id=1, source_target_pairs={{2,0},{4,6},{3,1},{5,7},{10,8},{12,14},{11,9},{13,15},{18,16},{20,... | collective-permute-start | bytes 1105928 | tf_op jit(solution)/shard_map/ppermute | solution.py:758
  23.6 12.5 %collective-permute-start.3 = (f32[720,128]{1,0:T(8,128)S(1)}, f32[720,128]{1,0:T(8,128)S(1)}, u32[]{:S(2)}, u32[]{:S(2)}) collective-permute-start(f32[720,128]{1,0:T(8,128)S(1)} %get-tuple-element.61), channel_id=1, source_target_pairs={{2,4},{4,2},{3,5},{5,3},{10,12},{12,10},{11,13},{13,11},{18,20},{2... | collective-permute-start | bytes 1105928 | tf_op jit(solution)/shard_map/ppermute | solution.py:758
  36.1 17.1 %collective-permute-start.8 = (f32[256,128]{1,0:T(8,128)S(1)}, f32[256,128]{1,0:T(8,128)S(1)}, u32[]{:S(2)}, u32[]{:S(2)}) collective-permute-start(f32[256,128]{1,0:T(8,128)S(1)} %shard_map.150.refs_2_), channel_id=1, source_target_pairs={{0,1},{1,0},{2,3},{3,2},{4,5},{5,4},{6,7},{7,6},{8,9},{9,8},{10,11... | collective-permute-start | bytes 393224 | tf_op jit(solution)/shard_map/ppermute | solution.py:838
  36.2 5.3 %collective-permute-start.4 = (f32[8,128]{1,0:T(8,128)S(1)}, f32[8,128]{1,0:T(8,128)S(1)}, u32[]{:S(2)}, u32[]{:S(2)}) collective-permute-start(f32[8,128]{1,0:T(8,128)S(1)} %get-tuple-element.70), channel_id=1, source_target_pairs={{0,2},{2,0},{4,6},{6,4},{1,3},{3,1},{5,7},{7,5},{8,10},{10,8},{12,... | collective-permute-start | bytes 12296 | tf_op jit(solution)/shard_map/ppermute | solution.py:764
  41.6 4.5 %collective-permute-start.5 = (f32[8,128]{1,0:T(8,128)S(1)}, f32[8,128]{1,0:T(8,128)S(1)}, u32[]{:S(2)}, u32[]{:S(2)}) collective-permute-start(f32[8,128]{1,0:T(8,128)S(1)} %add.9), channel_id=1, source_target_pairs={{0,4},{2,6},{4,0},{6,2},{1,5},{3,7},{5,1},{7,3},{8,12},{10,14},{12... | collective-permute-start | bytes 12296 | tf_op jit(solution)/shard_map/ppermute | solution.py:764
  46.1 3.6 %collective-permute-start.6 = (f32[8,128]{1,0:T(8,128)S(1)}, f32[8,128]{1,0:T(8,128)S(1)}, u32[]{:S(2)}, u32[]{:S(2)}) collective-permute-start(f32[8,128]{1,0:T(8,128)S(1)} %add.10), channel_id=1, source_target_pairs={{0,8},{8,0},{16,24},{24,16},{1,9},{9,1},{17,25},{25,17},{2,10},{10... | collective-permute-start | bytes 12296 | tf_op jit(solution)/shard_map/ppermute | solution.py:764
  49.7 3.6 %collective-permute-start.7 = (f32[8,128]{1,0:T(8,128)S(1)}, f32[8,128]{1,0:T(8,128)S(1)}, u32[]{:S(2)}, u32[]{:S(2)}) collective-permute-start(f32[8,128]{1,0:T(8,128)S(1)} %add.11.refs_0_), channel_id=1, source_target_pairs={{0,16},{8,24},{16,0},{24,8},{1,17},{9,25},{17,1},{25,9},{2,18},{10... | collective-permute-start | bytes 12296 | tf_op jit(solution)/shard_map/ppermute | solution.py:764

commit v5 on v4

--- a/solution.py
+++ b/solution.py
@@ -255,10 +255,11 @@
     return (iota((size, size), 0) == iota((size, size), 1)).astype(F32)
 
 
-def head_rows(heads, features):
-    width = features // heads
-    start = iota((heads, features), 0) * width
-    feature = iota((heads, features), 1)
+def head_rows(heads, width, chunk=slice(None)):
+    begin, end, _ = chunk.indices(heads * width)
+    shape = (heads, end - begin)
+    start = iota(shape, 0) * width
+    feature = iota(shape, 1) + begin
     return ((feature >= start) & (feature < start + width)).astype(BF16)
 
 
@@ -288,7 +289,7 @@
     rest = wide - high.astype(F32)
     middle = rest.astype(BF16)
     low = (rest - middle.astype(F32)).astype(BF16)
-    rows = head_rows(heads, features)
+    rows = head_rows(heads, features // heads)
     return (nn(high, rows) + nn(middle, rows) + nn(low, rows))[:1]
 
 
@@ -340,8 +341,8 @@
 
 
 AUX = (
-    "dt", "gate", "cum", "dout", "alpha_s", "beta_s", "alpha_u", "beta_u", "rate", "doc", "masks",
-    "short",
+    "dt", "gate", "cum", "din", "dout", "tot", "alpha_s", "beta_s", "alpha_u", "beta_u", "rate", "doc", "masks",
+    "short", "gain",
 )
 LOCAL = ("first", "x_gb", "skip")
 FAR = ("z_own", "w_own", "z_far", "w_far", "carried")
@@ -365,10 +366,20 @@
     )
 
 
+def fill(ref, scaled, *others):
+    span = scaled.shape[0]
+    base = 0
+    for block in range(scaled.shape[1] // LANES):
+        ref[base : base + span, :] = scaled[:, block * LANES : (block + 1) * LANES].astype(F32)
+        base = base + span
+    for part in others:
+        ref[base : base + part.shape[0], :] = part
+        base = base + part.shape[0]
+
+
 def prep_kernel(
     lens_hbm, raw_hbm, bias_hbm, alog_hbm, skip_hbm, x_hbm, g_hbm, b_hbm, c_hbm,
-    pay_one_ref, pay_two_ref, aux_ref, xs_ref, gs_ref, x_ref, g_ref, b_ref, c_ref, tot_ref,
-    gain_ref, lens_ref, raw_ref, bias_ref, alog_ref, skip_ref, sems,
+    pay_one_ref, pay_two_ref, aux_ref, xs_ref, gs_ref, x_ref, g_ref, b_ref, c_ref, lens_ref, raw_ref, bias_ref, alog_ref, skip_ref, sems,
 ):
     moves = (
         (lens_hbm, lens_ref), (raw_hbm.at[0], raw_ref), (bias_hbm, bias_ref),
@@ -387,7 +398,8 @@
     row, column = iota((span, span), 0), iota((span, span), 1)
     upto = (row <= column).astype(F32)
     beyond = (row > column).astype(F32)
-    rows = head_rows(heads, features)
+    part = slice(0, features // 2)
+    rows = head_rows(heads, features // heads, part)
     for copy in small:
         copy.wait()
     base = lax.axis_index("ctx") * span
@@ -409,9 +421,6 @@
     cum_last = cum[:, span - 1 : span]
     din = inward * jnp.exp(cum)
     dout = outward * jnp.exp(cum_last - cum)
-    tot_ref[...] = jnp.broadcast_to(
-        spread_row(as_row(whole * jnp.exp(cum_last)), features), tot_ref.shape
-    )
     pair = jnp.concatenate([dt, gate], axis=0)
     seen = nn(pair * inward, upto, EXACT)
     left = nn(pair * outward, beyond, EXACT)
@@ -420,45 +429,63 @@
     alpha_u = rate * seen[:heads]
     beta_u = rate * seen[heads:]
     put(aux_ref, AUX, heads, dict(
-        dt=dt, gate=gate, cum=cum, dout=dout,
+        dt=dt, gate=gate, cum=cum, din=din, dout=dout,
+        tot=jnp.broadcast_to(whole * jnp.exp(cum_last), dt.shape),
+        gain=jnp.broadcast_to(as_column(skip_ref[...]), dt.shape),
         alpha_s=alpha_s, beta_s=beta_s, alpha_u=alpha_u, beta_u=beta_u,
         rate=jnp.broadcast_to(rate, dt.shape), doc=jnp.broadcast_to(doc.astype(F32), dt.shape),
         masks=halves(inward, outward, heads),
         short=halves(jnp.full((1, span), short_before), jnp.full((1, span), short_last), heads),
     ))
-    gain_ref[...] = jnp.broadcast_to(spread_row(skip_ref[...], features), gain_ref.shape)
     x_factor, g_factor = spread(dout * dt, rows), spread(din, rows)
     for copy in large:
         copy.wait()
-    xs = (x_ref[...].astype(F32) * x_factor).astype(BF16)
-    gs = (g_ref[...].astype(F32) * g_factor).astype(BF16)
+    xs = (x_ref[:, part].astype(F32) * x_factor).astype(BF16)
+    gs = (g_ref[:, part].astype(F32) * g_factor).astype(BF16)
     xs_ref[...] = xs
     gs_ref[...] = gs
-
-    def fill(ref, scaled, wide, small):
-        blocks = features // LANES
-        for block in range(blocks):
-            ref[block * span : (block + 1) * span, :] = scaled[
-                :, block * LANES : (block + 1) * LANES
-            ].astype(F32)
-        base = blocks * span
-        ref[base : base + span, :] = wide.astype(F32)
-        base = base + span
-        for part in small:
-            ref[base : base + heads, :] = part
-            base = base + heads
-
     first = leads()
+
+    def mine(ref):
+        rows = span // lax.axis_size("head")
+        start = pl.multiple_of(lax.axis_index("head") * rows, rows)
+        return ref[pl.ds(start, rows), :].astype(F32)
 
     @pl.when(first)
     def _():
-        fill(pay_one_ref, xs, b_ref[...], (alpha_s, beta_s))
-        fill(pay_two_ref, gs, c_ref[...], (alpha_u, beta_u))
+        fill(pay_one_ref, xs, mine(b_ref), alpha_s, beta_s)
+        fill(pay_two_ref, gs, mine(c_ref), alpha_u, beta_u)
 
     @pl.when(jnp.logical_not(first))
     def _():
-        fill(pay_one_ref, gs, c_ref[...], (alpha_u, beta_u))
-        fill(pay_two_ref, xs, b_ref[...], (alpha_s, beta_s))
+        fill(pay_one_ref, gs, mine(c_ref), alpha_u, beta_u)
+        fill(pay_two_ref, xs, mine(b_ref), alpha_s, beta_s)
+
+
+def rest_kernel(x_ref, g_ref, aux_ref, pay_one_ref, pay_two_ref, xs_ref, gs_ref, tot_ref, gain_ref):
+    features = x_ref.shape[1]
+    heads = aux_ref.shape[0] // len(AUX)
+    part = slice(features // 2, features)
+    rows = head_rows(heads, features // heads, part)
+    dout, dt = take(aux_ref, AUX, "dout", heads), take(aux_ref, AUX, "dt", heads)
+    xs = (x_ref[:, part].astype(F32) * spread(dout * dt, rows)).astype(BF16)
+    gs = (g_ref[:, part].astype(F32) * spread(take(aux_ref, AUX, "din", heads), rows)).astype(BF16)
+    xs_ref[...] = xs
+    gs_ref[...] = gs
+    for name, ref in (("tot", tot_ref), ("gain", gain_ref)):
+        row = as_row(take(aux_ref, AUX, name, heads)[:, :1])
+        ref[...] = jnp.broadcast_to(spread_row(row, features), ref.shape)
+    first = leads()
+
+    @pl.when(first)
+    def _():
+        fill(pay_one_ref, xs)
+        fill(pay_two_ref, gs)
+
+    @pl.when(jnp.logical_not(first))
+    def _():
+        fill(pay_one_ref, gs)
+        fill(pay_two_ref, xs)
 
 
 def local_kernel(
@@ -535,39 +562,89 @@
     )
 
 
-def relay_kernel(
-    got_one_ref, got_two_ref, xs_ref, gs_ref, aux_ref, b_ref, c_ref, own_ref, tot_ref,
-    red_ref, far_ref, push_ref, far_push_ref, xp_ref, gn_ref, bp_ref, cn_ref,
-):
-    span, features = xs_ref.shape
-    heads = aux_ref.shape[0] // len(AUX)
-    blocks = features // LANES
-    behind, ahead = neighbours(got_one_ref, got_two_ref)
-    base = blocks * span
-    xp, bp = wide(behind, span, blocks), behind(slice(base, base + span)).astype(BF16)
-    gn, cn = wide(ahead, span, blocks), ahead(slice(base, base + span)).astype(BF16)
-    base = base + span
-    alpha_p = behind(slice(base, base + heads))
-    beta_p = behind(slice(base + heads, base + 2 * heads))
-    alpha_n = ahead(slice(base, base + heads))
-    beta_n = ahead(slice(base + heads, base + 2 * heads))
-    xs, gs, b, c = xs_ref[...], gs_ref[...], b_ref[...], c_ref[...]
-    columns = head_columns(features, heads)
-    gn_tot = (gn.astype(F32) * tot_ref[:1, :]).astype(BF16)
-
-    pull = nn(nt(c, bp).astype(BF16), xp)
-    push = nn(nt(b, cn).astype(BF16), gn)
-    far_pull = nn(nt(cn, bp).astype(BF16), xp)
-    far_push = nn(nt(bp, cn).astype(BF16), gn_tot)
-    products = [
+def relay_terms(xp, gn, xs, gs, tot, scores, rows, push_ref, far_push_ref):
+    gn_tot = (gn.astype(F32) * tot).astype(BF16)
+    pull, push = nn(scores[0], xp), nn(scores[1], gn)
+    far_pull, far_push = nn(scores[2], xp), nn(scores[3], gn_tot)
+    push_ref[...] = push
+    far_push_ref[...] = far_push
+    products = (
         gs.astype(F32) * pull,
         xs.astype(F32) * push,
         gn_tot.astype(F32) * far_pull,
         xp.astype(F32) * far_push,
-    ]
-    sums = jnp.concatenate([nn(item.astype(BF16), columns) for item in products], axis=1)
-    sums = nt(eye(4 * heads), sums, EXACT)
-    z_own, w_own, z_far, w_far = (sums[k * heads : (k + 1) * heads] for k in range(4))
+    )
+    return [nt(rows, item.astype(BF16)) for item in products]
+
+
+def maps_kernel(base, got_one_ref, got_two_ref, maps_ref):
+    behind, ahead = neighbours(got_one_ref, got_two_ref)
+    rows = maps_ref.shape[0] // 2
+    maps_ref[:rows, :] = behind(slice(base, base + rows))
+    maps_ref[rows:, :] = ahead(slice(base, base + rows))
+
+
+def relay_first_kernel(
+    got_one_ref, got_two_ref, maps_ref, other_ref, xs_ref, gs_ref, b_ref, c_ref, tot_ref, aux_ref,
+    push_ref, far_push_ref, xp_ref, gn_ref, bp_ref, cn_ref, scores_ref, part_ref, weights_ref,
+):
+    span, features = xs_ref.shape
+    heads = aux_ref.shape[0] // len(AUX)
+    width = tot_ref.shape[1] // heads
+    blocks = features // LANES
+    behind, ahead = neighbours(got_one_ref, got_two_ref)
+    rows = span // 2
+    lower = lax.axis_index("head") == 0
+
+    def whole(part):
+        one, two = maps_ref[part, :], other_ref[part, :]
+        return jnp.concatenate(
+            [jnp.where(lower, one, two), jnp.where(lower, two, one)], axis=0
+        ).astype(BF16)
+
+    xp, bp = wide(behind, span, blocks), whole(slice(0, rows))
+    gn, cn = wide(ahead, span, blocks), whole(slice(rows, 2 * rows))
+    base = blocks * span + rows
+    weights_ref[: 2 * heads, :] = behind(slice(base, base + 2 * heads))
+    weights_ref[2 * heads :, :] = ahead(slice(base, base + 2 * heads))
+    b, c = b_ref[...], c_ref[...]
+    scores = [item.astype(BF16) for item in (nt(c, bp), nt(b, cn), nt(cn, bp), nt(bp, cn))]
+    part = slice(0, features)
+    sums = relay_terms(
+        xp, gn, xs_ref[...], gs_ref[...], tot_ref[:1, part], scores,
+        head_rows(heads, width, part), push_ref, far_push_ref,
+    )
+    for index in range(4):
+        scores_ref[index * span : (index + 1) * span, :] = scores[index]
+        part_ref[index * heads : (index + 1) * heads, :] = sums[index]
+    xp_ref[...] = xp
+    gn_ref[...] = gn
+    bp_ref[...] = bp
+    cn_ref[...] = cn
+
+
+def relay_kernel(
+    got_one_ref, got_two_ref, xs_ref, gs_ref, tot_ref, aux_ref, scores_ref, part_ref, weights_ref,
+    own_ref, red_ref, far_ref, push_ref, far_push_ref, xp_ref, gn_ref,
+):
+    span, features = xs_ref.shape
+    heads = aux_ref.shape[0] // len(AUX)
+    total = tot_ref.shape[1]
+    blocks = features // LANES
+    behind, ahead = neighbours(got_one_ref, got_two_ref)
+    xp, gn = wide(behind, span, blocks), wide(ahead, span, blocks)
+    part = slice(total - features, total)
+    sums = relay_terms(
+        xp, gn, xs_ref[...], gs_ref[...], tot_ref[:1, part],
+        [scores_ref[index * span : (index + 1) * span, :] for index in range(4)],
+        head_rows(heads, total // heads, part), push_ref, far_push_ref,
+    )
+    z_own, w_own, z_far, w_far = (
+        sums[index] + part_ref[index * heads : (index + 1) * heads, :] for index in range(4)
+    )
+    alpha_p, beta_p, alpha_n, beta_n = (
+        weights_ref[index * heads : (index + 1) * heads, :] for index in range(4)
+    )
     carried = jnp.sum(z_far, axis=1, keepdims=True)
     rate = take(aux_ref, AUX, "rate", heads)
     alog = (
@@ -593,68 +670,82 @@
         z_own=z_own, w_own=w_own, z_far=z_far, w_far=w_far,
         carried=jnp.broadcast_to(carried, z_own.shape),
     ))
-    push_ref[...] = push
-    far_push_ref[...] = far_push
     xp_ref[...] = xp
     gn_ref[...] = gn
-    bp_ref[...] = bp
-    cn_ref[...] = cn
-
-
-def grads_kernel(
-    xp_ref, gn_ref, bp_ref, cn_ref, xs_ref, gs_ref, aux_ref, grads_ref, far_ref, far_push_ref,
-    tot_ref, hop_one_ref, hop_two_ref, sums_ref,
+
+
+def both(one_ref, two_ref):
+    return jnp.concatenate([one_ref[...], two_ref[...]], axis=1)
+
+
+def hops_kernel(
+    xp0_ref, xp1_ref, gn0_ref, gn1_ref, bp_ref, cn_ref, aux_ref, far_ref, push0_ref, push1_ref,
+    tot_ref, hop_one_ref, hop_two_ref,
 ):
-    span, features = xs_ref.shape
+    xp, gn, bp, cn = both(xp0_ref, xp1_ref), both(gn0_ref, gn1_ref), bp_ref[...], cn_ref[...]
+    span, features = xp.shape
     blocks = features // LANES
     heads = far_ref.shape[0] // len(FAR)
-    xp, gn, bp, cn = xp_ref[...], gn_ref[...], bp_ref[...], cn_ref[...]
     gn_tot = (gn.astype(F32) * tot_ref[:1, :]).astype(BF16)
-    sums_ref[:span, :] = grads_ref[:span, :] + nn(nt(xs_ref[...], gn).astype(BF16), cn)
-    sums_ref[span:, :] = grads_ref[span:, :] + nn(nt(gs_ref[...], xp).astype(BF16), bp)
     grad_b_far = nn(nt(xp, gn_tot).astype(BF16), cn)
     grad_c_far = nn(nt(gn_tot, xp).astype(BF16), bp)
     half = span // 2
     base = blocks * half
     short = take(aux_ref, AUX, "short", heads)[:1, :] > 0.5
 
-    def fill(ref, grad, name, heavy):
+    def load(ref, grad, name, heavy):
         if heavy:
             for block in range(blocks):
-                part = slice(block * LANES, (block + 1) * LANES)
+                push_ref = (push0_ref, push1_ref)[block * 2 // blocks]
+                inner = (block % (blocks // 2)) * LANES
                 ref[block * half : (block + 1) * half, :] = jnp.where(
-                    short, far_push_ref[half:, part], gn_tot[:half, part].astype(F32)
+                    short,
+                    push_ref[half:, inner : inner + LANES],
+                    gn_tot[:half, block * LANES : (block + 1) * LANES].astype(F32),
                 )
-            ref[base : base + half, :] = cn[:half].astype(F32)
+            ref[base : base + half, :] = jnp.where(short, grad[half:], cn[:half].astype(F32))
         else:
-            ref[: base + half, :] = jnp.zeros((base + half, LANES), F32)
+            ref[:span, :] = grad
+            ref[span : base + half, :] = jnp.zeros((base + half - span, LANES), F32)
         rest = base + half
-        ref[rest : rest + span, :] = grad
-        ref[rest + span : rest + span + heads, :] = take(far_ref, FAR, name, heads)
+        ref[rest : rest + heads, :] = take(far_ref, FAR, name, heads)
 
     first = leads()
 
     @pl.when(first)
     def _():
-        fill(hop_one_ref, grad_c_far, "z_far", False)
-        fill(hop_two_ref, grad_b_far, "w_far", True)
+        load(hop_one_ref, grad_c_far, "z_far", False)
+        load(hop_two_ref, grad_b_far, "w_far", True)
 
     @pl.when(jnp.logical_not(first))
     def _():
-        fill(hop_one_ref, grad_b_far, "w_far", True)
-        fill(hop_two_ref, grad_c_far, "z_far", False)
-
-
-def ready_kernel(g_ref, aux_ref, gain_ref, gbl_ref, push_ref, near_ref, weight_ref):
+        load(hop_one_ref, grad_b_far, "w_far", True)
+        load(hop_two_ref, grad_c_far, "z_far", False)
+
+
+def grads_kernel(
+    xp0_ref, xp1_ref, gn0_ref, gn1_ref, bp_ref, cn_ref, xs0_ref, xs1_ref, gs0_ref, gs1_ref,
+    grads_ref, sums_ref,
+):
+    xp, gn = both(xp0_ref, xp1_ref), both(gn0_ref, gn1_ref)
+    xs, gs = both(xs0_ref, xs1_ref), both(gs0_ref, gs1_ref)
+    span = xp.shape[0]
+    sums_ref[:span, :] = grads_ref[:span, :] + nn(nt(xs, gn).astype(BF16), cn_ref[...])
+    sums_ref[span:, :] = grads_ref[span:, :] + nn(nt(gs, xp).astype(BF16), bp_ref[...])
+
+
+def ready_kernel(
+    g_ref, aux_ref, gain_ref, gbl_ref, push0_ref, push1_ref, near_ref, weight_ref
+):
     features = g_ref.shape[1]
     heads = aux_ref.shape[0] // len(AUX)
-    rows = head_rows(heads, features)
+    rows = head_rows(heads, features // heads)
     dt = take(aux_ref, AUX, "dt", heads)
     weight = spread(dt * take(aux_ref, AUX, "dout", heads), rows)
     weight_ref[...] = weight
     near_ref[...] = (
         spread(dt, rows) * gbl_ref[...]
-        + weight * push_ref[...]
+        + weight * both(push0_ref, push1_ref)
         + gain_ref[:1, :] * g_ref[...].astype(F32)
     )
 
@@ -693,8 +784,8 @@
     inout = take(aux_ref, AUX, "masks", heads)
     inward, outward = inout[:1, :], inout[heads // 2 : heads // 2 + 1, :]
     rest = base + half
-    z = take(far_ref, FAR, "z_own", heads) + behind(slice(rest + span, rest + span + heads))
-    w = take(far_ref, FAR, "w_own", heads) + ahead(slice(rest + span, rest + span + heads))
+    z = take(far_ref, FAR, "z_own", heads) + behind(slice(rest, rest + heads))
+    w = take(far_ref, FAR, "w_own", heads) + ahead(slice(rest, rest + heads))
     row, column = iota((span, span), 0), iota((span, span), 1)
     decay_grad = (
         take(small_ref, LOCAL, "first", heads)
@@ -706,27 +797,34 @@
     gdt_ref[0] = (x_gb + rate * decay_grad) * gate
 
 
-def half_kernel(rest, far_one_ref, far_two_ref, sums_ref, half_ref):
-    span = sums_ref.shape[0] // 2
+def half_kernel(far_one_ref, far_two_ref, xs0_ref, xs1_ref, aux_ref, sums_ref, half_ref):
+    xs = both(xs0_ref, xs1_ref)
+    span, features = xs.shape
+    heads = aux_ref.shape[0] // len(AUX)
+    half = span // 2
+    blocks = features // LANES
+    base = blocks * half
     behind, ahead = neighbours(far_one_ref, far_two_ref)
-    half_ref[:span, :] = sums_ref[:span, :] + ahead(slice(rest, rest + span))
-    half_ref[span:, :] = sums_ref[span:, :] + behind(slice(rest, rest + span))
-
-
-def close_kernel(*refs):
-    count = len(refs) - 5
-    b_ref, c_ref, alog_ref, bias_ref, skip_ref = refs[count:]
+    short = take(aux_ref, AUX, "short", heads)[heads // 2 : heads // 2 + 1, :] > 0.5
+    last = ahead(slice(base, base + half))
+    gn = wide(ahead, half, blocks)
+    grad = nn(nt(xs, gn).astype(BF16), last.astype(BF16))
+    share = jnp.concatenate([jnp.zeros_like(last), last], axis=0)
+    half_ref[:span, :] = sums_ref[:span, :] + jnp.where(short, share, grad)
+    half_ref[span:, :] = sums_ref[span:, :] + behind(slice(0, span))
+
+
+def close_kernel(
+    red_ref, last_ref, half_ref, other_ref, b_ref, c_ref, alog_ref, bias_ref, skip_ref
+):
     span = b_ref.shape[1]
     heads = alog_ref.shape[1]
-    red = refs[0][:1, :] + refs[1][:1, :]
+    red = red_ref[:1, :] + last_ref[:1, :]
     alog_ref[...] = red[:, :heads]
     bias_ref[...] = red[:, heads : 2 * heads]
     skip_ref[...] = red[:, 2 * heads : 3 * heads]
-    total = refs[2][...]
-    for other in refs[3:count]:
-        total = total + other[...]
-    b_ref[0] = total[:span]
-    c_ref[0] = total[span:]
+    b_ref[0] = half_ref[:span, :] + other_ref[:span, :]
+    c_ref[0] = half_ref[span:, :] + other_ref[span:, :]
 
 
 def call(kernel, shapes, operands, raw=0, flops=0, scratch=()):
@@ -772,17 +870,23 @@
     struct = jax.ShapeDtypeStruct
     bias, alog, skip = (item.reshape(1, heads) for item in (dt_bias, a_log, skip_gain))
     raw = jnp.swapaxes(dt_raw, 1, 2)
-    base = features // LANES * span + span
-    pay = struct((base + 2 * heads, LANES), F32)
+    split = features // 2
+    sides = lax.axis_size("head")
+    blocks = split // LANES * span
+    base = 2 * blocks + span
+    pay = struct((blocks + span // sides + 2 * heads, LANES), F32)
+    pay_rest = struct((blocks, LANES), F32)
     full, low = struct((span, features), F32), struct((span, features), BF16)
+    full_part, low_part = struct((span, split), F32), struct((span, split), BF16)
     line = struct((8, features), F32)
     square = struct((span, state), BF16)
     pair = struct((2 * span, state), F32)
+    quad = struct((4 * heads, span), F32)
     one_row = pltpu.VMEM((1, heads), F32)
-    pay_one, pay_two, aux, xs, gs, x, g, b, c, tot, gain = call(
+    pay_one, pay_two, aux, xs0, gs0, x, g, b, c = call(
         prep_kernel,
-        (pay, pay, struct((len(AUX) * heads, span), F32), low, low, low, low, square, square, line,
-         line),
+        (pay, pay, struct((len(AUX) * heads, span), F32), low_part, low_part, low, low, square,
+         square),
         (doc_lengths, raw, bias, alog, skip, inputs, grad_out, b_in, c_in),
         raw=9, flops=10**8,
         scratch=[pltpu.SMEM(doc_lengths.shape, jnp.int32), pltpu.VMEM((heads, span), F32),
@@ -790,17 +894,34 @@
     )
     got_two = exchange(pay_two, 1, range(count))
     got_one = exchange(pay_one, 0, range(count))
+    pay_one, pay_two, xs1, gs1, tot, gain = call(
+        rest_kernel, (pay_rest, pay_rest, low_part, low_part, line, line), (x, g, aux), flops=10**7
+    )
+    more_two = exchange(pay_two, 1, range(count))
+    more_one = exchange(pay_one, 0, range(count))
     gb_local, small, grads, own = call(
         local_kernel,
         (full, struct((len(LOCAL) * heads, span), F32), pair, struct((3 * heads, span), F32)),
         (x, g, aux, b, c),
         flops=10**8,
     )
-    red, far, push, far_push, xp, gn, bp, cn = call(
+    maps = call(
+        functools.partial(maps_kernel, blocks), (struct((2 * span // sides, state), F32),),
+        (got_one, got_two), flops=10**5,
+    )[0]
+    other_maps = flip(maps, "head", 1)
+    push0, far_push0, xp0, gn0, bp, cn, scores, part, weights = call(
+        relay_first_kernel,
+        (full_part, full_part, low_part, low_part, square, square,
+         struct((4 * span, span), BF16), quad, quad),
+        (got_one, got_two, maps, other_maps, xs0, gs0, b, c, tot, aux),
+        flops=10**8,
+    )
+    red, far, push1, far_push1, xp1, gn1 = call(
         relay_kernel,
-        (struct((8, LANES), F32), struct((len(FAR) * heads, span), F32), full, full, low, low,
-         square, square),
-        (got_one, got_two, xs, gs, aux, b, c, own, tot),
+        (struct((8, LANES), F32), struct((len(FAR) * heads, span), F32), full_part, full_part,
+         low_part, low_part),
+        (more_one, more_two, xs1, gs1, tot, aux, scores, part, weights, own),
         flops=10**8,
     )
     steps = []
@@ -809,23 +930,28 @@
         while bit < lax.axis_size(axis):
             steps.append((axis, bit))
             bit *= 2
-    hop = struct((base // 2 + span + heads, LANES), F32)
-    hop_one, hop_two, sums = call(
-        grads_kernel,
-        (hop, hop, pair),
-        (xp, gn, bp, cn, xs, gs, aux, grads, far, far_push, tot),
+    hop = struct((base // 2 + heads, LANES), F32)
+    hop_one, hop_two = call(
+        hops_kernel,
+        (hop, hop),
+        (xp0, xp1, gn0, gn1, bp, cn, aux, far, far_push0, far_push1, tot),
         flops=10**8,
     )
+    sums = call(
+        grads_kernel, (pair,), (xp0, xp1, gn0, gn1, bp, cn, xs0, xs1, gs0, gs1, grads), flops=10**8
+    )[0]
     relays = range(1, count - 1)
     far_two = exchange(hop_two, 1, relays)
     far_one = exchange(hop_one, 0, relays)
     for axis, bit in steps[:-1]:
         red = red + flip(red, axis, bit)
     last_red = flip(red, *steps[-1])
-    near, weight = call(ready_kernel, (full, full), (g, aux, gain, gb_local, push), flops=10**8)
+    near, weight = call(
+        ready_kernel, (full, full), (g, aux, gain, gb_local, push0, push1), flops=10**8
+    )
     half = call(
-        functools.partial(half_kernel, base // 2), (pair,), (far_one, far_two, sums),
-        flops=10**5,
+        half_kernel, (pair,), (far_one, far_two, xs0, xs1, aux, sums),
+        flops=10**7,
     )[0]
     grad_x, grad_dt = call(
         final_kernel,
@@ -833,15 +959,11 @@
         (far_one, far_two, b, aux, near, weight, small, far),
         flops=10**8,
     )
-    sides = lax.axis_size("head")
-    others = [
-        lax.ppermute(half, "head", [(i, (i + step) % sides) for i in range(sides)])
-        for step in range(1, sides)
-    ]
+    other = flip(half, "head", 1)
     flat = struct((1, heads), F32)
     cube = struct((1, span, state), F32)
     b_total, c_total, alog_total, bias_total, skip_total = call(
-        close_kernel, (cube, cube, flat, flat, flat), (red, last_red, half, *others)
+        close_kernel, (cube, cube, flat, flat, flat), (red, last_red, half, other)
     )
     return (
         grad_x, jnp.swapaxes(grad_dt, 1, 2), b_total, c_total,
@@ -855,6 +977,7 @@
     near = (
         inputs.shape[1] == SPAN
         and shards[1] in (2, 4)
+        and lax.axis_size("head") == 2
         and shards[0] & (shards[0] - 1) == 0
         and b_in.shape[2] == LANES
         and inputs.shape[2] % LANES == 0

time: 54.2 us -> 51.5 us (0.950)
  waiting for transfers between devices: 27.8 us -> 19.6 us
  starting transfers between devices: 15.5 us -> 21.2 us
    ppermute x4 -> x6, waiting for transfers between devices: 21.9 us -> 13.7 us  [exchange(): lax.ppermute(array, 'ctx', [(i, j) for i, j in pairs if 0 <= j < count an...]
    ppermute x4 -> x6, starting transfers between devices: 5.78 us -> 10.9 us  [exchange(): lax.ppermute(array, 'ctx', [(i, j) for i, j in pairs if 0 <= j < count an...]
    ppermute x4 -> x6, starting transfers between devices: 9.65 us -> 10.3 us  [flip(): lax.ppermute(array, axis, [(i, i ^ bit) for i in range(lax.axis_size(axis...]
    pallas_call x8 -> x12, Pallas kernels: 9.92 us -> 9.86 us  [call(): pl.pallas_call(kernel, out_shape=shapes, in_specs=[pl.BlockSpec(memory_sp...]
    ppermute x4 -> x6, waiting for transfers between devices: 5.92 us -> 5.89 us  [flip(): lax.ppermute(array, axis, [(i, i ^ bit) for i in range(lax.axis_size(axis...]
  transfers between devices with their start and end apart: 9 -> 12, of which waited for: 6 -> 7; matrix products, arithmetic and copies ran while one was open for 0% -> 0% of each run, Pallas kernels for 8% -> 12%
where the time goes in v5:
time: 51.5 us; the launch traced here: 51.3 us
  starting transfers between devices  21.2 us (41%)
  waiting for transfers between devices  19.6 us (38%)
  Pallas kernels  9.86 us (19%)
  between operations  0.74 us (1%)
    ppermute x6, waiting for transfers between devices, exchange(): lax.ppermute(array, 'ctx', [(i, j) for i, j in pairs if 0 <= j < count an...  13.7 us
    ppermute x6, starting transfers between devices, exchange(): lax.ppermute(array, 'ctx', [(i, j) for i, j in pairs if 0 <= j < count an...  10.9 us
    ppermute x6, starting transfers between devices, flip(): lax.ppermute(array, axis, [(i, i ^ bit) for i in range(lax.axis_size(axis...  10.3 us
    pallas_call x12, Pallas kernels, call(): pl.pallas_call(kernel, out_shape=shapes, in_specs=[pl.BlockSpec(memory_sp...  9.86 us
    ppermute x6, waiting for transfers between devices, flip(): lax.ppermute(array, axis, [(i, i ^ bit) for i in range(lax.axis_size(axis...  5.89 us
  transfers between devices with their start and end apart: 12, of which 7 were waited for; matrix products, arithmetic and copies ran while one was open for 0% of the time, Pallas kernels for 12%

profile of v5, /device:TPU:0, one launch (start us, length us, event | category | flops | bytes accessed | tf_op | source)
XLA Modules:
  0.0 51.3 jit_solution(3542054098467552265)
XLA Ops:
  0.6 1.5 %shard_map.144 = (f32[608,128]{1,0:T(8,128)S(1)}, f32[608,128]{1,0:T(8,128)S(1)}, f32[240,128]{1,0:T(8,128)S(1)}, bf16[128,512]{1,0:T(8,128)(2,1)S(1)}, bf16[128...) custom-call(s32[1,4]{1,0:T(1,128)} %lens_hbm.1, ...), custom_call_target="tpu_custom_call" | custom-call | flops 100000000 | bytes 2195664 | tf_op jit(solution)/shard_map/pallas_call | solution.py:837
  2.2 3.1 %collective-permute-start = (f32[608,128]{1,0:T(8,128)S(1)}, f32[608,128]{1,0:T(8,128)S(1)}, u32[]{:S(2)}, u32[]{:S(2)}) collective-permute-start(f32[608,128]{1,0:T(8,128)S(1)} %get-tuple-element.52), channel_id=1, source_target_pairs={{0,2},{2,0},{4,6},{6,4},{1,3},{3,1},{5,7},{7,5},{8,10},{10,8},{12,... | collective-permute-start | bytes 933896 | tf_op jit(solution)/shard_map/ppermute | solution.py:856
  5.3 0.7 %collective-permute-start.1 = (f32[608,128]{1,0:T(8,128)S(1)}, f32[608,128]{1,0:T(8,128)S(1)}, u32[]{:S(2)}, u32[]{:S(2)}) collective-permute-start(f32[608,128]{1,0:T(8,128)S(1)} %get-tuple-element.53), channel_id=1, source_target_pairs={{2,4},{4,2},{3,5},{5,3},{10,12},{12,10},{11,13},{13,11},{18,20},{2... | collective-permute-start | bytes 933896 | tf_op jit(solution)/shard_map/ppermute | solution.py:856
  6.0 0.4 shard_map.146
  6.3 4.4 %collective-permute-start.3 = (f32[512,128]{1,0:T(8,128)S(1)}, f32[512,128]{1,0:T(8,128)S(1)}, u32[]{:S(2)}, u32[]{:S(2)}) collective-permute-start(f32[512,128]{1,0:T(8,128)S(1)} %get-tuple-element.63), channel_id=1, source_target_pairs={{0,2},{2,0},{4,6},{6,4},{1,3},{3,1},{5,7},{7,5},{8,10},{10,8},{12,... | collective-permute-start | bytes 786440 | tf_op jit(solution)/shard_map/ppermute | solution.py:856
  10.8 0.7 %collective-permute-start.4 = (f32[512,128]{1,0:T(8,128)S(1)}, f32[512,128]{1,0:T(8,128)S(1)}, u32[]{:S(2)}, u32[]{:S(2)}) collective-permute-start(f32[512,128]{1,0:T(8,128)S(1)} %get-tuple-element.64), channel_id=1, source_target_pairs={{2,4},{4,2},{3,5},{5,3},{10,12},{12,10},{11,13},{13,11},{18,20},{2... | collective-permute-start | bytes 786440 | tf_op jit(solution)/shard_map/ppermute | solution.py:856
  11.4 2.1 %collective-permute-done.got_one_ref = f32[608,128]{1,0:T(8,128)S(1)} collective-permute-done((f32[608,128]{1,0:T(8,128)S(1)}, f32[608,128]{1,0:T(8,128)S(1)}, u32[]{:S(2)}, u32[]{:S(2)}) %collective-permute-start) | collective-permute-done | bytes 311328 | tf_op jit(solution)/shard_map/ppermute | solution.py:856
  13.5 0.0 collective-permute-done.1.got_two_ref
  13.5 0.1 collective-permute-start.2
  13.6 2.9 %shard_map.148 = (f32[128,1024]{1,0:T(8,128)S(1)}, f32[48,128]{1,0:T(8,128)S(1)}, f32[256,128]{1,0:T(8,128)S(1)}, f32[48,128]{1,0:T(8,128)S(1)}) custom-call(bf16[128,1024]{1,0:T(8,128)(2,1)S(1)} %get-tuple-element.58.x_ref, bf16[128,1024]{1,0:T(8,128)(2,1)S(1)} %get-tuple-element.59.g_ref, f32[240,128]{1,0:T(8,128)S(1)} %get-tuple-element.60.aux_ref, ...), custom_call_target="tpu_custom_call" | custom-call | flops 100000000 | bytes 1417216 | tf_op jit(solution)/shard_map/pallas_call | solution.py:837
  16.5 0.0 collective-permute-done.2.other_ref
  16.5 0.6 %shard_map.147 = (f32[128,512]{1,0:T(8,128)S(1)}, f32[128,512]{1,0:T(8,128)S(1)}, bf16[128,512]{1,0:T(8,128)(2,1)S(1)}, bf16[128,512]{1,0:T(8,128)(2,1)S(1)}, bf...) custom-call(f32[608,128]{1,0:T(8,128)S(1)} %collective-permute-done., ...), custom_call_target="tpu_custom_call" | custom-call | flops 100000000 | bytes 2285568 | tf_op jit(solution)/shard_map/pallas_call | solution.py:837
  17.1 1.2 %collective-permute-done.3.got_one_ref = f32[512,128]{1,0:T(8,128)S(1)} collective-permute-done((f32[512,128]{1,0:T(8,128)S(1)}, f32[512,128]{1,0:T(8,128)S(1)}, u32[]{:S(2)}, u32[]{:S(2)}) %collective-permute-start.3) | collective-permute-done | bytes 262176 | tf_op jit(solution)/shard_map/ppermute | solution.py:856
  18.3 0.0 collective-permute-done.4.got_two_ref
  18.3 0.7 %shard_map.149 = (f32[8,128]{1,0:T(8,128)S(1)}, f32[80,128]{1,0:T(8,128)S(1)}, f32[128,512]{1,0:T(8,128)S(1)}, f32[128,512]{1,0:T(8,128)S(1)}, bf16[128,512]{1,0...) custom-call(f32[512,128]{1,0:T(8,128)S(1)} %collective-permute-done.3.got_one_ref, ...), custom_call_target="tpu_custom_call" | custom-call | flops 100000000 | bytes 1994752 | tf_op jit(solution)/shard_map/pallas_call | solution.py:837
  18.9 0.7 %shard_map.150 = (f32[592,128]{1,0:T(8,128)S(1)}, f32[592,128]{1,0:T(8,128)S(1)}) custom-call(bf16[128,512]{1,0:T(8,128)(2,1)S(1)} %get-tuple-element.62.xp0_ref, bf16[128,512]{1,0:T(8,128)(2,1)S(1)} %get-tuple-element.71.xp1_ref, bf16[128,512]{1,0:T(8,128)(2,1)S(1)} %get-tuple-element.72.gn0_ref, bf16[128,512]{1,0:T(8,128)(2,1)S(1)} %get-tuple-element.73.gn1_ref, ...), custom_call_target="tpu_custom_call" | custom-call | flops 100000000 | bytes 1916928 | tf_op jit(solution)/shard_map/pallas_call | solution.py:837
  19.6 1.3 %collective-permute-start.5 = (f32[592,128]{1,0:T(8,128)S(1)}, f32[592,128]{1,0:T(8,128)S(1)}, u32[]{:S(2)}, u32[]{:S(2)}) collective-permute-start(f32[592,128]{1,0:T(8,128)S(1)} %get-tuple-element.79), channel_id=1, source_target_pairs={{2,0},{4,6},{3,1},{5,7},{10,8},{12,14},{11,9},{13,15},{18,16},{20,... | collective-permute-start | bytes 909320 | tf_op jit(solution)/shard_map/ppermute | solution.py:856
  20.9 0.7 %collective-permute-start.6 = (f32[592,128]{1,0:T(8,128)S(1)}, f32[592,128]{1,0:T(8,128)S(1)}, u32[]{:S(2)}, u32[]{:S(2)}) collective-permute-start(f32[592,128]{1,0:T(8,128)S(1)} %get-tuple-element.80), channel_id=1, source_target_pairs={{2,4},{4,2},{3,5},{5,3},{10,12},{12,10},{11,13},{13,11},{18,20},{2... | collective-permute-start | bytes 909320 | tf_op jit(solution)/shard_map/ppermute | solution.py:856
  21.6 0.7 %shard_map.153.sums_ref = f32[256,128]{1,0:T(8,128)S(1)} custom-call(bf16[128,512]{1,0:T(8,128)(2,1)S(1)} %get-tuple-element.62.xp0_ref, bf16[128,512]{1,0:T(8,128)(2,1)S(1)} %get-tuple-element.71.xp1_ref, bf16[128,512]{1,0:T(8,128)(2,1)S(1)} %get-tuple-element.72.gn0_ref, bf16[128,512]{1,0:T(8,128)(2,1)S(1)} %get-tuple-element.73.gn1_ref, ...), custom_call_target="tpu_custom_call" | custom-call | flops 100000000 | bytes 1376256 | tf_op jit(solution)/shard_map/pallas_call | solution.py:837
  22.3 10.4 %collective-permute-done.5.far_one_ref = f32[592,128]{1,0:T(8,128)S(1)} collective-permute-done((f32[592,128]{1,0:T(8,128)S(1)}, f32[592,128]{1,0:T(8,128)S(1)}, u32[]{:S(2)}, u32[]{:S(2)}) %collective-permute-start.5) | collective-permute-done | bytes 303136 | tf_op jit(solution)/shard_map/ppermute | solution.py:856
  32.7 0.0 collective-permute-done.6.far_two_ref
  32.7 0.4 shard_map.154.half_ref
  33.0 0.1 collective-permute-start.11
  33.1 4.0 %collective-permute-start.7 = (f32[8,128]{1,0:T(8,128)S(1)}, f32[8,128]{1,0:T(8,128)S(1)}, u32[]{:S(2)}, u32[]{:S(2)}) collective-permute-start(f32[8,128]{1,0:T(8,128)S(1)} %get-tuple-element.90), channel_id=1, source_target_pairs={{0,2},{2,0},{4,6},{6,4},{1,3},{3,1},{5,7},{7,5},{8,10},{10,8},{12,... | collective-permute-start | bytes 12296 | tf_op jit(solution)/shard_map/ppermute | solution.py:862
  37.1 1.6 %collective-permute-done.7 = f32[8,128]{1,0:T(8,128)S(1)} collective-permute-done((f32[8,128]{1,0:T(8,128)S(1)}, f32[8,128]{1,0:T(8,128)S(1)}, u32[]{:S(2)}, u32[]{:S(2)}) %collective-permute-start.7) | collective-permute-done | bytes 4128 | tf_op jit(solution)/shard_map/ppermute | solution.py:862
  38.7 3.2 %collective-permute-start.8 = (f32[8,128]{1,0:T(8,128)S(1)}, f32[8,128]{1,0:T(8,128)S(1)}, u32[]{:S(2)}, u32[]{:S(2)}) collective-permute-start(f32[8,128]{1,0:T(8,128)S(1)} %add.9), channel_id=1, source_target_pairs={{0,4},{2,6},{4,0},{6,2},{1,5},{3,7},{5,1},{7,3},{8,12},{10,14},{12... | collective-permute-start | bytes 12296 | tf_op jit(solution)/shard_map/ppermute | solution.py:862
  41.9 1.6 %collective-permute-done.8 = f32[8,128]{1,0:T(8,128)S(1)} collective-permute-done((f32[8,128]{1,0:T(8,128)S(1)}, f32[8,128]{1,0:T(8,128)S(1)}, u32[]{:S(2)}, u32[]{:S(2)}) %collective-permute-start.8) | collective-permute-done | bytes 4128 | tf_op jit(solution)/shard_map/ppermute | solution.py:862
  43.4 1.5 %collective-permute-start.9 = (f32[8,128]{1,0:T(8,128)S(1)}, f32[8,128]{1,0:T(8,128)S(1)}, u32[]{:S(2)}, u32[]{:S(2)}) collective-permute-start(f32[8,128]{1,0:T(8,128)S(1)} %add.10), channel_id=1, source_target_pairs={{0,8},{8,0},{16,24},{24,16},{1,9},{9,1},{17,25},{25,17},{2,10},{10... | collective-permute-start | bytes 12296 | tf_op jit(solution)/shard_map/ppermute | solution.py:862
  45.0 0.4 shard_map.151
  45.3 1.7 %collective-permute-done.9 = f32[8,128]{1,0:T(8,128)S(1)} collective-permute-done((f32[8,128]{1,0:T(8,128)S(1)}, f32[8,128]{1,0:T(8,128)S(1)}, u32[]{:S(2)}, u32[]{:S(2)}) %collective-permute-start.9) | collective-permute-done | bytes 4128 | tf_op jit(solution)/shard_map/ppermute | solution.py:862
  47.1 1.5 %collective-permute-start.10 = (f32[8,128]{1,0:T(8,128)S(1)}, f32[8,128]{1,0:T(8,128)S(1)}, u32[]{:S(2)}, u32[]{:S(2)}) collective-permute-start(f32[8,128]{1,0:T(8,128)S(1)} %add.11.red_ref), channel_id=1, source_target_pairs={{0,16},{8,24},{16,0},{24,8},{1,17},{9,25},{17,1},{25,9},{2,18},{10... | collective-permute-start | bytes 12296 | tf_op jit(solution)/shard_map/ppermute | solution.py:862
  48.6 1.1 %shard_map.152 = (bf16[1,128,1024]{2,1,0:T(8,128)(2,1)}, f32[1,16,128]{2,1,0:T(8,128)}) custom-call(f32[592,128]{1,0:T(8,128)S(1)} %collective-permute-done.5.far_one_ref, f32[592,128]{1,0:T(8,128)S(1)} %collective-permute-done.6.far_two_ref, bf16[128,128]{1,0:T(8,128)(2,1)S(1)} %get-tuple-element.56.b_ref, f32[240,128]{1,0:T(8,128)S(1)} %get-tuple-element.60.aux_ref, ...), custom_call_target="tpu_custom_call" | custom-call | flops 100000000 | bytes 2146304 | tf_op jit(solution)/shard_map/pallas_call | solution.py:837
  49.7 1.0 %collective-permute-done.10.last_ref = f32[8,128]{1,0:T(8,128)S(1)} collective-permute-done((f32[8,128]{1,0:T(8,128)S(1)}, f32[8,128]{1,0:T(8,128)S(1)}, u32[]{:S(2)}, u32[]{:S(2)}) %collective-permute-start.10) | collective-permute-done | bytes 4128 | tf_op jit(solution)/shard_map/ppermute | solution.py:862
  50.7 0.0 collective-permute-done.11.other_ref
  50.7 0.7 %shard_map.155 = (f32[1,128,128]{2,1,0:T(8,128)}, f32[1,128,128]{2,1,0:T(8,128)}, f32[1,16]{1,0:T(1,128)}, f32[1,16]{1,0:T(1,128)}, f32[1,16]{1,0:T(1,128)}) custom-call(f32[8,128]{1,0:T(8,128)S(1)} %add.11.red_ref, f32[8,128]{1,0:T(8,128)S(1)} %collective-permute-done.10.last_ref, f32[256,128]{1,0:T(8,128)S(1)} %shard_map.154.half_ref, ...), custom_call_target="tpu_custom_call" | custom-call | bytes 401600 | tf_op jit(solution)/shard_map/pallas_call | solution.py:837
  (4 shorter events, 0.0 us)
Async XLA Ops:
  2.2 11.3 %collective-permute-start = (f32[608,128]{1,0:T(8,128)S(1)}, f32[608,128]{1,0:T(8,128)S(1)}, u32[]{:S(2)}, u32[]{:S(2)}) collective-permute-start(f32[608,128]{1,0:T(8,128)S(1)} %get-tuple-element.52), channel_id=1, source_target_pairs={{0,2},{2,0},{4,6},{6,4},{1,3},{3,1},{5,7},{7,5},{8,10},{10,8},{12,... | collective-permute-start | bytes 933896 | tf_op jit(solution)/shard_map/ppermute | solution.py:856
  5.3 8.2 %collective-permute-start.1 = (f32[608,128]{1,0:T(8,128)S(1)}, f32[608,128]{1,0:T(8,128)S(1)}, u32[]{:S(2)}, u32[]{:S(2)}) collective-permute-start(f32[608,128]{1,0:T(8,128)S(1)} %get-tuple-element.53), channel_id=1, source_target_pairs={{2,4},{4,2},{3,5},{5,3},{10,12},{12,10},{11,13},{13,11},{18,20},{2... | collective-permute-start | bytes 933896 | tf_op jit(solution)/shard_map/ppermute | solution.py:856
  6.3 11.9 %collective-permute-start.3 = (f32[512,128]{1,0:T(8,128)S(1)}, f32[512,128]{1,0:T(8,128)S(1)}, u32[]{:S(2)}, u32[]{:S(2)}) collective-permute-start(f32[512,128]{1,0:T(8,128)S(1)} %get-tuple-element.63), channel_id=1, source_target_pairs={{0,2},{2,0},{4,6},{6,4},{1,3},{3,1},{5,7},{7,5},{8,10},{10,8},{12,... | collective-permute-start | bytes 786440 | tf_op jit(solution)/shard_map/ppermute | solution.py:856
  10.8 7.5 %collective-permute-start.4 = (f32[512,128]{1,0:T(8,128)S(1)}, f32[512,128]{1,0:T(8,128)S(1)}, u32[]{:S(2)}, u32[]{:S(2)}) collective-permute-start(f32[512,128]{1,0:T(8,128)S(1)} %get-tuple-element.64), channel_id=1, source_target_pairs={{2,4},{4,2},{3,5},{5,3},{10,12},{12,10},{11,13},{13,11},{18,20},{2... | collective-permute-start | bytes 786440 | tf_op jit(solution)/shard_map/ppermute | solution.py:856
  13.5 3.0 %collective-permute-start.2 = (f32[128,128]{1,0:T(8,128)S(1)}, f32[128,128]{1,0:T(8,128)S(1)}, u32[]{:S(2)}, u32[]{:S(2)}) collective-permute-start(f32[128,128]{1,0:T(8,128)S(1)} %shard_map.145.maps_ref), channel_id=1, source_target_pairs={{0,1},{1,0},{2,3},{3,2},{4,5},{5,4},{6,7},{7,6},{8,9},{9,8},{10,11... | collective-permute-start | bytes 196616 | tf_op jit(solution)/shard_map/ppermute | solution.py:862
  19.6 13.0 %collective-permute-start.5 = (f32[592,128]{1,0:T(8,128)S(1)}, f32[592,128]{1,0:T(8,128)S(1)}, u32[]{:S(2)}, u32[]{:S(2)}) collective-permute-start(f32[592,128]{1,0:T(8,128)S(1)} %get-tuple-element.79), channel_id=1, source_target_pairs={{2,0},{4,6},{3,1},{5,7},{10,8},{12,14},{11,9},{13,15},{18,16},{20,... | collective-permute-start | bytes 909320 | tf_op jit(solution)/shard_map/ppermute | solution.py:856
  20.9 11.7 %collective-permute-start.6 = (f32[592,128]{1,0:T(8,128)S(1)}, f32[592,128]{1,0:T(8,128)S(1)}, u32[]{:S(2)}, u32[]{:S(2)}) collective-permute-start(f32[592,128]{1,0:T(8,128)S(1)} %get-tuple-element.80), channel_id=1, source_target_pairs={{2,4},{4,2},{3,5},{5,3},{10,12},{12,10},{11,13},{13,11},{18,20},{2... | collective-permute-start | bytes 909320 | tf_op jit(solution)/shard_map/ppermute | solution.py:856
  33.0 17.6 %collective-permute-start.11 = (f32[256,128]{1,0:T(8,128)S(1)}, f32[256,128]{1,0:T(8,128)S(1)}, u32[]{:S(2)}, u32[]{:S(2)}) collective-permute-start(f32[256,128]{1,0:T(8,128)S(1)} %shard_map.154.half_ref), channel_id=1, source_target_pairs={{0,1},{1,0},{2,3},{3,2},{4,5},{5,4},{6,7},{7,6},{8,9},{9,8},{10,11... | collective-permute-start | bytes 393224 | tf_op jit(solution)/shard_map/ppermute | solution.py:862
  33.1 5.5 %collective-permute-start.7 = (f32[8,128]{1,0:T(8,128)S(1)}, f32[8,128]{1,0:T(8,128)S(1)}, u32[]{:S(2)}, u32[]{:S(2)}) collective-permute-start(f32[8,128]{1,0:T(8,128)S(1)} %get-tuple-element.90), channel_id=1, source_target_pairs={{0,2},{2,0},{4,6},{6,4},{1,3},{3,1},{5,7},{7,5},{8,10},{10,8},{12,... | collective-permute-start | bytes 12296 | tf_op jit(solution)/shard_map/ppermute | solution.py:862
  38.7 4.8 %collective-permute-start.8 = (f32[8,128]{1,0:T(8,128)S(1)}, f32[8,128]{1,0:T(8,128)S(1)}, u32[]{:S(2)}, u32[]{:S(2)}) collective-permute-start(f32[8,128]{1,0:T(8,128)S(1)} %add.9), channel_id=1, source_target_pairs={{0,4},{2,6},{4,0},{6,2},{1,5},{3,7},{5,1},{7,3},{8,12},{10,14},{12... | collective-permute-start | bytes 12296 | tf_op jit(solution)/shard_map/ppermute | solution.py:862
  43.4 3.6 %collective-permute-start.9 = (f32[8,128]{1,0:T(8,128)S(1)}, f32[8,128]{1,0:T(8,128)S(1)}, u32[]{:S(2)}, u32[]{:S(2)}) collective-permute-start(f32[8,128]{1,0:T(8,128)S(1)} %add.10), channel_id=1, source_target_pairs={{0,8},{8,0},{16,24},{24,16},{1,9},{9,1},{17,25},{25,17},{2,10},{10... | collective-permute-start | bytes 12296 | tf_op jit(solution)/shard_map/ppermute | solution.py:862
  47.1 3.6 %collective-permute-start.10 = (f32[8,128]{1,0:T(8,128)S(1)}, f32[8,128]{1,0:T(8,128)S(1)}, u32[]{:S(2)}, u32[]{:S(2)}) collective-permute-start(f32[8,128]{1,0:T(8,128)S(1)} %add.11.red_ref), channel_id=1, source_target_pairs={{0,16},{8,24},{16,0},{24,8},{1,17},{9,25},{17,1},{25,9},{2,18},{10... | collective-permute-start | bytes 12296 | tf_op jit(solution)/shard_map/ppermute | solution.py:862

commit v6 on v5

--- a/solution.py
+++ b/solution.py
@@ -340,23 +340,22 @@
     return lax.rem(lax.axis_index("ctx"), 2) == 0
 
 
-AUX = (
-    "dt", "gate", "cum", "din", "dout", "tot", "alpha_s", "beta_s", "alpha_u", "beta_u", "rate", "doc", "masks",
-    "short", "gain",
-)
-LOCAL = ("first", "x_gb", "skip")
-FAR = ("z_own", "w_own", "z_far", "w_far", "carried")
-
-
-def take(ref, names, name, heads):
-    slot = names.index(name) * heads
-    return ref[slot : slot + heads, :]
-
-
-def put(ref, names, heads, values):
-    for name, value in values.items():
-        slot = names.index(name) * heads
-        ref[slot : slot + heads, :] = value
+(
+    DT, GATE, CUM, DIN, DOUT, TOT, ALPHA_S, BETA_S, ALPHA_U, BETA_U, RATE, DOC, MASKS, SHORT, GAIN
+) = range(15)
+AUX = 15
+FIRST, X_GB = range(2)
+Z_OWN, W_OWN, Z_FAR, W_FAR, CARRIED = range(5)
+FAR = 5
+
+
+def take(ref, slot, heads):
+    return ref[slot * heads : (slot + 1) * heads, :]
+
+
+def put(ref, heads, values):
+    for slot, value in values.items():
+        ref[slot * heads : (slot + 1) * heads, :] = value
 
 
 def halves(upper, lower, rows):
@@ -428,15 +427,15 @@
     beta_s = rate * left[heads:] + gate / dt
     alpha_u = rate * seen[:heads]
     beta_u = rate * seen[heads:]
-    put(aux_ref, AUX, heads, dict(
-        dt=dt, gate=gate, cum=cum, din=din, dout=dout,
-        tot=jnp.broadcast_to(whole * jnp.exp(cum_last), dt.shape),
-        gain=jnp.broadcast_to(as_column(skip_ref[...]), dt.shape),
-        alpha_s=alpha_s, beta_s=beta_s, alpha_u=alpha_u, beta_u=beta_u,
-        rate=jnp.broadcast_to(rate, dt.shape), doc=jnp.broadcast_to(doc.astype(F32), dt.shape),
-        masks=halves(inward, outward, heads),
-        short=halves(jnp.full((1, span), short_before), jnp.full((1, span), short_last), heads),
-    ))
+    put(aux_ref, heads, {
+        DT: dt, GATE: gate, CUM: cum, DIN: din, DOUT: dout,
+        TOT: jnp.broadcast_to(whole * jnp.exp(cum_last), dt.shape),
+        GAIN: jnp.broadcast_to(as_column(skip_ref[...]), dt.shape),
+        ALPHA_S: alpha_s, BETA_S: beta_s, ALPHA_U: alpha_u, BETA_U: beta_u,
+        RATE: jnp.broadcast_to(rate, dt.shape), DOC: jnp.broadcast_to(doc.astype(F32), dt.shape),
+        MASKS: halves(inward, outward, heads),
+        SHORT: halves(jnp.full((1, span), short_before), jnp.full((1, span), short_last), heads),
+    })
     x_factor, g_factor = spread(dout * dt, rows), spread(din, rows)
     for copy in large:
         copy.wait()
@@ -464,16 +463,16 @@
 
 def rest_kernel(x_ref, g_ref, aux_ref, pay_one_ref, pay_two_ref, xs_ref, gs_ref, tot_ref, gain_ref):
     features = x_ref.shape[1]
-    heads = aux_ref.shape[0] // len(AUX)
+    heads = aux_ref.shape[0] // AUX
     part = slice(features // 2, features)
     rows = head_rows(heads, features // heads, part)
-    dout, dt = take(aux_ref, AUX, "dout", heads), take(aux_ref, AUX, "dt", heads)
+    dout, dt = take(aux_ref, DOUT, heads), take(aux_ref, DT, heads)
     xs = (x_ref[:, part].astype(F32) * spread(dout * dt, rows)).astype(BF16)
-    gs = (g_ref[:, part].astype(F32) * spread(take(aux_ref, AUX, "din", heads), rows)).astype(BF16)
+    gs = (g_ref[:, part].astype(F32) * spread(take(aux_ref, DIN, heads), rows)).astype(BF16)
     xs_ref[...] = xs
     gs_ref[...] = gs
-    for name, ref in (("tot", tot_ref), ("gain", gain_ref)):
-        row = as_row(take(aux_ref, AUX, name, heads)[:, :1])
+    for slot, ref in ((TOT, tot_ref), (GAIN, gain_ref)):
+        row = as_row(take(aux_ref, slot, heads)[:, :1])
         ref[...] = jnp.broadcast_to(spread_row(row, features), ref.shape)
     first = leads()
 
@@ -492,14 +491,14 @@
     x_ref, g_ref, aux_ref, b_ref, c_ref, gb_ref, small_ref, grads_ref, own_ref
 ):
     span, features = x_ref.shape
-    heads = aux_ref.shape[0] // len(AUX)
+    heads = aux_ref.shape[0] // AUX
     width = features // heads
     row, column = iota((span, span), 0), iota((span, span), 1)
-    dt = take(aux_ref, AUX, "dt", heads)
-    gate = take(aux_ref, AUX, "gate", heads)
-    cum = take(aux_ref, AUX, "cum", heads)
-    rate = take(aux_ref, AUX, "rate", heads)
-    doc = take(aux_ref, AUX, "doc", heads)
+    dt = take(aux_ref, DT, heads)
+    gate = take(aux_ref, GATE, heads)
+    cum = take(aux_ref, CUM, heads)
+    rate = take(aux_ref, RATE, heads)
+    doc = take(aux_ref, DOC, heads)
     upright = nt(eye(span), jnp.concatenate([dt, cum, doc], axis=0), EXACT)
     doc_s = upright[:, 2 * heads : 2 * heads + 1]
     closed = jnp.where((column >= row) & (jnp.abs(doc_s - doc[:1, :]) < 0.5), 0.0, -1e30)
@@ -536,7 +535,7 @@
     )
     sums = nt(eye(2 * heads), sums, EXACT)
     x_gb, skip = sums[:heads], sums[heads:]
-    put(small_ref, LOCAL, heads, dict(first=first, x_gb=x_gb, skip=skip))
+    put(small_ref, heads, {FIRST: first, X_GB: x_gb})
     own_ref[:heads, :] = rate * dt * first
     own_ref[heads : 2 * heads, :] = gate * (x_gb + rate * first)
     own_ref[2 * heads :, :] = skip
@@ -589,7 +588,7 @@
     push_ref, far_push_ref, xp_ref, gn_ref, bp_ref, cn_ref, scores_ref, part_ref, weights_ref,
 ):
     span, features = xs_ref.shape
-    heads = aux_ref.shape[0] // len(AUX)
+    heads = aux_ref.shape[0] // AUX
     width = tot_ref.shape[1] // heads
     blocks = features // LANES
     behind, ahead = neighbours(got_one_ref, got_two_ref)
@@ -628,7 +627,7 @@
     own_ref, red_ref, far_ref, push_ref, far_push_ref, xp_ref, gn_ref,
 ):
     span, features = xs_ref.shape
-    heads = aux_ref.shape[0] // len(AUX)
+    heads = aux_ref.shape[0] // AUX
     total = tot_ref.shape[1]
     blocks = features // LANES
     behind, ahead = neighbours(got_one_ref, got_two_ref)
@@ -646,30 +645,30 @@
         weights_ref[index * heads : (index + 1) * heads, :] for index in range(4)
     )
     carried = jnp.sum(z_far, axis=1, keepdims=True)
-    rate = take(aux_ref, AUX, "rate", heads)
+    rate = take(aux_ref, RATE, heads)
     alog = (
         own_ref[:heads, :]
-        + z_own * take(aux_ref, AUX, "alpha_u", heads)
-        + w_own * take(aux_ref, AUX, "alpha_s", heads)
-        + carried * rate * take(aux_ref, AUX, "dt", heads)
+        + z_own * take(aux_ref, ALPHA_U, heads)
+        + w_own * take(aux_ref, ALPHA_S, heads)
+        + carried * rate * take(aux_ref, DT, heads)
         + z_far * alpha_n
         + w_far * alpha_p
     )
     bias = (
         own_ref[heads : 2 * heads, :]
-        + z_own * take(aux_ref, AUX, "beta_u", heads)
-        + w_own * take(aux_ref, AUX, "beta_s", heads)
-        + carried * rate * take(aux_ref, AUX, "gate", heads)
+        + z_own * take(aux_ref, BETA_U, heads)
+        + w_own * take(aux_ref, BETA_S, heads)
+        + carried * rate * take(aux_ref, GATE, heads)
         + z_far * beta_n
         + w_far * beta_p
     )
     stack = jnp.concatenate([alog, bias, own_ref[2 * heads :, :]], axis=0)
     red_ref[:, : 3 * heads] = nt(jnp.ones((8, span), F32), stack, EXACT)
     red_ref[:, 3 * heads :] = jnp.zeros((8, red_ref.shape[1] - 3 * heads), F32)
-    put(far_ref, FAR, heads, dict(
-        z_own=z_own, w_own=w_own, z_far=z_far, w_far=w_far,
-        carried=jnp.broadcast_to(carried, z_own.shape),
-    ))
+    put(far_ref, heads, {
+        Z_OWN: z_own, W_OWN: w_own, Z_FAR: z_far, W_FAR: w_far,
+        CARRIED: jnp.broadcast_to(carried, z_own.shape),
+    })
     xp_ref[...] = xp
     gn_ref[...] = gn
 
@@ -682,45 +681,49 @@
     xp0_ref, xp1_ref, gn0_ref, gn1_ref, bp_ref, cn_ref, aux_ref, far_ref, push0_ref, push1_ref,
     tot_ref, hop_one_ref, hop_two_ref,
 ):
-    xp, gn, bp, cn = both(xp0_ref, xp1_ref), both(gn0_ref, gn1_ref), bp_ref[...], cn_ref[...]
-    span, features = xp.shape
-    blocks = features // LANES
-    heads = far_ref.shape[0] // len(FAR)
-    gn_tot = (gn.astype(F32) * tot_ref[:1, :]).astype(BF16)
-    grad_b_far = nn(nt(xp, gn_tot).astype(BF16), cn)
-    grad_c_far = nn(nt(gn_tot, xp).astype(BF16), bp)
-    half = span // 2
-    base = blocks * half
-    short = take(aux_ref, AUX, "short", heads)[:1, :] > 0.5
-
-    def load(ref, grad, name, heavy):
-        if heavy:
-            for block in range(blocks):
-                push_ref = (push0_ref, push1_ref)[block * 2 // blocks]
-                inner = (block % (blocks // 2)) * LANES
-                ref[block * half : (block + 1) * half, :] = jnp.where(
-                    short,
-                    push_ref[half:, inner : inner + LANES],
-                    gn_tot[:half, block * LANES : (block + 1) * LANES].astype(F32),
-                )
-            ref[base : base + half, :] = jnp.where(short, grad[half:], cn[:half].astype(F32))
-        else:
-            ref[:span, :] = grad
-            ref[span : base + half, :] = jnp.zeros((base + half - span, LANES), F32)
-        rest = base + half
-        ref[rest : rest + heads, :] = take(far_ref, FAR, name, heads)
-
-    first = leads()
-
-    @pl.when(first)
+    ctx = lax.axis_index("ctx")
+
+    @pl.when((ctx > 0) & (ctx < lax.axis_size("ctx") - 1))
     def _():
-        load(hop_one_ref, grad_c_far, "z_far", False)
-        load(hop_two_ref, grad_b_far, "w_far", True)
-
-    @pl.when(jnp.logical_not(first))
-    def _():
-        load(hop_one_ref, grad_b_far, "w_far", True)
-        load(hop_two_ref, grad_c_far, "z_far", False)
+        xp, gn, bp, cn = both(xp0_ref, xp1_ref), both(gn0_ref, gn1_ref), bp_ref[...], cn_ref[...]
+        span, features = xp.shape
+        blocks = features // LANES
+        heads = far_ref.shape[0] // FAR
+        gn_tot = (gn.astype(F32) * tot_ref[:1, :]).astype(BF16)
+        grad_b_far = nn(nt(xp, gn_tot).astype(BF16), cn)
+        grad_c_far = nn(nt(gn_tot, xp).astype(BF16), bp)
+        half = span // 2
+        base = blocks * half
+        short = take(aux_ref, SHORT, heads)[:1, :] > 0.5
+
+        def load(ref, grad, slot, heavy):
+            if heavy:
+                for block in range(blocks):
+                    push_ref = (push0_ref, push1_ref)[block * 2 // blocks]
+                    inner = (block % (blocks // 2)) * LANES
+                    ref[block * half : (block + 1) * half, :] = jnp.where(
+                        short,
+                        push_ref[half:, inner : inner + LANES],
+                        gn_tot[:half, block * LANES : (block + 1) * LANES].astype(F32),
+                    )
+                ref[base : base + half, :] = jnp.where(short, grad[half:], cn[:half].astype(F32))
+            else:
+                ref[:span, :] = grad
+                ref[span : base + half, :] = jnp.zeros((base + half - span, LANES), F32)
+            rest = base + half
+            ref[rest : rest + heads, :] = take(far_ref, slot, heads)
+
+        first = leads()
+
+        @pl.when(first)
+        def _():
+            load(hop_one_ref, grad_c_far, Z_FAR, False)
+            load(hop_two_ref, grad_b_far, W_FAR, True)
+
+        @pl.when(jnp.logical_not(first))
+        def _():
+            load(hop_one_ref, grad_b_far, W_FAR, True)
+            load(hop_two_ref, grad_c_far, Z_FAR, False)
 
 
 def grads_kernel(
@@ -738,10 +741,10 @@
     g_ref, aux_ref, gain_ref, gbl_ref, push0_ref, push1_ref, near_ref, weight_ref
 ):
     features = g_ref.shape[1]
-    heads = aux_ref.shape[0] // len(AUX)
+    heads = aux_ref.shape[0] // AUX
     rows = head_rows(heads, features // heads)
-    dt = take(aux_ref, AUX, "dt", heads)
-    weight = spread(dt * take(aux_ref, AUX, "dout", heads), rows)
+    dt = take(aux_ref, DT, heads)
+    weight = spread(dt * take(aux_ref, DOUT, heads), rows)
     weight_ref[...] = weight
     near_ref[...] = (
         spread(dt, rows) * gbl_ref[...]
@@ -755,12 +758,12 @@
     gx_ref, gdt_ref,
 ):
     span, features = near_ref.shape
-    heads = aux_ref.shape[0] // len(AUX)
+    heads = aux_ref.shape[0] // AUX
     blocks = features // LANES
     half = span // 2
     behind, ahead = neighbours(far_one_ref, far_two_ref)
     base = blocks * half
-    short = take(aux_ref, AUX, "short", heads)[heads // 2 : heads // 2 + 1, :] > 0.5
+    short = take(aux_ref, SHORT, heads)[heads // 2 : heads // 2 + 1, :] > 0.5
     cn = ahead(slice(base, base + half)).astype(BF16)
     scores = nt(b_ref[...], cn).astype(BF16)
     parts = [ahead(slice(k * half, (k + 1) * half)) for k in range(blocks)]
@@ -778,34 +781,34 @@
         axis=1,
     )
     gx_ref[0] = (near_ref[...] + weight_ref[...] * push).astype(BF16)
-    dt = take(aux_ref, AUX, "dt", heads)
-    gate = take(aux_ref, AUX, "gate", heads)
-    rate = take(aux_ref, AUX, "rate", heads)
-    inout = take(aux_ref, AUX, "masks", heads)
+    dt = take(aux_ref, DT, heads)
+    gate = take(aux_ref, GATE, heads)
+    rate = take(aux_ref, RATE, heads)
+    inout = take(aux_ref, MASKS, heads)
     inward, outward = inout[:1, :], inout[heads // 2 : heads // 2 + 1, :]
     rest = base + half
-    z = take(far_ref, FAR, "z_own", heads) + behind(slice(rest, rest + heads))
-    w = take(far_ref, FAR, "w_own", heads) + ahead(slice(rest, rest + heads))
+    z = take(far_ref, Z_OWN, heads) + behind(slice(rest, rest + heads))
+    w = take(far_ref, W_OWN, heads) + ahead(slice(rest, rest + heads))
     row, column = iota((span, span), 0), iota((span, span), 1)
     decay_grad = (
-        take(small_ref, LOCAL, "first", heads)
+        take(small_ref, FIRST, heads)
         + inward * nn(z, (row >= column).astype(F32), EXACT)
         + outward * nn(w, (row < column).astype(F32), EXACT)
-        + take(far_ref, FAR, "carried", heads)
-    )
-    x_gb = take(small_ref, LOCAL, "x_gb", heads) + w / dt
+        + take(far_ref, CARRIED, heads)
+    )
+    x_gb = take(small_ref, X_GB, heads) + w / dt
     gdt_ref[0] = (x_gb + rate * decay_grad) * gate
 
 
 def half_kernel(far_one_ref, far_two_ref, xs0_ref, xs1_ref, aux_ref, sums_ref, half_ref):
     xs = both(xs0_ref, xs1_ref)
     span, features = xs.shape
-    heads = aux_ref.shape[0] // len(AUX)
+    heads = aux_ref.shape[0] // AUX
     half = span // 2
     blocks = features // LANES
     base = blocks * half
     behind, ahead = neighbours(far_one_ref, far_two_ref)
-    short = take(aux_ref, AUX, "short", heads)[heads // 2 : heads // 2 + 1, :] > 0.5
+    short = take(aux_ref, SHORT, heads)[heads // 2 : heads // 2 + 1, :] > 0.5
     last = ahead(slice(base, base + half))
     gn = wide(ahead, half, blocks)
     grad = nn(nt(xs, gn).astype(BF16), last.astype(BF16))
@@ -885,7 +888,7 @@
     one_row = pltpu.VMEM((1, heads), F32)
     pay_one, pay_two, aux, xs0, gs0, x, g, b, c = call(
         prep_kernel,
-        (pay, pay, struct((len(AUX) * heads, span), F32), low_part, low_part, low, low, square,
+        (pay, pay, struct((AUX * heads, span), F32), low_part, low_part, low, low, square,
          square),
         (doc_lengths, raw, bias, alog, skip, inputs, grad_out, b_in, c_in),
         raw=9, flops=10**8,
@@ -901,7 +904,7 @@
     more_one = exchange(pay_one, 0, range(count))
     gb_local, small, grads, own = call(
         local_kernel,
-        (full, struct((len(LOCAL) * heads, span), F32), pair, struct((3 * heads, span), F32)),
+        (full, struct((2 * heads, span), F32), pair, struct((3 * heads, span), F32)),
         (x, g, aux, b, c),
         flops=10**8,
     )
@@ -919,7 +922,7 @@
     )
     red, far, push1, far_push1, xp1, gn1 = call(
         relay_kernel,
-        (struct((8, LANES), F32), struct((len(FAR) * heads, span), F32), full_part, full_part,
+        (struct((8, LANES), F32), struct((FAR * heads, span), F32), full_part, full_part,
          low_part, low_part),
         (more_one, more_two, xs1, gs1, tot, aux, scores, part, weights, own),
         flops=10**8,

time: 51.5 us -> 51.5 us (level)
  Pallas kernels: 9.86 us -> 9.16 us
  waiting for transfers between devices: 19.6 us -> 20.2 us
    pallas_call x12, Pallas kernels: 9.86 us -> 9.16 us  [call(): pl.pallas_call(kernel, out_shape=shapes, in_specs=[pl.BlockSpec(memory_sp...]
    ppermute x6, waiting for transfers between devices: 13.7 us -> 14.3 us  [exchange(): lax.ppermute(array, 'ctx', [(i, j) for i, j in pairs if 0 <= j < count an...]
where the time goes in v6:
time: 51.5 us; the launch traced here: 51.3 us
  starting transfers between devices  21.2 us (41%)
  waiting for transfers between devices  20.2 us (39%)
  Pallas kernels  9.16 us (18%)
  between operations  0.74 us (1%)
    ppermute x6, waiting for transfers between devices, exchange(): lax.ppermute(array, 'ctx', [(i, j) for i, j in pairs if 0 <= j < count an...  14.3 us
    ppermute x6, starting transfers between devices, exchange(): lax.ppermute(array, 'ctx', [(i, j) for i, j in pairs if 0 <= j < count an...  10.9 us
    ppermute x6, starting transfers between devices, flip(): lax.ppermute(array, axis, [(i, i ^ bit) for i in range(lax.axis_size(axis...  10.3 us
    pallas_call x12, Pallas kernels, call(): pl.pallas_call(kernel, out_shape=shapes, in_specs=[pl.BlockSpec(memory_sp...  9.16 us
    ppermute x6, waiting for transfers between devices, flip(): lax.ppermute(array, axis, [(i, i ^ bit) for i in range(lax.axis_size(axis...  5.87 us
  transfers between devices with their start and end apart: 12, of which 7 were waited for; matrix products, arithmetic and copies ran while one was open for 0% of the time, Pallas kernels for 12%

profile of v6, /device:TPU:0, one launch (start us, length us, event | category | flops | bytes accessed | tf_op | source)
XLA Modules:
  0.0 51.3 jit_solution(9749616223699900820)
XLA Ops:
  0.6 1.5 %shard_map.144 = (f32[608,128]{1,0:T(8,128)S(1)}, f32[608,128]{1,0:T(8,128)S(1)}, f32[240,128]{1,0:T(8,128)S(1)}, bf16[128,512]{1,0:T(8,128)(2,1)S(1)}, bf16[128...) custom-call(s32[1,4]{1,0:T(1,128)} %lens_hbm.1, ...), custom_call_target="tpu_custom_call" | custom-call | flops 100000000 | bytes 2195664 | tf_op jit(solution)/shard_map/pallas_call | solution.py:840
  2.2 3.1 %collective-permute-start = (f32[608,128]{1,0:T(8,128)S(1)}, f32[608,128]{1,0:T(8,128)S(1)}, u32[]{:S(2)}, u32[]{:S(2)}) collective-permute-start(f32[608,128]{1,0:T(8,128)S(1)} %get-tuple-element.52), channel_id=1, source_target_pairs={{0,2},{2,0},{4,6},{6,4},{1,3},{3,1},{5,7},{7,5},{8,10},{10,8},{12,... | collective-permute-start | bytes 933896 | tf_op jit(solution)/shard_map/ppermute | solution.py:859
  5.3 0.7 %collective-permute-start.1 = (f32[608,128]{1,0:T(8,128)S(1)}, f32[608,128]{1,0:T(8,128)S(1)}, u32[]{:S(2)}, u32[]{:S(2)}) collective-permute-start(f32[608,128]{1,0:T(8,128)S(1)} %get-tuple-element.53), channel_id=1, source_target_pairs={{2,4},{4,2},{3,5},{5,3},{10,12},{12,10},{11,13},{13,11},{18,20},{2... | collective-permute-start | bytes 933896 | tf_op jit(solution)/shard_map/ppermute | solution.py:859
  6.0 0.4 shard_map.146
  6.3 4.4 %collective-permute-start.3 = (f32[512,128]{1,0:T(8,128)S(1)}, f32[512,128]{1,0:T(8,128)S(1)}, u32[]{:S(2)}, u32[]{:S(2)}) collective-permute-start(f32[512,128]{1,0:T(8,128)S(1)} %get-tuple-element.63), channel_id=1, source_target_pairs={{0,2},{2,0},{4,6},{6,4},{1,3},{3,1},{5,7},{7,5},{8,10},{10,8},{12,... | collective-permute-start | bytes 786440 | tf_op jit(solution)/shard_map/ppermute | solution.py:859
  10.8 0.7 %collective-permute-start.4 = (f32[512,128]{1,0:T(8,128)S(1)}, f32[512,128]{1,0:T(8,128)S(1)}, u32[]{:S(2)}, u32[]{:S(2)}) collective-permute-start(f32[512,128]{1,0:T(8,128)S(1)} %get-tuple-element.64), channel_id=1, source_target_pairs={{2,4},{4,2},{3,5},{5,3},{10,12},{12,10},{11,13},{13,11},{18,20},{2... | collective-permute-start | bytes 786440 | tf_op jit(solution)/shard_map/ppermute | solution.py:859
  11.4 2.1 %collective-permute-done.got_one_ref = f32[608,128]{1,0:T(8,128)S(1)} collective-permute-done((f32[608,128]{1,0:T(8,128)S(1)}, f32[608,128]{1,0:T(8,128)S(1)}, u32[]{:S(2)}, u32[]{:S(2)}) %collective-permute-start) | collective-permute-done | bytes 311328 | tf_op jit(solution)/shard_map/ppermute | solution.py:859
  13.5 0.0 collective-permute-done.1.got_two_ref
  13.5 0.1 collective-permute-start.2
  13.6 2.9 %shard_map.148 = (f32[128,1024]{1,0:T(8,128)S(1)}, f32[32,128]{1,0:T(8,128)S(1)}, f32[256,128]{1,0:T(8,128)S(1)}, f32[48,128]{1,0:T(8,128)S(1)}) custom-call(bf16[128,1024]{1,0:T(8,128)(2,1)S(1)} %get-tuple-element.58.x_ref, bf16[128,1024]{1,0:T(8,128)(2,1)S(1)} %get-tuple-element.59.g_ref, f32[240,128]{1,0:T(8,128)S(1)} %get-tuple-element.60.aux_ref, ...), custom_call_target="tpu_custom_call" | custom-call | flops 100000000 | bytes 1409024 | tf_op jit(solution)/shard_map/pallas_call | solution.py:840
  16.5 0.0 collective-permute-done.2.other_ref
  16.5 0.6 %shard_map.147 = (f32[128,512]{1,0:T(8,128)S(1)}, f32[128,512]{1,0:T(8,128)S(1)}, bf16[128,512]{1,0:T(8,128)(2,1)S(1)}, bf16[128,512]{1,0:T(8,128)(2,1)S(1)}, bf...) custom-call(f32[608,128]{1,0:T(8,128)S(1)} %collective-permute-done., ...), custom_call_target="tpu_custom_call" | custom-call | flops 100000000 | bytes 2285568 | tf_op jit(solution)/shard_map/pallas_call | solution.py:840
  17.1 1.2 %collective-permute-done.3.got_one_ref = f32[512,128]{1,0:T(8,128)S(1)} collective-permute-done((f32[512,128]{1,0:T(8,128)S(1)}, f32[512,128]{1,0:T(8,128)S(1)}, u32[]{:S(2)}, u32[]{:S(2)}) %collective-permute-start.3) | collective-permute-done | bytes 262176 | tf_op jit(solution)/shard_map/ppermute | solution.py:859
  18.3 0.0 collective-permute-done.4.got_two_ref
  18.3 0.7 %shard_map.149 = (f32[8,128]{1,0:T(8,128)S(1)}, f32[80,128]{1,0:T(8,128)S(1)}, f32[128,512]{1,0:T(8,128)S(1)}, f32[128,512]{1,0:T(8,128)S(1)}, bf16[128,512]{1,0...) custom-call(f32[512,128]{1,0:T(8,128)S(1)} %collective-permute-done.3.got_one_ref, ...), custom_call_target="tpu_custom_call" | custom-call | flops 100000000 | bytes 1994752 | tf_op jit(solution)/shard_map/pallas_call | solution.py:840
  18.9 1.3 %collective-permute-start.5 = (f32[592,128]{1,0:T(8,128)S(1)}, f32[592,128]{1,0:T(8,128)S(1)}, u32[]{:S(2)}, u32[]{:S(2)}) collective-permute-start(f32[592,128]{1,0:T(8,128)S(1)} %get-tuple-element.79), channel_id=1, source_target_pairs={{2,0},{4,6},{3,1},{5,7},{10,8},{12,14},{11,9},{13,15},{18,16},{20,... | collective-permute-start | bytes 909320 | tf_op jit(solution)/shard_map/ppermute | solution.py:859
  20.3 0.7 %collective-permute-start.6 = (f32[592,128]{1,0:T(8,128)S(1)}, f32[592,128]{1,0:T(8,128)S(1)}, u32[]{:S(2)}, u32[]{:S(2)}) collective-permute-start(f32[592,128]{1,0:T(8,128)S(1)} %get-tuple-element.80), channel_id=1, source_target_pairs={{2,4},{4,2},{3,5},{5,3},{10,12},{12,10},{11,13},{13,11},{18,20},{2... | collective-permute-start | bytes 909320 | tf_op jit(solution)/shard_map/ppermute | solution.py:859
  20.9 0.7 %shard_map.153.sums_ref = f32[256,128]{1,0:T(8,128)S(1)} custom-call(bf16[128,512]{1,0:T(8,128)(2,1)S(1)} %get-tuple-element.62.xp0_ref, bf16[128,512]{1,0:T(8,128)(2,1)S(1)} %get-tuple-element.71.xp1_ref, bf16[128,512]{1,0:T(8,128)(2,1)S(1)} %get-tuple-element.72.gn0_ref, bf16[128,512]{1,0:T(8,128)(2,1)S(1)} %get-tuple-element.73.gn1_ref, ...), custom_call_target="tpu_custom_call" | custom-call | flops 100000000 | bytes 1376256 | tf_op jit(solution)/shard_map/pallas_call | solution.py:840
  21.6 11.1 %collective-permute-done.5.far_one_ref = f32[592,128]{1,0:T(8,128)S(1)} collective-permute-done((f32[592,128]{1,0:T(8,128)S(1)}, f32[592,128]{1,0:T(8,128)S(1)}, u32[]{:S(2)}, u32[]{:S(2)}) %collective-permute-start.5) | collective-permute-done | bytes 303136 | tf_op jit(solution)/shard_map/ppermute | solution.py:859
  32.7 0.0 collective-permute-done.6.far_two_ref
  32.7 0.4 shard_map.154.half_ref
  33.0 0.1 collective-permute-start.11
  33.1 3.9 %collective-permute-start.7 = (f32[8,128]{1,0:T(8,128)S(1)}, f32[8,128]{1,0:T(8,128)S(1)}, u32[]{:S(2)}, u32[]{:S(2)}) collective-permute-start(f32[8,128]{1,0:T(8,128)S(1)} %get-tuple-element.90), channel_id=1, source_target_pairs={{0,2},{2,0},{4,6},{6,4},{1,3},{3,1},{5,7},{7,5},{8,10},{10,8},{12,... | collective-permute-start | bytes 12296 | tf_op jit(solution)/shard_map/ppermute | solution.py:865
  37.1 1.6 %collective-permute-done.7 = f32[8,128]{1,0:T(8,128)S(1)} collective-permute-done((f32[8,128]{1,0:T(8,128)S(1)}, f32[8,128]{1,0:T(8,128)S(1)}, u32[]{:S(2)}, u32[]{:S(2)}) %collective-permute-start.7) | collective-permute-done | bytes 4128 | tf_op jit(solution)/shard_map/ppermute | solution.py:865
  38.7 3.2 %collective-permute-start.8 = (f32[8,128]{1,0:T(8,128)S(1)}, f32[8,128]{1,0:T(8,128)S(1)}, u32[]{:S(2)}, u32[]{:S(2)}) collective-permute-start(f32[8,128]{1,0:T(8,128)S(1)} %add.9), channel_id=1, source_target_pairs={{0,4},{2,6},{4,0},{6,2},{1,5},{3,7},{5,1},{7,3},{8,12},{10,14},{12... | collective-permute-start | bytes 12296 | tf_op jit(solution)/shard_map/ppermute | solution.py:865
  41.8 1.6 %collective-permute-done.8 = f32[8,128]{1,0:T(8,128)S(1)} collective-permute-done((f32[8,128]{1,0:T(8,128)S(1)}, f32[8,128]{1,0:T(8,128)S(1)}, u32[]{:S(2)}, u32[]{:S(2)}) %collective-permute-start.8) | collective-permute-done | bytes 4128 | tf_op jit(solution)/shard_map/ppermute | solution.py:865
  43.4 1.5 %collective-permute-start.9 = (f32[8,128]{1,0:T(8,128)S(1)}, f32[8,128]{1,0:T(8,128)S(1)}, u32[]{:S(2)}, u32[]{:S(2)}) collective-permute-start(f32[8,128]{1,0:T(8,128)S(1)} %add.10), channel_id=1, source_target_pairs={{0,8},{8,0},{16,24},{24,16},{1,9},{9,1},{17,25},{25,17},{2,10},{10... | collective-permute-start | bytes 12296 | tf_op jit(solution)/shard_map/ppermute | solution.py:865
  44.9 0.4 shard_map.151
  45.3 1.7 %collective-permute-done.9 = f32[8,128]{1,0:T(8,128)S(1)} collective-permute-done((f32[8,128]{1,0:T(8,128)S(1)}, f32[8,128]{1,0:T(8,128)S(1)}, u32[]{:S(2)}, u32[]{:S(2)}) %collective-permute-start.9) | collective-permute-done | bytes 4128 | tf_op jit(solution)/shard_map/ppermute | solution.py:865
  47.0 1.5 %collective-permute-start.10 = (f32[8,128]{1,0:T(8,128)S(1)}, f32[8,128]{1,0:T(8,128)S(1)}, u32[]{:S(2)}, u32[]{:S(2)}) collective-permute-start(f32[8,128]{1,0:T(8,128)S(1)} %add.11.red_ref), channel_id=1, source_target_pairs={{0,16},{8,24},{16,0},{24,8},{1,17},{9,25},{17,1},{25,9},{2,18},{10... | collective-permute-start | bytes 12296 | tf_op jit(solution)/shard_map/ppermute | solution.py:865
  48.6 1.1 %shard_map.152 = (bf16[1,128,1024]{2,1,0:T(8,128)(2,1)}, f32[1,16,128]{2,1,0:T(8,128)}) custom-call(f32[592,128]{1,0:T(8,128)S(1)} %collective-permute-done.5.far_one_ref, f32[592,128]{1,0:T(8,128)S(1)} %collective-permute-done.6.far_two_ref, bf16[128,128]{1,0:T(8,128)(2,1)S(1)} %get-tuple-element.56.b_ref, f32[240,128]{1,0:T(8,128)S(1)} %get-tuple-element.60.aux_ref, ...), custom_call_target="tpu_custom_call" | custom-call | flops 100000000 | bytes 2138112 | tf_op jit(solution)/shard_map/pallas_call | solution.py:840
  49.7 1.0 %collective-permute-done.10.last_ref = f32[8,128]{1,0:T(8,128)S(1)} collective-permute-done((f32[8,128]{1,0:T(8,128)S(1)}, f32[8,128]{1,0:T(8,128)S(1)}, u32[]{:S(2)}, u32[]{:S(2)}) %collective-permute-start.10) | collective-permute-done | bytes 4128 | tf_op jit(solution)/shard_map/ppermute | solution.py:865
  50.6 0.0 collective-permute-done.11.other_ref
  50.7 0.7 %shard_map.155 = (f32[1,128,128]{2,1,0:T(8,128)}, f32[1,128,128]{2,1,0:T(8,128)}, f32[1,16]{1,0:T(1,128)}, f32[1,16]{1,0:T(1,128)}, f32[1,16]{1,0:T(1,128)}) custom-call(f32[8,128]{1,0:T(8,128)S(1)} %add.11.red_ref, f32[8,128]{1,0:T(8,128)S(1)} %collective-permute-done.10.last_ref, f32[256,128]{1,0:T(8,128)S(1)} %shard_map.154.half_ref, ...), custom_call_target="tpu_custom_call" | custom-call | bytes 401600 | tf_op jit(solution)/shard_map/pallas_call | solution.py:840
  (5 shorter events, 0.0 us)
Async XLA Ops:
  2.2 11.3 %collective-permute-start = (f32[608,128]{1,0:T(8,128)S(1)}, f32[608,128]{1,0:T(8,128)S(1)}, u32[]{:S(2)}, u32[]{:S(2)}) collective-permute-start(f32[608,128]{1,0:T(8,128)S(1)} %get-tuple-element.52), channel_id=1, source_target_pairs={{0,2},{2,0},{4,6},{6,4},{1,3},{3,1},{5,7},{7,5},{8,10},{10,8},{12,... | collective-permute-start | bytes 933896 | tf_op jit(solution)/shard_map/ppermute | solution.py:859
  5.3 8.2 %collective-permute-start.1 = (f32[608,128]{1,0:T(8,128)S(1)}, f32[608,128]{1,0:T(8,128)S(1)}, u32[]{:S(2)}, u32[]{:S(2)}) collective-permute-start(f32[608,128]{1,0:T(8,128)S(1)} %get-tuple-element.53), channel_id=1, source_target_pairs={{2,4},{4,2},{3,5},{5,3},{10,12},{12,10},{11,13},{13,11},{18,20},{2... | collective-permute-start | bytes 933896 | tf_op jit(solution)/shard_map/ppermute | solution.py:859
  6.3 11.9 %collective-permute-start.3 = (f32[512,128]{1,0:T(8,128)S(1)}, f32[512,128]{1,0:T(8,128)S(1)}, u32[]{:S(2)}, u32[]{:S(2)}) collective-permute-start(f32[512,128]{1,0:T(8,128)S(1)} %get-tuple-element.63), channel_id=1, source_target_pairs={{0,2},{2,0},{4,6},{6,4},{1,3},{3,1},{5,7},{7,5},{8,10},{10,8},{12,... | collective-permute-start | bytes 786440 | tf_op jit(solution)/shard_map/ppermute | solution.py:859
  10.8 7.5 %collective-permute-start.4 = (f32[512,128]{1,0:T(8,128)S(1)}, f32[512,128]{1,0:T(8,128)S(1)}, u32[]{:S(2)}, u32[]{:S(2)}) collective-permute-start(f32[512,128]{1,0:T(8,128)S(1)} %get-tuple-element.64), channel_id=1, source_target_pairs={{2,4},{4,2},{3,5},{5,3},{10,12},{12,10},{11,13},{13,11},{18,20},{2... | collective-permute-start | bytes 786440 | tf_op jit(solution)/shard_map/ppermute | solution.py:859
  13.5 3.0 %collective-permute-start.2 = (f32[128,128]{1,0:T(8,128)S(1)}, f32[128,128]{1,0:T(8,128)S(1)}, u32[]{:S(2)}, u32[]{:S(2)}) collective-permute-start(f32[128,128]{1,0:T(8,128)S(1)} %shard_map.145.maps_ref), channel_id=1, source_target_pairs={{0,1},{1,0},{2,3},{3,2},{4,5},{5,4},{6,7},{7,6},{8,9},{9,8},{10,11... | collective-permute-start | bytes 196616 | tf_op jit(solution)/shard_map/ppermute | solution.py:865
  18.9 13.7 %collective-permute-start.5 = (f32[592,128]{1,0:T(8,128)S(1)}, f32[592,128]{1,0:T(8,128)S(1)}, u32[]{:S(2)}, u32[]{:S(2)}) collective-permute-start(f32[592,128]{1,0:T(8,128)S(1)} %get-tuple-element.79), channel_id=1, source_target_pairs={{2,0},{4,6},{3,1},{5,7},{10,8},{12,14},{11,9},{13,15},{18,16},{20,... | collective-permute-start | bytes 909320 | tf_op jit(solution)/shard_map/ppermute | solution.py:859
  20.3 12.4 %collective-permute-start.6 = (f32[592,128]{1,0:T(8,128)S(1)}, f32[592,128]{1,0:T(8,128)S(1)}, u32[]{:S(2)}, u32[]{:S(2)}) collective-permute-start(f32[592,128]{1,0:T(8,128)S(1)} %get-tuple-element.80), channel_id=1, source_target_pairs={{2,4},{4,2},{3,5},{5,3},{10,12},{12,10},{11,13},{13,11},{18,20},{2... | collective-permute-start | bytes 909320 | tf_op jit(solution)/shard_map/ppermute | solution.py:859
  33.0 17.6 %collective-permute-start.11 = (f32[256,128]{1,0:T(8,128)S(1)}, f32[256,128]{1,0:T(8,128)S(1)}, u32[]{:S(2)}, u32[]{:S(2)}) collective-permute-start(f32[256,128]{1,0:T(8,128)S(1)} %shard_map.154.half_ref), channel_id=1, source_target_pairs={{0,1},{1,0},{2,3},{3,2},{4,5},{5,4},{6,7},{7,6},{8,9},{9,8},{10,11... | collective-permute-start | bytes 393224 | tf_op jit(solution)/shard_map/ppermute | solution.py:865
  33.1 5.5 %collective-permute-start.7 = (f32[8,128]{1,0:T(8,128)S(1)}, f32[8,128]{1,0:T(8,128)S(1)}, u32[]{:S(2)}, u32[]{:S(2)}) collective-permute-start(f32[8,128]{1,0:T(8,128)S(1)} %get-tuple-element.90), channel_id=1, source_target_pairs={{0,2},{2,0},{4,6},{6,4},{1,3},{3,1},{5,7},{7,5},{8,10},{10,8},{12,... | collective-permute-start | bytes 12296 | tf_op jit(solution)/shard_map/ppermute | solution.py:865
  38.7 4.8 %collective-permute-start.8 = (f32[8,128]{1,0:T(8,128)S(1)}, f32[8,128]{1,0:T(8,128)S(1)}, u32[]{:S(2)}, u32[]{:S(2)}) collective-permute-start(f32[8,128]{1,0:T(8,128)S(1)} %add.9), channel_id=1, source_target_pairs={{0,4},{2,6},{4,0},{6,2},{1,5},{3,7},{5,1},{7,3},{8,12},{10,14},{12... | collective-permute-start | bytes 12296 | tf_op jit(solution)/shard_map/ppermute | solution.py:865
  43.4 3.6 %collective-permute-start.9 = (f32[8,128]{1,0:T(8,128)S(1)}, f32[8,128]{1,0:T(8,128)S(1)}, u32[]{:S(2)}, u32[]{:S(2)}) collective-permute-start(f32[8,128]{1,0:T(8,128)S(1)} %add.10), channel_id=1, source_target_pairs={{0,8},{8,0},{16,24},{24,16},{1,9},{9,1},{17,25},{25,17},{2,10},{10... | collective-permute-start | bytes 12296 | tf_op jit(solution)/shard_map/ppermute | solution.py:865
  47.0 3.6 %collective-permute-start.10 = (f32[8,128]{1,0:T(8,128)S(1)}, f32[8,128]{1,0:T(8,128)S(1)}, u32[]{:S(2)}, u32[]{:S(2)}) collective-permute-start(f32[8,128]{1,0:T(8,128)S(1)} %add.11.red_ref), channel_id=1, source_target_pairs={{0,16},{8,24},{16,0},{24,8},{1,17},{9,25},{17,1},{25,9},{2,18},{10... | collective-permute-start | bytes 12296 | tf_op jit(solution)/shard_map/ppermute | solution.py:865

commit v7 on v6

--- a/solution.py
+++ b/solution.py
@@ -341,9 +341,10 @@
 
 
 (
-    DT, GATE, CUM, DIN, DOUT, TOT, ALPHA_S, BETA_S, ALPHA_U, BETA_U, RATE, DOC, MASKS, SHORT, GAIN
-) = range(15)
-AUX = 15
+    DT, GATE, CUM, DIN, DOUT, TOT, RATE, DOC, MASKS, SHORT, GAIN
+) = range(11)
+AUX = 11
+ALPHA_S, BETA_S, ALPHA_U, BETA_U = range(4)
 FIRST, X_GB = range(2)
 Z_OWN, W_OWN, Z_FAR, W_FAR, CARRIED = range(5)
 FAR = 5
@@ -396,11 +397,18 @@
     heads = raw_ref.shape[0]
     row, column = iota((span, span), 0), iota((span, span), 1)
     upto = (row <= column).astype(F32)
-    beyond = (row > column).astype(F32)
     part = slice(0, features // 2)
     rows = head_rows(heads, features // heads, part)
-    for copy in small:
+    for copy in small[1:4]:
         copy.wait()
+    preact = raw_ref[...] + as_column(bias_ref[...])
+    dt = jnp.maximum(preact, 0.0) + jnp.log1p(jnp.exp(-jnp.abs(preact)))
+    gate = 1.0 / (1.0 + jnp.exp(-preact))
+    rate = -jnp.exp(as_column(alog_ref[...]))
+    cum = nn(dt * rate, upto, EXACT)
+    cum_last = cum[:, span - 1 : span]
+    small[0].wait()
+    small[4].wait()
     base = lax.axis_index("ctx") * span
     doc = doc_of(lens_ref, base + iota((1, span), 1))
     before = doc_scalar(lens_ref, base - 1)
@@ -412,26 +420,12 @@
     short_last = jnp.where(
         base + span - doc_start(lens_ref, base + span - 1) <= span // 2, 1.0, 0.0
     )
-    preact = raw_ref[...] + as_column(bias_ref[...])
-    dt = jnp.maximum(preact, 0.0) + jnp.log1p(jnp.exp(-jnp.abs(preact)))
-    gate = 1.0 / (1.0 + jnp.exp(-preact))
-    rate = -jnp.exp(as_column(alog_ref[...]))
-    cum = nn(dt * rate, upto, EXACT)
-    cum_last = cum[:, span - 1 : span]
     din = inward * jnp.exp(cum)
     dout = outward * jnp.exp(cum_last - cum)
-    pair = jnp.concatenate([dt, gate], axis=0)
-    seen = nn(pair * inward, upto, EXACT)
-    left = nn(pair * outward, beyond, EXACT)
-    alpha_s = rate * left[:heads]
-    beta_s = rate * left[heads:] + gate / dt
-    alpha_u = rate * seen[:heads]
-    beta_u = rate * seen[heads:]
     put(aux_ref, heads, {
         DT: dt, GATE: gate, CUM: cum, DIN: din, DOUT: dout,
         TOT: jnp.broadcast_to(whole * jnp.exp(cum_last), dt.shape),
         GAIN: jnp.broadcast_to(as_column(skip_ref[...]), dt.shape),
-        ALPHA_S: alpha_s, BETA_S: beta_s, ALPHA_U: alpha_u, BETA_U: beta_u,
         RATE: jnp.broadcast_to(rate, dt.shape), DOC: jnp.broadcast_to(doc.astype(F32), dt.shape),
         MASKS: halves(inward, outward, heads),
         SHORT: halves(jnp.full((1, span), short_before), jnp.full((1, span), short_last), heads),
@@ -452,17 +446,20 @@
 
     @pl.when(first)
     def _():
-        fill(pay_one_ref, xs, mine(b_ref), alpha_s, beta_s)
-        fill(pay_two_ref, gs, mine(c_ref), alpha_u, beta_u)
+        fill(pay_one_ref, xs, mine(b_ref))
+        fill(pay_two_ref, gs, mine(c_ref))
 
     @pl.when(jnp.logical_not(first))
     def _():
-        fill(pay_one_ref, gs, mine(c_ref), alpha_u, beta_u)
-        fill(pay_two_ref, xs, mine(b_ref), alpha_s, beta_s)
-
-
-def rest_kernel(x_ref, g_ref, aux_ref, pay_one_ref, pay_two_ref, xs_ref, gs_ref, tot_ref, gain_ref):
-    features = x_ref.shape[1]
+        fill(pay_one_ref, gs, mine(c_ref))
+        fill(pay_two_ref, xs, mine(b_ref))
+
+
+def rest_kernel(
+    x_ref, g_ref, aux_ref,
+    pay_one_ref, pay_two_ref, xs_ref, gs_ref, tot_ref, gain_ref, weights_ref,
+):
+    span, features = x_ref.shape
     heads = aux_ref.shape[0] // AUX
     part = slice(features // 2, features)
     rows = head_rows(heads, features // heads, part)
@@ -474,17 +471,27 @@
     for slot, ref in ((TOT, tot_ref), (GAIN, gain_ref)):
         row = as_row(take(aux_ref, slot, heads)[:, :1])
         ref[...] = jnp.broadcast_to(spread_row(row, features), ref.shape)
+    row, column = iota((span, span), 0), iota((span, span), 1)
+    gate, rate = take(aux_ref, GATE, heads), take(aux_ref, RATE, heads)
+    inout = take(aux_ref, MASKS, heads)
+    inward, outward = inout[:1, :], inout[heads // 2 : heads // 2 + 1, :]
+    pair = jnp.concatenate([dt, gate], axis=0)
+    seen = nn(pair * inward, (row <= column).astype(F32), EXACT)
+    left = nn(pair * outward, (row > column).astype(F32), EXACT)
+    alpha_s, beta_s = rate * left[:heads], rate * left[heads:] + gate / dt
+    alpha_u, beta_u = rate * seen[:heads], rate * seen[heads:]
+    put(weights_ref, heads, {ALPHA_S: alpha_s, BETA_S: beta_s, ALPHA_U: alpha_u, BETA_U: beta_u})
     first = leads()
 
     @pl.when(first)
     def _():
-        fill(pay_one_ref, xs)
-        fill(pay_two_ref, gs)
+        fill(pay_one_ref, xs, alpha_s, beta_s)
+        fill(pay_two_ref, gs, alpha_u, beta_u)
 
     @pl.when(jnp.logical_not(first))
     def _():
-        fill(pay_one_ref, gs)
-        fill(pay_two_ref, xs)
+        fill(pay_one_ref, gs, alpha_u, beta_u)
+        fill(pay_two_ref, xs, alpha_s, beta_s)
 
 
 def local_kernel(
@@ -573,7 +580,7 @@
         gn_tot.astype(F32) * far_pull,
         xp.astype(F32) * far_push,
     )
-    return [nt(rows, item.astype(BF16)) for item in products]
+    return [nt(rows, item.astype(BF16)) for item in products], gn_tot
 
 
 def maps_kernel(base, got_one_ref, got_two_ref, maps_ref):
@@ -585,7 +592,7 @@
 
 def relay_first_kernel(
     got_one_ref, got_two_ref, maps_ref, other_ref, xs_ref, gs_ref, b_ref, c_ref, tot_ref, aux_ref,
-    push_ref, far_push_ref, xp_ref, gn_ref, bp_ref, cn_ref, scores_ref, part_ref, weights_ref,
+    push_ref, far_push_ref, xp_ref, gn_ref, bp_ref, cn_ref, scores_ref, part_ref, cross_b_ref, cross_c_ref,
 ):
     span, features = xs_ref.shape
     heads = aux_ref.shape[0] // AUX
@@ -603,19 +610,18 @@
 
     xp, bp = wide(behind, span, blocks), whole(slice(0, rows))
     gn, cn = wide(ahead, span, blocks), whole(slice(rows, 2 * rows))
-    base = blocks * span + rows
-    weights_ref[: 2 * heads, :] = behind(slice(base, base + 2 * heads))
-    weights_ref[2 * heads :, :] = ahead(slice(base, base + 2 * heads))
     b, c = b_ref[...], c_ref[...]
     scores = [item.astype(BF16) for item in (nt(c, bp), nt(b, cn), nt(cn, bp), nt(bp, cn))]
     part = slice(0, features)
-    sums = relay_terms(
+    sums, gn_tot = relay_terms(
         xp, gn, xs_ref[...], gs_ref[...], tot_ref[:1, part], scores,
         head_rows(heads, width, part), push_ref, far_push_ref,
     )
     for index in range(4):
         scores_ref[index * span : (index + 1) * span, :] = scores[index]
         part_ref[index * heads : (index + 1) * heads, :] = sums[index]
+    cross_b_ref[...] = nt(xp, gn_tot)
+    cross_c_ref[...] = nt(gn_tot, xp)
     xp_ref[...] = xp
     gn_ref[...] = gn
     bp_ref[...] = bp
@@ -633,7 +639,7 @@
     behind, ahead = neighbours(got_one_ref, got_two_ref)
     xp, gn = wide(behind, span, blocks), wide(ahead, span, blocks)
     part = slice(total - features, total)
-    sums = relay_terms(
+    sums, _ = relay_terms(
         xp, gn, xs_ref[...], gs_ref[...], tot_ref[:1, part],
         [scores_ref[index * span : (index + 1) * span, :] for index in range(4)],
         head_rows(heads, total // heads, part), push_ref, far_push_ref,
@@ -641,30 +647,30 @@
     z_own, w_own, z_far, w_far = (
         sums[index] + part_ref[index * heads : (index + 1) * heads, :] for index in range(4)
     )
-    alpha_p, beta_p, alpha_n, beta_n = (
-        weights_ref[index * heads : (index + 1) * heads, :] for index in range(4)
-    )
+    base = blocks * span
+    alpha_p, beta_p = behind(slice(base, base + heads)), behind(slice(base + heads, base + 2 * heads))
+    alpha_n, beta_n = ahead(slice(base, base + heads)), ahead(slice(base + heads, base + 2 * heads))
     carried = jnp.sum(z_far, axis=1, keepdims=True)
     rate = take(aux_ref, RATE, heads)
     alog = (
         own_ref[:heads, :]
-        + z_own * take(aux_ref, ALPHA_U, heads)
-        + w_own * take(aux_ref, ALPHA_S, heads)
+        + z_own * take(weights_ref, ALPHA_U, heads)
+        + w_own * take(weights_ref, ALPHA_S, heads)
         + carried * rate * take(aux_ref, DT, heads)
         + z_far * alpha_n
         + w_far * alpha_p
     )
     bias = (
         own_ref[heads : 2 * heads, :]
-        + z_own * take(aux_ref, BETA_U, heads)
-        + w_own * take(aux_ref, BETA_S, heads)
+        + z_own * take(weights_ref, BETA_U, heads)
+        + w_own * take(weights_ref, BETA_S, heads)
         + carried * rate * take(aux_ref, GATE, heads)
         + z_far * beta_n
         + w_far * beta_p
     )
     stack = jnp.concatenate([alog, bias, own_ref[2 * heads :, :]], axis=0)
-    red_ref[:, : 3 * heads] = nt(jnp.ones((8, span), F32), stack, EXACT)
-    red_ref[:, 3 * heads :] = jnp.zeros((8, red_ref.shape[1] - 3 * heads), F32)
+    red_ref[:, : 3 * heads] = nt(jnp.ones((8, span), F32), stack, EXACT)[:1]
+    red_ref[:, 3 * heads :] = jnp.zeros((1, red_ref.shape[1] - 3 * heads), F32)
     put(far_ref, heads, {
         Z_OWN: z_own, W_OWN: w_own, Z_FAR: z_far, W_FAR: w_far,
         CARRIED: jnp.broadcast_to(carried, z_own.shape),
@@ -678,20 +684,21 @@
 
 
 def hops_kernel(
-    xp0_ref, xp1_ref, gn0_ref, gn1_ref, bp_ref, cn_ref, aux_ref, far_ref, push0_ref, push1_ref,
-    tot_ref, hop_one_ref, hop_two_ref,
+    xp1_ref, gn0_ref, gn1_ref, bp_ref, cn_ref, aux_ref, far_ref, push0_ref, push1_ref, tot_ref,
+    cross_b_ref, cross_c_ref, hop_one_ref, hop_two_ref,
 ):
     ctx = lax.axis_index("ctx")
 
     @pl.when((ctx > 0) & (ctx < lax.axis_size("ctx") - 1))
     def _():
-        xp, gn, bp, cn = both(xp0_ref, xp1_ref), both(gn0_ref, gn1_ref), bp_ref[...], cn_ref[...]
-        span, features = xp.shape
+        bp, cn, xp = bp_ref[...], cn_ref[...], xp1_ref[...]
+        span, split = xp.shape
+        features = tot_ref.shape[1]
         blocks = features // LANES
         heads = far_ref.shape[0] // FAR
-        gn_tot = (gn.astype(F32) * tot_ref[:1, :]).astype(BF16)
-        grad_b_far = nn(nt(xp, gn_tot).astype(BF16), cn)
-        grad_c_far = nn(nt(gn_tot, xp).astype(BF16), bp)
+        scaled = (gn1_ref[...].astype(F32) * tot_ref[:1, features - split :]).astype(BF16)
+        grad_b_far = nn((cross_b_ref[...] + nt(xp, scaled)).astype(BF16), cn)
+        grad_c_far = nn((cross_c_ref[...] + nt(scaled, xp)).astype(BF16), bp)
         half = span // 2
         base = blocks * half
         short = take(aux_ref, SHORT, heads)[:1, :] > 0.5
@@ -699,12 +706,15 @@
         def load(ref, grad, slot, heavy):
             if heavy:
                 for block in range(blocks):
-                    push_ref = (push0_ref, push1_ref)[block * 2 // blocks]
+                    late = block * 2 // blocks
+                    push_ref, g_ref = ((push0_ref, gn0_ref), (push1_ref, gn1_ref))[late]
                     inner = (block % (blocks // 2)) * LANES
+                    tot = tot_ref[:1, block * LANES : (block + 1) * LANES]
+                    g_rows = g_ref[:half, inner : inner + LANES].astype(F32)
                     ref[block * half : (block + 1) * half, :] = jnp.where(
                         short,
                         push_ref[half:, inner : inner + LANES],
-                        gn_tot[:half, block * LANES : (block + 1) * LANES].astype(F32),
+                        (g_rows * tot).astype(BF16).astype(F32),
                     )
                 ref[base : base + half, :] = jnp.where(short, grad[half:], cn[:half].astype(F32))
             else:
@@ -877,13 +887,14 @@
     sides = lax.axis_size("head")
     blocks = split // LANES * span
     base = 2 * blocks + span
-    pay = struct((blocks + span // sides + 2 * heads, LANES), F32)
-    pay_rest = struct((blocks, LANES), F32)
+    pay = struct((blocks + span // sides, LANES), F32)
+    pay_rest = struct((blocks + 2 * heads, LANES), F32)
     full, low = struct((span, features), F32), struct((span, features), BF16)
     full_part, low_part = struct((span, split), F32), struct((span, split), BF16)
     line = struct((8, features), F32)
     square = struct((span, state), BF16)
     pair = struct((2 * span, state), F32)
+    tile = struct((span, span), F32)
     quad = struct((4 * heads, span), F32)
     one_row = pltpu.VMEM((1, heads), F32)
     pay_one, pay_two, aux, xs0, gs0, x, g, b, c = call(
@@ -897,8 +908,11 @@
     )
     got_two = exchange(pay_two, 1, range(count))
     got_one = exchange(pay_one, 0, range(count))
-    pay_one, pay_two, xs1, gs1, tot, gain = call(
-        rest_kernel, (pay_rest, pay_rest, low_part, low_part, line, line), (x, g, aux), flops=10**7
+    pay_one, pay_two, xs1, gs1, tot, gain, weights = call(
+        rest_kernel,
+        (pay_rest, pay_rest, low_part, low_part, line, line, quad),
+        (x, g, aux),
+        flops=10**7,
     )
     more_two = exchange(pay_two, 1, range(count))
     more_one = exchange(pay_one, 0, range(count))
@@ -913,16 +927,16 @@
         (got_one, got_two), flops=10**5,
     )[0]
     other_maps = flip(maps, "head", 1)
-    push0, far_push0, xp0, gn0, bp, cn, scores, part, weights = call(
+    push0, far_push0, xp0, gn0, bp, cn, scores, part, cross_b, cross_c = call(
         relay_first_kernel,
         (full_part, full_part, low_part, low_part, square, square,
-         struct((4 * span, span), BF16), quad, quad),
+         struct((4 * span, span), BF16), quad, tile, tile),
         (got_one, got_two, maps, other_maps, xs0, gs0, b, c, tot, aux),
         flops=10**8,
     )
     red, far, push1, far_push1, xp1, gn1 = call(
         relay_kernel,
-        (struct((8, LANES), F32), struct((FAR * heads, span), F32), full_part, full_part,
+        (struct((1, LANES), F32), struct((FAR * heads, span), F32), full_part, full_part,
          low_part, low_part),
         (more_one, more_two, xs1, gs1, tot, aux, scores, part, weights, own),
         flops=10**8,
@@ -937,7 +951,7 @@
     hop_one, hop_two = call(
         hops_kernel,
         (hop, hop),
-        (xp0, xp1, gn0, gn1, bp, cn, aux, far, far_push0, far_push1, tot),
+        (xp1, gn0, gn1, bp, cn, aux, far, far_push0, far_push1, tot, cross_b, cross_c),
         flops=10**8,
     )
     sums = call(

time: 51.5 us -> 51 us (level)
  waiting for transfers between devices: 20.2 us -> 19.4 us
    ppermute x6, waiting for transfers between devices: 14.3 us -> 13.7 us  [exchange(): lax.ppermute(array, 'ctx', [(i, j) for i, j in pairs if 0 <= j < count an...]
where the time goes in v7:
time: 51 us; the launch traced here: 50.8 us
  starting transfers between devices  21.2 us (42%)
  waiting for transfers between devices  19.4 us (38%)
  Pallas kernels  9.4 us (18%)
  between operations  0.74 us (1%)
    ppermute x6, waiting for transfers between devices, exchange(): lax.ppermute(array, 'ctx', [(i, j) for i, j in pairs if 0 <= j < count an...  13.7 us
    ppermute x6, starting transfers between devices, exchange(): lax.ppermute(array, 'ctx', [(i, j) for i, j in pairs if 0 <= j < count an...  10.9 us
    ppermute x6, starting transfers between devices, flip(): lax.ppermute(array, axis, [(i, i ^ bit) for i in range(lax.axis_size(axis...  10.3 us
    pallas_call x12, Pallas kernels, call(): pl.pallas_call(kernel, out_shape=shapes, in_specs=[pl.BlockSpec(memory_sp...  9.4 us
    ppermute x6, waiting for transfers between devices, flip(): lax.ppermute(array, axis, [(i, i ^ bit) for i in range(lax.axis_size(axis...  5.74 us
  transfers between devices with their start and end apart: 12, of which 7 were waited for; matrix products, arithmetic and copies ran while one was open for 0% of the time, Pallas kernels for 12%

profile of v7, /device:TPU:0, one launch (start us, length us, event | category | flops | bytes accessed | tf_op | source)
XLA Modules:
  0.0 50.8 jit_solution(13846127748768081984)
XLA Ops:
  0.6 1.5 %shard_map.144 = (f32[576,128]{1,0:T(8,128)S(1)}, f32[576,128]{1,0:T(8,128)S(1)}, f32[176,128]{1,0:T(8,128)S(1)}, bf16[128,512]{1,0:T(8,128)(2,1)S(1)}, bf16[128...) custom-call(s32[1,4]{1,0:T(1,128)} %lens_hbm.1, ...), custom_call_target="tpu_custom_call" | custom-call | flops 100000000 | bytes 2130128 | tf_op jit(solution)/shard_map/pallas_call | solution.py:850
  2.2 3.1 %collective-permute-start.2 = (f32[576,128]{1,0:T(8,128)S(1)}, f32[576,128]{1,0:T(8,128)S(1)}, u32[]{:S(2)}, u32[]{:S(2)}) collective-permute-start(f32[576,128]{1,0:T(8,128)S(1)} %get-tuple-element.62), channel_id=1, source_target_pairs={{0,2},{2,0},{4,6},{6,4},{1,3},{3,1},{5,7},{7,5},{8,10},{10,8},{12,... | collective-permute-start | bytes 884744 | tf_op jit(solution)/shard_map/ppermute | solution.py:869
  5.3 0.7 %collective-permute-start.3 = (f32[576,128]{1,0:T(8,128)S(1)}, f32[576,128]{1,0:T(8,128)S(1)}, u32[]{:S(2)}, u32[]{:S(2)}) collective-permute-start(f32[576,128]{1,0:T(8,128)S(1)} %get-tuple-element.63), channel_id=1, source_target_pairs={{2,4},{4,2},{3,5},{5,3},{10,12},{12,10},{11,13},{13,11},{18,20},{2... | collective-permute-start | bytes 884744 | tf_op jit(solution)/shard_map/ppermute | solution.py:869
  6.0 0.5 shard_map.145
  6.4 4.5 %collective-permute-start = (f32[544,128]{1,0:T(8,128)S(1)}, f32[544,128]{1,0:T(8,128)S(1)}, u32[]{:S(2)}, u32[]{:S(2)}) collective-permute-start(f32[544,128]{1,0:T(8,128)S(1)} %get-tuple-element.57), channel_id=1, source_target_pairs={{0,2},{2,0},{4,6},{6,4},{1,3},{3,1},{5,7},{7,5},{8,10},{10,8},{12,... | collective-permute-start | bytes 835592 | tf_op jit(solution)/shard_map/ppermute | solution.py:869
  10.9 0.7 %collective-permute-start.1 = (f32[544,128]{1,0:T(8,128)S(1)}, f32[544,128]{1,0:T(8,128)S(1)}, u32[]{:S(2)}, u32[]{:S(2)}) collective-permute-start(f32[544,128]{1,0:T(8,128)S(1)} %get-tuple-element.58), channel_id=1, source_target_pairs={{2,4},{4,2},{3,5},{5,3},{10,12},{12,10},{11,13},{13,11},{18,20},{2... | collective-permute-start | bytes 835592 | tf_op jit(solution)/shard_map/ppermute | solution.py:869
  11.6 1.6 %collective-permute-done.2.got_one_ref = f32[576,128]{1,0:T(8,128)S(1)} collective-permute-done((f32[576,128]{1,0:T(8,128)S(1)}, f32[576,128]{1,0:T(8,128)S(1)}, u32[]{:S(2)}, u32[]{:S(2)}) %collective-permute-start.2) | collective-permute-done | bytes 294944 | tf_op jit(solution)/shard_map/ppermute | solution.py:869
  13.2 0.0 collective-permute-done.3.got_two_ref
  13.2 0.1 collective-permute-start.4
  13.3 2.9 %shard_map.148 = (f32[128,1024]{1,0:T(8,128)S(1)}, f32[32,128]{1,0:T(8,128)S(1)}, f32[256,128]{1,0:T(8,128)S(1)}, f32[48,128]{1,0:T(8,128)S(1)}) custom-call(bf16[128,1024]{1,0:T(8,128)(2,1)S(1)} %get-tuple-element.54.x_ref, bf16[128,1024]{1,0:T(8,128)(2,1)S(1)} %get-tuple-element.55.g_ref, f32[176,128]{1,0:T(8,128)S(1)} %get-tuple-element.56.aux_ref, ...), custom_call_target="tpu_custom_call" | custom-call | flops 100000000 | bytes 1376256 | tf_op jit(solution)/shard_map/pallas_call | solution.py:850
  16.1 0.0 collective-permute-done.4.other_ref
  16.2 0.7 %shard_map.147 = (f32[128,512]{1,0:T(8,128)S(1)}, f32[128,512]{1,0:T(8,128)S(1)}, bf16[128,512]{1,0:T(8,128)(2,1)S(1)}, bf16[128,512]{1,0:T(8,128)(2,1)S(1)}, bf...) custom-call(f32[576,128]{1,0:T(8,128)S(1)} %collective-permute-done., ...), custom_call_target="tpu_custom_call" | custom-call | flops 100000000 | bytes 2318336 | tf_op jit(solution)/shard_map/pallas_call | solution.py:850
  16.9 1.4 %collective-permute-done.got_one_ref = f32[544,128]{1,0:T(8,128)S(1)} collective-permute-done((f32[544,128]{1,0:T(8,128)S(1)}, f32[544,128]{1,0:T(8,128)S(1)}, u32[]{:S(2)}, u32[]{:S(2)}) %collective-permute-start) | collective-permute-done | bytes 278560 | tf_op jit(solution)/shard_map/ppermute | solution.py:869
  18.3 0.0 collective-permute-done.1.got_two_ref
  18.3 0.7 %shard_map.149 = (f32[1,128]{1,0:T(1,128)S(1)}, f32[80,128]{1,0:T(8,128)S(1)}, f32[128,512]{1,0:T(8,128)S(1)}, f32[128,512]{1,0:T(8,128)S(1)}, bf16[128,512]{1,0...) custom-call(f32[544,128]{1,0:T(8,128)S(1)} %collective-permute-done.got_one_ref, ...), custom_call_target="tpu_custom_call" | custom-call | flops 100000000 | bytes 1991168 | tf_op jit(solution)/shard_map/pallas_call | solution.py:850
  18.9 1.3 %collective-permute-start.5 = (f32[592,128]{1,0:T(8,128)S(1)}, f32[592,128]{1,0:T(8,128)S(1)}, u32[]{:S(2)}, u32[]{:S(2)}) collective-permute-start(f32[592,128]{1,0:T(8,128)S(1)} %get-tuple-element.82), channel_id=1, source_target_pairs={{2,0},{4,6},{3,1},{5,7},{10,8},{12,14},{11,9},{13,15},{18,16},{20,... | collective-permute-start | bytes 909320 | tf_op jit(solution)/shard_map/ppermute | solution.py:869
  20.3 0.7 %collective-permute-start.6 = (f32[592,128]{1,0:T(8,128)S(1)}, f32[592,128]{1,0:T(8,128)S(1)}, u32[]{:S(2)}, u32[]{:S(2)}) collective-permute-start(f32[592,128]{1,0:T(8,128)S(1)} %get-tuple-element.83), channel_id=1, source_target_pairs={{2,4},{4,2},{3,5},{5,3},{10,12},{12,10},{11,13},{13,11},{18,20},{2... | collective-permute-start | bytes 909320 | tf_op jit(solution)/shard_map/ppermute | solution.py:869
  21.0 0.7 %shard_map.153.sums_ref = f32[256,128]{1,0:T(8,128)S(1)} custom-call(bf16[128,512]{1,0:T(8,128)(2,1)S(1)} %get-tuple-element.94.xp0_ref, bf16[128,512]{1,0:T(8,128)(2,1)S(1)} %get-tuple-element.72.xp1_ref, bf16[128,512]{1,0:T(8,128)(2,1)S(1)} %get-tuple-element.73.gn0_ref, bf16[128,512]{1,0:T(8,128)(2,1)S(1)} %get-tuple-element.74.gn1_ref, ...), custom_call_target="tpu_custom_call" | custom-call | flops 100000000 | bytes 1376256 | tf_op jit(solution)/shard_map/pallas_call | solution.py:850
  21.6 10.7 %collective-permute-done.5.far_one_ref = f32[592,128]{1,0:T(8,128)S(1)} collective-permute-done((f32[592,128]{1,0:T(8,128)S(1)}, f32[592,128]{1,0:T(8,128)S(1)}, u32[]{:S(2)}, u32[]{:S(2)}) %collective-permute-start.5) | collective-permute-done | bytes 303136 | tf_op jit(solution)/shard_map/ppermute | solution.py:869
  32.3 0.0 collective-permute-done.6.far_two_ref
  32.3 0.4 shard_map.154.half_ref
  32.7 0.1 collective-permute-start.11
  32.7 3.9 %collective-permute-start.7 = (f32[1,128]{1,0:T(1,128)S(1)}, f32[1,128]{1,0:T(1,128)S(1)}, u32[]{:S(2)}, u32[]{:S(2)}) collective-permute-start(f32[1,128]{1,0:T(1,128)S(1)} %get-tuple-element.93), channel_id=1, source_target_pairs={{0,2},{2,0},{4,6},{6,4},{1,3},{3,1},{5,7},{7,5},{8,10},{10,8},{12,... | collective-permute-start | bytes 1544 | tf_op jit(solution)/shard_map/ppermute | solution.py:875
  36.7 1.5 %collective-permute-done.7 = f32[1,128]{1,0:T(1,128)S(1)} collective-permute-done((f32[1,128]{1,0:T(1,128)S(1)}, f32[1,128]{1,0:T(1,128)S(1)}, u32[]{:S(2)}, u32[]{:S(2)}) %collective-permute-start.7) | collective-permute-done | bytes 544 | tf_op jit(solution)/shard_map/ppermute | solution.py:875
  38.2 3.2 %collective-permute-start.8 = (f32[1,128]{1,0:T(1,128)S(1)}, f32[1,128]{1,0:T(1,128)S(1)}, u32[]{:S(2)}, u32[]{:S(2)}) collective-permute-start(f32[1,128]{1,0:T(1,128)S(1)} %add.9), channel_id=1, source_target_pairs={{0,4},{2,6},{4,0},{6,2},{1,5},{3,7},{5,1},{7,3},{8,12},{10,14},{12... | collective-permute-start | bytes 1544 | tf_op jit(solution)/shard_map/ppermute | solution.py:875
  41.4 1.5 %collective-permute-done.8 = f32[1,128]{1,0:T(1,128)S(1)} collective-permute-done((f32[1,128]{1,0:T(1,128)S(1)}, f32[1,128]{1,0:T(1,128)S(1)}, u32[]{:S(2)}, u32[]{:S(2)}) %collective-permute-start.8) | collective-permute-done | bytes 544 | tf_op jit(solution)/shard_map/ppermute | solution.py:875
  42.9 1.5 %collective-permute-start.9 = (f32[1,128]{1,0:T(1,128)S(1)}, f32[1,128]{1,0:T(1,128)S(1)}, u32[]{:S(2)}, u32[]{:S(2)}) collective-permute-start(f32[1,128]{1,0:T(1,128)S(1)} %add.10), channel_id=1, source_target_pairs={{0,8},{8,0},{16,24},{24,16},{1,9},{9,1},{17,25},{25,17},{2,10},{10... | collective-permute-start | bytes 1544 | tf_op jit(solution)/shard_map/ppermute | solution.py:875
  44.5 0.4 shard_map.151
  44.8 1.7 %collective-permute-done.9 = f32[1,128]{1,0:T(1,128)S(1)} collective-permute-done((f32[1,128]{1,0:T(1,128)S(1)}, f32[1,128]{1,0:T(1,128)S(1)}, u32[]{:S(2)}, u32[]{:S(2)}) %collective-permute-start.9) | collective-permute-done | bytes 544 | tf_op jit(solution)/shard_map/ppermute | solution.py:875
  46.5 1.5 %collective-permute-start.10 = (f32[1,128]{1,0:T(1,128)S(1)}, f32[1,128]{1,0:T(1,128)S(1)}, u32[]{:S(2)}, u32[]{:S(2)}) collective-permute-start(f32[1,128]{1,0:T(1,128)S(1)} %add.11.red_ref), channel_id=1, source_target_pairs={{0,16},{8,24},{16,0},{24,8},{1,17},{9,25},{17,1},{25,9},{2,18},{10... | collective-permute-start | bytes 1544 | tf_op jit(solution)/shard_map/ppermute | solution.py:875
  48.0 1.1 %shard_map.152 = (bf16[1,128,1024]{2,1,0:T(8,128)(2,1)}, f32[1,16,128]{2,1,0:T(8,128)}) custom-call(f32[592,128]{1,0:T(8,128)S(1)} %collective-permute-done.5.far_one_ref, f32[592,128]{1,0:T(8,128)S(1)} %collective-permute-done.6.far_two_ref, bf16[128,128]{1,0:T(8,128)(2,1)S(1)} %get-tuple-element.66.b_ref, f32[176,128]{1,0:T(8,128)S(1)} %get-tuple-element.56.aux_ref, ...), custom_call_target="tpu_custom_call" | custom-call | flops 100000000 | bytes 2105344 | tf_op jit(solution)/shard_map/pallas_call | solution.py:850
  49.1 1.0 %collective-permute-done.10.last_ref = f32[1,128]{1,0:T(1,128)S(1)} collective-permute-done((f32[1,128]{1,0:T(1,128)S(1)}, f32[1,128]{1,0:T(1,128)S(1)}, u32[]{:S(2)}, u32[]{:S(2)}) %collective-permute-start.10) | collective-permute-done | bytes 544 | tf_op jit(solution)/shard_map/ppermute | solution.py:875
  50.1 0.0 collective-permute-done.11.other_ref
  50.1 0.7 %shard_map.155 = (f32[1,128,128]{2,1,0:T(8,128)}, f32[1,128,128]{2,1,0:T(8,128)}, f32[1,16]{1,0:T(1,128)}, f32[1,16]{1,0:T(1,128)}, f32[1,16]{1,0:T(1,128)}) custom-call(f32[1,128]{1,0:T(1,128)S(1)} %add.11.red_ref, f32[1,128]{1,0:T(1,128)S(1)} %collective-permute-done.10.last_ref, f32[256,128]{1,0:T(8,128)S(1)} %shard_map.154.half_ref, ...), custom_call_target="tpu_custom_call" | custom-call | bytes 394432 | tf_op jit(solution)/shard_map/pallas_call | solution.py:850
  (5 shorter events, 0.0 us)
Async XLA Ops:
  2.2 11.0 %collective-permute-start.2 = (f32[576,128]{1,0:T(8,128)S(1)}, f32[576,128]{1,0:T(8,128)S(1)}, u32[]{:S(2)}, u32[]{:S(2)}) collective-permute-start(f32[576,128]{1,0:T(8,128)S(1)} %get-tuple-element.62), channel_id=1, source_target_pairs={{0,2},{2,0},{4,6},{6,4},{1,3},{3,1},{5,7},{7,5},{8,10},{10,8},{12,... | collective-permute-start | bytes 884744 | tf_op jit(solution)/shard_map/ppermute | solution.py:869
  5.3 7.9 %collective-permute-start.3 = (f32[576,128]{1,0:T(8,128)S(1)}, f32[576,128]{1,0:T(8,128)S(1)}, u32[]{:S(2)}, u32[]{:S(2)}) collective-permute-start(f32[576,128]{1,0:T(8,128)S(1)} %get-tuple-element.63), channel_id=1, source_target_pairs={{2,4},{4,2},{3,5},{5,3},{10,12},{12,10},{11,13},{13,11},{18,20},{2... | collective-permute-start | bytes 884744 | tf_op jit(solution)/shard_map/ppermute | solution.py:869
  6.4 11.8 %collective-permute-start = (f32[544,128]{1,0:T(8,128)S(1)}, f32[544,128]{1,0:T(8,128)S(1)}, u32[]{:S(2)}, u32[]{:S(2)}) collective-permute-start(f32[544,128]{1,0:T(8,128)S(1)} %get-tuple-element.57), channel_id=1, source_target_pairs={{0,2},{2,0},{4,6},{6,4},{1,3},{3,1},{5,7},{7,5},{8,10},{10,8},{12,... | collective-permute-start | bytes 835592 | tf_op jit(solution)/shard_map/ppermute | solution.py:869
  10.9 7.4 %collective-permute-start.1 = (f32[544,128]{1,0:T(8,128)S(1)}, f32[544,128]{1,0:T(8,128)S(1)}, u32[]{:S(2)}, u32[]{:S(2)}) collective-permute-start(f32[544,128]{1,0:T(8,128)S(1)} %get-tuple-element.58), channel_id=1, source_target_pairs={{2,4},{4,2},{3,5},{5,3},{10,12},{12,10},{11,13},{13,11},{18,20},{2... | collective-permute-start | bytes 835592 | tf_op jit(solution)/shard_map/ppermute | solution.py:869
  13.2 3.0 %collective-permute-start.4 = (f32[128,128]{1,0:T(8,128)S(1)}, f32[128,128]{1,0:T(8,128)S(1)}, u32[]{:S(2)}, u32[]{:S(2)}) collective-permute-start(f32[128,128]{1,0:T(8,128)S(1)} %shard_map.146.maps_ref), channel_id=1, source_target_pairs={{0,1},{1,0},{2,3},{3,2},{4,5},{5,4},{6,7},{7,6},{8,9},{9,8},{10,11... | collective-permute-start | bytes 196616 | tf_op jit(solution)/shard_map/ppermute | solution.py:875
  18.9 13.3 %collective-permute-start.5 = (f32[592,128]{1,0:T(8,128)S(1)}, f32[592,128]{1,0:T(8,128)S(1)}, u32[]{:S(2)}, u32[]{:S(2)}) collective-permute-start(f32[592,128]{1,0:T(8,128)S(1)} %get-tuple-element.82), channel_id=1, source_target_pairs={{2,0},{4,6},{3,1},{5,7},{10,8},{12,14},{11,9},{13,15},{18,16},{20,... | collective-permute-start | bytes 909320 | tf_op jit(solution)/shard_map/ppermute | solution.py:869
  20.3 12.0 %collective-permute-start.6 = (f32[592,128]{1,0:T(8,128)S(1)}, f32[592,128]{1,0:T(8,128)S(1)}, u32[]{:S(2)}, u32[]{:S(2)}) collective-permute-start(f32[592,128]{1,0:T(8,128)S(1)} %get-tuple-element.83), channel_id=1, source_target_pairs={{2,4},{4,2},{3,5},{5,3},{10,12},{12,10},{11,13},{13,11},{18,20},{2... | collective-permute-start | bytes 909320 | tf_op jit(solution)/shard_map/ppermute | solution.py:869
  32.7 17.4 %collective-permute-start.11 = (f32[256,128]{1,0:T(8,128)S(1)}, f32[256,128]{1,0:T(8,128)S(1)}, u32[]{:S(2)}, u32[]{:S(2)}) collective-permute-start(f32[256,128]{1,0:T(8,128)S(1)} %shard_map.154.half_ref), channel_id=1, source_target_pairs={{0,1},{1,0},{2,3},{3,2},{4,5},{5,4},{6,7},{7,6},{8,9},{9,8},{10,11... | collective-permute-start | bytes 393224 | tf_op jit(solution)/shard_map/ppermute | solution.py:875
  32.7 5.5 %collective-permute-start.7 = (f32[1,128]{1,0:T(1,128)S(1)}, f32[1,128]{1,0:T(1,128)S(1)}, u32[]{:S(2)}, u32[]{:S(2)}) collective-permute-start(f32[1,128]{1,0:T(1,128)S(1)} %get-tuple-element.93), channel_id=1, source_target_pairs={{0,2},{2,0},{4,6},{6,4},{1,3},{3,1},{5,7},{7,5},{8,10},{10,8},{12,... | collective-permute-start | bytes 1544 | tf_op jit(solution)/shard_map/ppermute | solution.py:875
  38.2 4.7 %collective-permute-start.8 = (f32[1,128]{1,0:T(1,128)S(1)}, f32[1,128]{1,0:T(1,128)S(1)}, u32[]{:S(2)}, u32[]{:S(2)}) collective-permute-start(f32[1,128]{1,0:T(1,128)S(1)} %add.9), channel_id=1, source_target_pairs={{0,4},{2,6},{4,0},{6,2},{1,5},{3,7},{5,1},{7,3},{8,12},{10,14},{12... | collective-permute-start | bytes 1544 | tf_op jit(solution)/shard_map/ppermute | solution.py:875
  42.9 3.6 %collective-permute-start.9 = (f32[1,128]{1,0:T(1,128)S(1)}, f32[1,128]{1,0:T(1,128)S(1)}, u32[]{:S(2)}, u32[]{:S(2)}) collective-permute-start(f32[1,128]{1,0:T(1,128)S(1)} %add.10), channel_id=1, source_target_pairs={{0,8},{8,0},{16,24},{24,16},{1,9},{9,1},{17,25},{25,17},{2,10},{10... | collective-permute-start | bytes 1544 | tf_op jit(solution)/shard_map/ppermute | solution.py:875
  46.5 3.6 %collective-permute-start.10 = (f32[1,128]{1,0:T(1,128)S(1)}, f32[1,128]{1,0:T(1,128)S(1)}, u32[]{:S(2)}, u32[]{:S(2)}) collective-permute-start(f32[1,128]{1,0:T(1,128)S(1)} %add.11.red_ref), channel_id=1, source_target_pairs={{0,16},{8,24},{16,0},{24,8},{1,17},{9,25},{17,1},{25,9},{2,18},{10... | collective-permute-start | bytes 1544 | tf_op jit(solution)/shard_map/ppermute | solution.py:875
